TPU v7x, 128 devices: a whole 4x4x4 slice. The times are simulated.
128 devices in a mesh: band: 8 (over z_hi, y), lon: 16 (over z_lo, x, core).
Axes of the slice: x: 4, y: 4, z: 4 (z_hi: 2, z_lo: 2; z = z_hi * 2 + z_lo), core: 2. Of those that a mesh axis runs over, the one named last changes fastest.
Arguments:
- latent: bfloat16 [256, 2048, 256], P('band', 'lon'), may hold values from -6 to 6
- row_index: int32 [8, 16, 32], P('band', 'lon'), may hold values from 0 to 31
- interp_weights: bfloat16 [4096, 128, 128], P(('band', 'lon')), may hold values from -0.5 to 0.5
- observation_slot_index: int32 [4096, 128], P(('band', 'lon')), may hold values from 0 to 6
- counts: int32 [4096], P(('band', 'lon')), may hold values from 32 to 128
- targets: bfloat16 [4096, 128, 128], P(('band', 'lon')), may hold values from -6 to 6
- gain: float32 [256], replicated, may hold values from 0.5 to 1.5
- w_in: bfloat16 [256, 512], replicated, may hold values from -0.375 to 0.375
- w_out: bfloat16 [512, 256], replicated, may hold values from -0.25 to 0.25
- head: bfloat16 [256, 128], replicated, may hold values from -0.375 to 0.375
Outputs:
- grad_latent: float32 [256, 2048, 256], P('band', 'lon')
- grad_w_in: float32 [256, 512], replicated
- grad_w_out: float32 [512, 256], replicated
- grad_gain: float32 [256], replicated
- grad_head: float32 [256, 128], replicated
All inputs are finite; a program needn't handle non-finite values.
Results may differ from a plain program's by a relative error of at most 0.007.
Values may be sent and summed in bfloat16 or wider, within the bound.
No kernel may reach another device: no remote copies, remote signals or barrier semaphores. Data moves between devices by JAX's collectives and lax.ppermute only.
A program may use at most 128 MiB of HBM per device.

v0:
```python
import math

import jax
import jax.numpy as jnp
from jax import lax
from jax.sharding import PartitionSpec as P

WINDOW_SLOTS = 7


norm_eps = 1e-05


def padded_2(cells, sides, width):
    for axis, dim in sides:
        count = lax.axis_size(axis)
        head = lax.slice_in_dim(cells, 0, width, axis=dim)
        tail = lax.slice_in_dim(cells, cells.shape[dim] - width, cells.shape[dim], axis=dim)
        cells = jnp.concatenate(
            [
                lax.ppermute(tail, axis, [(i, (i + 1) % count) for i in range(count)]),
                cells,
                lax.ppermute(head, axis, [((i + 1) % count, i) for i in range(count)]),
            ],
            axis=dim,
        )
    return cells


def rounded_slots(values):
    return lax.optimization_barrier(values.astype(jnp.bfloat16))


def padded_mix(padded):
    return padded[:, 1:-1] + 0.5 * (padded[:, :-2] + padded[:, 2:])


def silu_slope(pre_act):
    sigmoid_a = jax.nn.sigmoid(pre_act)
    return sigmoid_a * (1.0 + pre_act * (1.0 - sigmoid_a))


def project_pair(weights, tile_pairs, temporal_weight, channels):
    proj_old = jnp.einsum(
        "bol,blc->boc", weights, tile_pairs[..., :channels], preferred_element_type=jnp.float32
    )
    proj_new = jnp.einsum(
        "bol,blc->boc", weights, tile_pairs[..., channels:], preferred_element_type=jnp.float32
    )
    return ((1.0 - temporal_weight) * proj_old + temporal_weight * proj_new).astype(jnp.bfloat16)


def pull_back(weights, obs_grad, temporal_weight):
    obs_float = obs_grad.astype(jnp.float32)
    back_old = ((1.0 - temporal_weight) * obs_float).astype(jnp.bfloat16)
    back_new = (temporal_weight * obs_float).astype(jnp.bfloat16)
    tile_old = jnp.einsum("bol,boc->blc", weights, back_old, preferred_element_type=jnp.float32)
    tile_new = jnp.einsum("bol,boc->blc", weights, back_new, preferred_element_type=jnp.float32)
    return jnp.concatenate([tile_old, tile_new], axis=-1).astype(jnp.bfloat16)


def decode(obs_latent, live_rows, goals, head, loss_scale):
    blocks, obs_rows, channels = obs_latent.shape
    flat_latent = obs_latent.reshape(-1, channels)
    predicted = jnp.dot(flat_latent, head, preferred_element_type=jnp.float32)
    residual = jnp.where(
        live_rows, predicted - goals.reshape(-1, head.shape[1]).astype(jnp.float32), 0.0
    )
    pred_grad = (residual * loss_scale).astype(jnp.bfloat16)
    head_grad = jnp.einsum("rc,rv->cv", flat_latent, pred_grad, preferred_element_type=jnp.float32)
    obs_grad = jnp.einsum("rv,cv->rc", pred_grad, head, preferred_element_type=jnp.float32).astype(
        jnp.bfloat16
    )
    return (head_grad, obs_grad.reshape(blocks, obs_rows, channels))


def body(
    latent,
    row_index,
    interp_weights,
    observation_slot_index,
    counts,
    targets,
    gain,
    w_in,
    w_out,
    head,
):
    lat_rows, lon_cells, channels = latent.shape
    peer_count = lax.axis_size("lon")
    devices_all = lax.axis_size("band") * peer_count
    blocks = interp_weights.shape[0]
    obs_rows = interp_weights.shape[1]
    per_peer = blocks // peer_count
    padded = padded_2(latent, (("lon", 1),), 1)
    summed = padded_mix(padded.astype(jnp.float32))
    inv_rms = lax.rsqrt(jnp.mean(summed * summed, axis=-1, keepdims=True) + norm_eps)
    normed = (summed * inv_rms * gain).astype(jnp.bfloat16)
    pre_act = jnp.einsum("lmc,ch->lmh", normed, w_in, preferred_element_type=jnp.float32)
    activated = jax.nn.silu(pre_act).astype(jnp.bfloat16)
    advanced = (
        latent.astype(jnp.float32)
        + jnp.einsum("lmh,hc->lmc", activated, w_out, preferred_element_type=jnp.float32)
    ).astype(jnp.bfloat16)
    stacked = jnp.concatenate([latent, advanced], axis=-1)
    requested = row_index.reshape(blocks)
    picked = stacked[requested]
    row_select = (requested[:, None] == jnp.arange(lat_rows, dtype=jnp.int32)[None, :]).astype(
        jnp.bfloat16
    )
    temporal_weight = rounded_slots(observation_slot_index.astype(jnp.float32) / (WINDOW_SLOTS - 1))
    live_flags = jnp.arange(obs_rows, dtype=jnp.int32)[None, :] < counts[:, None]
    live_rows = live_flags.reshape(-1, 1)
    loss_scale = 1.0 / math.sqrt(obs_rows)
    tile_pairs = lax.all_to_all(
        picked.reshape(peer_count, per_peer, lon_cells, 2 * channels),
        "lon",
        split_axis=0,
        concat_axis=0,
        tiled=True,
    )
    local_coef = temporal_weight.reshape(blocks, obs_rows, 1).astype(jnp.float32)
    obs_latent = project_pair(
        interp_weights, tile_pairs.reshape(blocks, lon_cells, 2 * channels), local_coef, channels
    )
    head_grad, obs_grad = decode(obs_latent, live_rows, targets, head, loss_scale)
    tile_grads = pull_back(interp_weights, obs_grad, local_coef)
    returned = lax.all_to_all(
        tile_grads.reshape(peer_count, per_peer, lon_cells, 2 * channels),
        "lon",
        split_axis=0,
        concat_axis=0,
        tiled=True,
    )
    grid_grad = jnp.einsum(
        "br,bx->rx",
        row_select,
        returned.reshape(blocks, lon_cells * 2 * channels),
        preferred_element_type=jnp.float32,
    )
    grid_grad = grid_grad.reshape(lat_rows, lon_cells, 2 * channels)
    grad_adv = grid_grad[..., channels:].astype(jnp.bfloat16)
    grad_out = jnp.einsum("lmh,lmc->hc", activated, grad_adv, preferred_element_type=jnp.float32)
    act_grad = jnp.einsum("lmc,hc->lmh", grad_adv, w_out, preferred_element_type=jnp.float32)
    pre_grad = (act_grad * silu_slope(pre_act)).astype(jnp.bfloat16)
    grad_in = jnp.einsum("lmc,lmh->ch", normed, pre_grad, preferred_element_type=jnp.float32)
    normed_grad = jnp.einsum("lmh,ch->lmc", pre_grad, w_in, preferred_element_type=jnp.float32)
    grad_gain = jnp.sum(normed_grad * summed * inv_rms, axis=(0, 1))
    gained = normed_grad * gain
    summed_grad = inv_rms * (
        gained - summed * inv_rms * inv_rms * jnp.mean(gained * summed, axis=-1, keepdims=True)
    )
    grad_padded = padded_2(summed_grad.astype(jnp.bfloat16), (("lon", 1),), 1).astype(
        summed_grad.dtype
    )
    grad_latent = grid_grad[..., :channels] + grid_grad[..., channels:] + padded_mix(grad_padded)
    totals = lax.psum((grad_in, grad_out, grad_gain, head_grad), ("band", "lon"))
    return (
        grad_latent,
        totals[0] / devices_all,
        totals[1] / devices_all,
        totals[2] / devices_all,
        totals[3] / devices_all,
    )


def solution(mesh):
    return jax.shard_map(
        body,
        mesh=mesh,
        in_specs=(
            P("band", "lon", None),
            P("band", "lon", None),
            P(("band", "lon"), None, None),
            P(("band", "lon"), None),
            P(("band", "lon")),
            P(("band", "lon"), None, None),
            P(),
            P(),
            P(),
            P(),
        ),
        out_specs=(P("band", "lon", None), P(), P(), P(), P()),
        check_vma=False,
    )
```

profile of v0, /device:TPU:1, one launch (start us, length us, event | category | flops | bytes accessed | tf_op | source)
XLA Modules:
  0.0 456.2 jit_solution(16606701495915434797)
XLA Ops:
  7.2 2.9 copy.28
  10.1 2.7 collective-permute-start
  12.8 0.8 collective-permute-done
  13.6 2.6 collective-permute-done.1
  16.5 0.8 multiply_reduce_fusion.2
  17.4 0.8 multiply_convert_fusion.5
  18.5 5.2 %multiply_convert_fusion.1 = (bf16[32,128,512]{2,1,0:T(8,128)(2,1)S(1)}, f32[32,128,512]{2,1,0:T(8,128)}) fusion(bf16[256,512]{1,0:T(8,128)(2,1)S(1)} %copy-done.21, bf16[32,128,256]{2,0,1:T(8,128)(2,1)S(1)} %multiply_convert_fusion.5), kind=kOutput, calls=%fused_computation.2 | convolution fusion | flops 1084227584 | bytes 14942208 | tf_op jit(solution)/shard_map/lmc,ch->lmh/dot_general | solution.py:99
  23.7 1.9 copy-done.10
  25.6 1.3 add_convert_fusion.1
  26.9 2.3 pad_maximum_fusion
  29.2 5.0 %gather_fusion = bf16[32,128,512]{2,1,0:T(8,128)(2,1)} fusion(bf16[32,128,512]{2,1,0:T(8,128)(2,1)} %pad_maximum_fusion, s32[1024]{0:T(1024)S(1)} %pad_clamp_fusion), kind=kCustom, calls=%fused_computation | custom fusion | bytes 8388736 | tf_op jit(solution)/shard_map/gather | solution.py:107
  34.2 6.4 %all-to-all-start = ((bf16[16,2,128,512]{3,2,1,0:T(8,128)(2,1)}), bf16[16,2,128,512]{3,2,1,0:T(8,128)(2,1)}, u32[]{:S(2)}, u32[]{:S(2)}) async-start(bf16[16,2,128,512]{3,2,1,0:T(8,128)(2,1)} %bitcast.68), calls=%async_computation | async-start | bytes 8388608 | tf_op jit(solution)/shard_map/all_to_all | solution.py:115
  40.8 56.3 %all-to-all-done = bf16[16,2,128,512]{3,2,1,0:T(8,128)(2,1)} async-done(((bf16[16,2,128,512]{3,2,1,0:T(8,128)(2,1)}), bf16[16,2,128,512]{3,2,1,0:T(8,128)(2,1)}, u32[]{:S(2)}, u32[]{:S(2)}) %all-to-all-start) | async-done | bytes 4194336 | tf_op jit(solution)/shard_map/all_to_all | solution.py:115
  97.0 2.3 fusion.18
  99.4 2.6 add_convert_fusion
  102.0 1.4 copy-done.6
  103.4 2.3 fusion.2
  105.7 1.1 copy-done.8
  106.7 0.7 convolution_convert_fusion
  107.4 3.4 copy.32
  110.9 3.0 fusion.24
  113.9 0.4 copy-done.3
  114.3 2.0 fusion.25
  116.3 3.9 copy.34
  120.3 2.6 copy.35
  122.8 4.6 %pad_maximum_fusion.1 = bf16[16,2,128,512]{3,2,1,0:T(8,128)(2,1)} fusion(bf16[16,2,128,256]{3,2,1,0:T(8,128)(2,1)} %copy.35, bf16[16,2,128,256]{3,2,1,0:T(8,128)(2,1)} %copy.34), kind=kLoop, calls=%fused_computation.21 | loop fusion | flops 8388608 | bytes 8388608 | tf_op jit(solution)/shard_map/concatenate | solution.py:59
  127.5 5.1 %all-to-all-start.1 = ((bf16[16,2,128,512]{3,2,1,0:T(8,128)(2,1)}), bf16[16,2,128,512]{3,2,1,0:T(8,128)(2,1)}, u32[]{:S(2)}, u32[]{:S(2)}) async-start(bf16[16,2,128,512]{3,2,1,0:T(8,128)(2,1)} %pad_maximum_fusion.1), calls=%async_computation.1 | async-start | bytes 8388608 | tf_op jit(solution)/shard_map/all_to_all | solution.py:128
  132.9 1.4 fusion.47
  134.3 54.1 %all-to-all-done.1 = bf16[16,2,128,512]{3,2,1,0:T(8,128)(2,1)} async-done(((bf16[16,2,128,512]{3,2,1,0:T(8,128)(2,1)}), bf16[16,2,128,512]{3,2,1,0:T(8,128)(2,1)}, u32[]{:S(2)}, u32[]{:S(2)}) %all-to-all-start.1) | async-done | bytes 4194336 | tf_op jit(solution)/shard_map/all_to_all | solution.py:128
  188.4 5.4 %fusion.3 = f32[32,128,512]{2,0,1:T(8,128)S(1)} fusion(s32[32]{0:T(128)S(1)} %bitcast.74, bf16[4,8,128,512]{3,2,1,0:T(8,128)(2,1)} %bitcast.28), kind=kOutput, calls=%fused_computation.9 | convolution fusion | flops 134218752 | bytes 12583040 | tf_op jit(solution)/shard_map/br,bx->rx/dot_general | solution.py:135
  194.2 4.9 %copy-done.11 = bf16[32,128,512]{2,1,0:T(8,128)(2,1)S(1)} copy-done((bf16[32,128,512]{2,1,0:T(8,128)(2,1)S(1)}, bf16[32,128,512]{2,1,0:T(8,128)(2,1)}, u32[]{:S(2)}) %copy-start.11) | copy-done | bytes 4194328
  199.1 3.6 fusion.32
  202.6 6.6 %multiply_convert_fusion = bf16[32,128,512]{2,1,0:T(8,128)(2,1)S(1)} fusion(f32[32,128,512]{2,1,0:T(8,128)} %get-tuple-element.27, bf16[32,128,256]{2,0,1:T(8,128)(2,1)S(1)} %slice.98, bf16[512,256]{1,0:T(8,128)(2,1)S(1)} %copy-done.14), kind=kOutput, calls=%fused_computation.1 | convolution fusion | flops 1092616192 | bytes 14942208 | tf_op jit(solution)/shard_map/lmc,hc->lmh/dot_general | solution.py:144
  209.2 1.9 copy-done.23
  211.2 3.7 fusion.29
  214.8 8.9 %multiply_reduce_fusion = (f32[256]{0:T(256)S(1)}, f32[32,128]{0,1:T(8,128)S(1)}, f32[32,128,256]{2,0,1:T(8,128)}) fusion(f32[32,128,256]{2,0,1:T(8,128)} %copy-done.4, f32[32,128]{0,1:T(8,128)S(1)} %add_rsqrt_fusion, f32[256]{0:T(256)S(1)} %copy-done.17, bf16[256,512]{1,0:T(8,128)(2,1)S(1)} %copy-done.22, bf16[32,128,512]{2,1,0:T(8,128)(2,1)} %copy-done.23), kind=kOutput, calls=%fused_computation.22 | convolution fusion | flops 1080028928 | bytes 12879872 | tf_op jit(solution)/shard_map/lmh,ch->lmc/dot_general | solution.py:147
  223.7 67.3 %psum.30 = f32[256]{0:T(256)S(1)} all-reduce(f32[256]{0:T(256)S(1)} %get-tuple-element.15), channel_id=1, replica_groups=mesh['band'=8,'lon'=16] {'band','lon'}, use_global_device_ids=true, to_apply=%region_5.6 | all-reduce | flops 256 | bytes 2048 | tf_op jit(solution)/shard_map/psum | solution.py:157
  291.1 4.1 multiply_convert_fusion.2
  295.2 0.7 collective-permute-start.2
  295.9 0.5 collective-permute-start.3
  296.4 0.6 broadcast_multiply_fusion.4
  297.0 2.0 collective-permute-done.3
  299.4 5.1 %fusion.8 = f32[32,128,256]{2,0,1:T(8,128)S(1)} fusion(f32[32,130,256]{2,0,1:T(8,128)S(1)} %maximum_convert_fusion.1, f32[32,128,512]{2,0,1:T(8,128)} %copy-done.2), kind=kLoop, calls=%fused_computation.15 | loop fusion | flops 5242880 | bytes 25165824 | tf_op jit(solution)/shard_map/add | solution.py:156
  304.5 4.4 copy.43
  309.0 135.1 %all-reduce.3.cloned.1.call-done = (f32[256,512]{1,0:T(8,128)}, f32[512,256]{1,0:T(8,128)}, f32[256,128]{1,0:T(8,128)}) async-done(((f32[256,512]{1,0:T(8,128)}, f32[512,256]{1,0:T(8,128)}, f32[256,128]{1,0:T(8,128)}), (f32[256,512]{1,0:T(8,128)}, f32[512,256]{1,0:T(8,128)}, f32[256,128]{1,0:T(8,128)})) %all-reduce.3.cloned.1.call-update) | async-done | bytes 1179664 | tf_op jit(solution)/shard_map/psum | solution.py:157
  444.1 1.9 broadcast_multiply_fusion.1
  445.9 1.6 broadcast_multiply_fusion.2
  447.5 1.9 broadcast_multiply_fusion
  (59 shorter events, 1.8 us)
Async XLA Ops:
  7.2 89.9 %copy-start = (bf16[32,128,128]{2,1,0:T(8,128)(2,1)S(1)}, bf16[32,128,128]{2,1,0:T(8,128)(2,1)}, u32[]{:S(2)}) copy-start(bf16[32,128,128]{2,1,0:T(8,128)(2,1)} %param.12) | copy-start | bytes 3145732
  7.2 5.6 %copy-start.18 = (s32[1,1,32]{2,1,0:T(1,128)S(1)}, s32[1,1,32]{2,1,0:T(1,128)}, u32[]{:S(2)}) copy-start(s32[1,1,32]{2,1,0:T(1,128)} %param.11) | copy-start | bytes 388
  10.1 3.5 collective-permute-start
  12.7 3.5 collective-permute-start.1
  16.5 0.9 copy-start.17
  17.4 6.3 %copy-start.4 = (f32[32,128,256]{2,0,1:T(8,128)}, f32[32,128,256]{2,0,1:T(8,128)S(1)}, u32[]{:S(2)}) copy-start(f32[32,128,256]{2,0,1:T(8,128)S(1)} %get-tuple-element.21) | copy-start | bytes 12582916
  17.4 1.1 copy-start.21
  18.5 5.2 %copy-start.12 = (bf16[32,128,256]{2,0,1:T(8,128)(2,1)}, bf16[32,128,256]{2,0,1:T(8,128)(2,1)S(1)}, u32[]{:S(2)}) copy-start(bf16[32,128,256]{2,0,1:T(8,128)(2,1)S(1)} %multiply_convert_fusion.5) | copy-start | bytes 6291460
  18.5 7.1 %copy-start.5 = (bf16[32,128,256]{2,1,0:T(8,128)(2,1)S(1)}, bf16[32,128,256]{2,1,0:T(8,128)(2,1)}, u32[]{:S(2)}) copy-start(bf16[32,128,256]{2,1,0:T(8,128)(2,1)} %param.10) | copy-start | bytes 6291460
  18.5 7.1 %copy-start.14 = (bf16[512,256]{1,0:T(8,128)(2,1)S(1)}, bf16[512,256]{1,0:T(8,128)(2,1)}, u32[]{:S(2)}) copy-start(bf16[512,256]{1,0:T(8,128)(2,1)} %param.18) | copy-start | bytes 786436
  23.7 1.9 copy-start.10
  34.2 6.5 %copy-start.16 = (s32[32,128]{1,0:T(8,128)S(1)}, s32[32,128]{1,0:T(8,128)}, u32[]{:S(2)}) copy-start(s32[32,128]{1,0:T(8,128)} %param.13) | copy-start | bytes 49156
  34.2 6.5 %copy-start.19 = (s32[32]{0:T(128)S(1)}, s32[32]{0:T(128)}, u32[]{:S(2)}) copy-start(s32[32]{0:T(128)} %param.14) | copy-start | bytes 388
  34.2 62.8 %all-to-all-start = ((bf16[16,2,128,512]{3,2,1,0:T(8,128)(2,1)}), bf16[16,2,128,512]{3,2,1,0:T(8,128)(2,1)}, u32[]{:S(2)}, u32[]{:S(2)}) async-start(bf16[16,2,128,512]{3,2,1,0:T(8,128)(2,1)} %bitcast.68), calls=%async_computation | async-start | bytes 8388608 | tf_op jit(solution)/shard_map/all_to_all | solution.py:115
  99.3 4.1 copy-start.15
  99.3 4.1 copy-start.20
  102.0 1.4 copy-start.6
  105.7 1.1 copy-start.8
  110.9 3.4 copy-start.3
  127.5 5.4 %copy-start.7 = (bf16[32,256,128]{1,2,0:T(8,128)(2,1)S(1)}, bf16[32,256,128]{1,2,0:T(8,128)(2,1)}, u32[]{:S(2)}) copy-start(bf16[32,256,128]{1,2,0:T(8,128)(2,1)} %copy-done.6) | copy-start | bytes 6291460
  127.5 5.4 %copy-start.9 = (bf16[4096,128]{1,0:T(8,128)(2,1)S(1)}, bf16[4096,128]{1,0:T(8,128)(2,1)}, u32[]{:S(2)}) copy-start(bf16[4096,128]{1,0:T(8,128)(2,1)} %copy-done.8) | copy-start | bytes 3145732
  127.5 60.9 %all-to-all-start.1 = ((bf16[16,2,128,512]{3,2,1,0:T(8,128)(2,1)}), bf16[16,2,128,512]{3,2,1,0:T(8,128)(2,1)}, u32[]{:S(2)}, u32[]{:S(2)}) async-start(bf16[16,2,128,512]{3,2,1,0:T(8,128)(2,1)} %pad_maximum_fusion.1), calls=%async_computation.1 | async-start | bytes 8388608 | tf_op jit(solution)/shard_map/all_to_all | solution.py:128
  132.6 311.5 %all-reduce.3.cloned.1.call-start = ((), (), s32[]{:S(2)}) async-start(), calls=%async_computation.2 | async-start | bytes 2359296 | tf_op jit(solution)/shard_map/psum | solution.py:157
  193.8 8.8 %copy-start.2 = (f32[32,128,512]{2,0,1:T(8,128)}, f32[32,128,512]{2,0,1:T(8,128)S(1)}, u32[]{:S(2)}) copy-start(f32[32,128,512]{2,0,1:T(8,128)S(1)} %fusion.3) | copy-start | bytes 25165828
  193.8 5.2 %copy-start.11 = (bf16[32,128,512]{2,1,0:T(8,128)(2,1)S(1)}, bf16[32,128,512]{2,1,0:T(8,128)(2,1)}, u32[]{:S(2)}) copy-start(bf16[32,128,512]{2,1,0:T(8,128)(2,1)} %copy-done.10) | copy-start | bytes 12582916
  202.6 8.5 %copy-start.13 = (bf16[32,128,256]{2,0,1:T(8,128)(2,1)S(1)}, bf16[32,128,256]{2,0,1:T(8,128)(2,1)}, u32[]{:S(2)}) copy-start(bf16[32,128,256]{2,0,1:T(8,128)(2,1)} %copy-done.12) | copy-start | bytes 6291460
  209.2 2.0 copy-start.23
  211.1 3.7 copy-start.22
  295.2 1.8 collective-permute-start.2
  295.9 3.2 collective-permute-start.3
  299.4 150.0 %copy-start.1 = (bf16[32,128,128]{2,1,0:T(8,128)(2,1)S(1)}, bf16[32,128,128]{2,1,0:T(8,128)(2,1)}, u32[]{:S(2)}) copy-start(bf16[32,128,128]{2,1,0:T(8,128)(2,1)} %param.12) | copy-start | bytes 3145732
Sparse Core Ops, SparseCore 0:
  297.2 146.8 all-reduce.2
where the time goes:
time: 457 us; the launch traced here: 456 us
  waiting for transfers between devices  251 us (55%)
  blocking collectives  67.3 us (15%)
  matrix products  48.9 us (11%)
  local copies, waits for them, and re-layouts  34.6 us (8%)
  other arithmetic  24.4 us (5%)
  starting transfers between devices  15.7 us (3%)
  between operations  14.3 us (3%)
    psum x1, waiting for transfers between devices, body(): lax.psum((grad_in, grad_out, grad_gain, head_grad), ('band', 'lon'))  135 us
    psum x1, blocking collectives, body(): lax.psum((grad_in, grad_out, grad_gain, head_grad), ('band', 'lon'))  67.3 us
    all_to_all x1, waiting for transfers between devices, body(): lax.all_to_all(picked.reshape(peer_count, per_peer, lon_cells, 2 * channe...  56.3 us
    all_to_all x1, waiting for transfers between devices, body(): lax.all_to_all(tile_grads.reshape(peer_count, per_peer, lon_cells, 2 * ch...  54.1 us
    unnamed x50, local copies, waits for them, and re-layouts  19.3 us
  transfers between devices with their start and end apart: 7, of which 6 were waited for; matrix products, arithmetic and copies ran while one was open for 3% of the time, Pallas kernels for 0%

commit v1 on v0

v1 whole, which is shorter than its diff:
```python
import functools
import math

import jax
import jax.numpy as jnp
from jax import lax
from jax.experimental import pallas as pl
from jax.experimental.pallas import tpu as pltpu
from jax.sharding import PartitionSpec as P

WINDOW_SLOTS = 7
NORM_EPS = 1e-05
ROWS_STEP = 4
BLOCKS_STEP = 4
META = 8
VMEM_LIMIT = 48 * 2**20

f32 = jnp.float32
bf16 = jnp.bfloat16


def dot(a, b):
    return jnp.dot(a, b, preferred_element_type=f32)


def dot_t(a, b):
    return lax.dot_general(a, b, (((0,), (0,)), ((), ())), preferred_element_type=f32)


def params(**kw):
    return pltpu.CompilerParams(vmem_limit_bytes=VMEM_LIMIT, **kw)


def cost(flops, nbytes, trans=0):
    return pl.CostEstimate(flops=flops, bytes_accessed=nbytes, transcendentals=trans)


def pack_kernel(counts, slot_ref, w_hbm, t_hbm, out_hbm, meta, sems):
    blocks, obs = slot_ref.shape
    nv = t_hbm.shape[1]
    copies = [
        pltpu.make_async_copy(w_hbm, out_hbm.at[:, pl.ds(0, obs), :], sems.at[0]),
        pltpu.make_async_copy(t_hbm, out_hbm.at[:, pl.ds(obs, nv), :], sems.at[1]),
    ]
    for c in copies:
        c.start()
    coef = slot_ref[...].astype(f32) / (WINDOW_SLOTS - 1)
    lane = lax.broadcasted_iota(jnp.int32, (META, obs), 1)
    row = lax.broadcasted_iota(jnp.int32, (META, obs), 0)
    for b in range(blocks):
        live = jnp.where(lane < counts[b], 1.0, 0.0)
        meta[b] = jnp.where(row == 0, coef[b : b + 1, :], live).astype(bf16)
    last = pltpu.make_async_copy(meta, out_hbm.at[:, pl.ds(obs + nv, META), :], sems.at[2])
    last.start()
    for c in copies:
        c.wait()
    last.wait()


def pack(weights, targets, slots, counts):
    blocks, obs, cells = weights.shape
    return pl.pallas_call(
        pack_kernel,
        out_shape=jax.ShapeDtypeStruct((blocks, 2 * obs + META, cells), bf16),
        in_specs=[
            pl.BlockSpec(memory_space=pltpu.SMEM),
            pl.BlockSpec(memory_space=pltpu.VMEM),
            pl.BlockSpec(memory_space=pl.ANY),
            pl.BlockSpec(memory_space=pl.ANY),
        ],
        out_specs=pl.BlockSpec(memory_space=pl.ANY),
        scratch_shapes=[pltpu.VMEM((blocks, META, obs), bf16), pltpu.SemaphoreType.DMA((3,))],
        compiler_params=params(),
        cost_estimate=cost(1, 4 * 2**20),
        name="pack",
    )(counts, slots, weights, targets)


def mixed(x, left, right):
    cells = x.shape[1]
    place = lax.broadcasted_iota(jnp.int32, x.shape, 1)
    from_left = jnp.where(place == 0, left, pltpu.roll(x, 1, 1))
    from_right = jnp.where(place == cells - 1, right, pltpu.roll(x, cells - 1, 1))
    return x + 0.5 * (from_left + from_right)


def normalized(lat, left, right):
    summed = mixed(lat, left, right)
    inv = lax.rsqrt(jnp.mean(summed * summed, axis=-1, keepdims=True) + NORM_EPS)
    return summed * inv, inv


def forward_kernel(lat_ref, left_ref, right_ref, gain_ref, w_in_ref, w_out_ref, stk_ref, slope_ref, act_t_ref, xhat_t_ref):
    rows, cells, ch = lat_ref.shape
    lat_b = lat_ref[...]
    lat = lat_b.astype(f32)
    xhat, _ = normalized(lat, left_ref[...], right_ref[...])
    xhat = xhat.reshape(rows * cells, ch)
    pre = dot((xhat * gain_ref[...]).astype(bf16), w_in_ref[...])
    sig = jax.nn.sigmoid(pre)
    act = pre * sig
    act_b = act.astype(bf16)
    slope_ref[...] = (sig * (1.0 + pre * (1.0 - sig))).astype(bf16)
    new = lat.reshape(rows * cells, ch) + dot(act_b, w_out_ref[...])
    stk_ref[:, 0:cells, :] = lat_b
    stk_ref[:, cells : 2 * cells, :] = new.astype(bf16).reshape(rows, cells, ch)
    act_t_ref[...] = act_b.T
    xhat_t_ref[...] = xhat.astype(bf16).T


def forward(latent, left, right, gain, w_in, w_out):
    rows, cells, ch = latent.shape
    hid = w_in.shape[1]
    n = rows * cells
    step = ROWS_STEP * cells
    return pl.pallas_call(
        forward_kernel,
        grid=(rows // ROWS_STEP,),
        out_shape=(
            jax.ShapeDtypeStruct((rows, 2 * cells, ch), bf16),
            jax.ShapeDtypeStruct((n, hid), bf16),
            jax.ShapeDtypeStruct((hid, n), bf16),
            jax.ShapeDtypeStruct((ch, n), bf16),
        ),
        in_specs=[
            pl.BlockSpec((ROWS_STEP, cells, ch), lambda i: (i, 0, 0)),
            pl.BlockSpec((ROWS_STEP, 1, ch), lambda i: (i, 0, 0)),
            pl.BlockSpec((ROWS_STEP, 1, ch), lambda i: (i, 0, 0)),
            pl.BlockSpec((1, ch), lambda i: (0, 0)),
            pl.BlockSpec((ch, hid), lambda i: (0, 0)),
            pl.BlockSpec((hid, ch), lambda i: (0, 0)),
        ],
        out_specs=(
            pl.BlockSpec((ROWS_STEP, 2 * cells, ch), lambda i: (i, 0, 0)),
            pl.BlockSpec((step, hid), lambda i: (i, 0)),
            pl.BlockSpec((hid, step), lambda i: (0, i)),
            pl.BlockSpec((ch, step), lambda i: (0, i)),
        ),
        compiler_params=params(),
        cost_estimate=cost(4 * n * ch * hid, 16 * 2**20, 2 * n * hid),
        name="forward",
    )(latent, left, right, gain, w_in, w_out)


def decode_kernel(
    rows_ref, got_ref, stk_ref, head_ref, head_t_ref, w_out_t_ref, slope_ref, act_t_ref, xhat_t_ref,
    pre_grad_ref, both_ref, sums_ref,
    acc_both, acc_new, acc_head, acc_in, acc_out,
    *, obs_steps, row_steps,
):
    i = pl.program_id(0)
    nb = got_ref.shape[0]
    ch, nv = head_ref.shape
    obs = (got_ref.shape[1] - META) // 2
    cells = got_ref.shape[2]
    scale = 1.0 / math.sqrt(obs)

    @pl.when(i == 0)
    def _():
        acc_both[...] = jnp.zeros_like(acc_both)
        acc_new[...] = jnp.zeros_like(acc_new)
        acc_head[...] = jnp.zeros_like(acc_head)
        acc_in[...] = jnp.zeros_like(acc_in)
        acc_out[...] = jnp.zeros_like(acc_out)

    @pl.when(i < obs_steps)
    def _():
        places = [rows_ref[0, 0, i * nb + j] for j in range(nb)]
        latents, coefs, lives = [], [], []
        for j in range(nb):
            meta = got_ref[j, 2 * obs : 2 * obs + META, :].astype(f32).T
            t, live = meta[:, 0:1], meta[:, 1:2]
            w = got_ref[j, 0:obs, :].astype(f32)
            pair = jnp.concatenate([(w * (1.0 - t)).astype(bf16), (w * t).astype(bf16)], axis=1)
            latents.append(dot(pair, stk_ref[places[j]]).astype(bf16))
            coefs.append(t)
            lives.append(live)
        obs_latent = jnp.concatenate(latents, axis=0)
        pred = dot(obs_latent, head_ref[...])
        goals = jnp.concatenate([got_ref[j, obs : 2 * obs, :] for j in range(nb)], axis=0)
        live = jnp.concatenate(lives, axis=0)
        residual = jnp.where(live > 0.5, pred - goals.astype(f32), 0.0)
        pred_grad = (residual * scale).astype(bf16)
        acc_head[...] += dot_t(pred_grad, obs_latent)
        grad = dot(pred_grad, head_t_ref[...])
        for j in range(nb):
            g = grad[j * obs : (j + 1) * obs, :]
            w = got_ref[j, 0:obs, :]
            pulled = dot_t(w, jnp.concatenate([g.astype(bf16), (g * coefs[j]).astype(bf16)], axis=1))
            acc_both[places[j]] += pulled[:, :ch]
            acc_new[places[j]] += pulled[:, ch:]

    @pl.when(i >= obs_steps)
    def _():
        k = i - obs_steps
        nr = both_ref.shape[0]
        both_ref[...] = acc_both[pl.ds(k * nr, nr)]
        adv = acc_new[pl.ds(k * nr, nr)].reshape(nr * cells, ch).astype(bf16)
        pre_grad = (dot(adv, w_out_t_ref[...]) * slope_ref[...].astype(f32)).astype(bf16)
        pre_grad_ref[...] = pre_grad
        acc_in[...] += dot(xhat_t_ref[...], pre_grad)
        acc_out[...] += dot(act_t_ref[...], adv)

    @pl.when(i == obs_steps + row_steps - 1)
    def _():
        put_chunks(sums_ref, 0, acc_in)
        put_chunks(sums_ref, 1, acc_out)
        put_chunks(sums_ref, 2, acc_head)
        left = acc_head.shape[0] * acc_head.shape[1] // (8 * 128)
        sums_ref[left:, 16:24, :] = jnp.zeros((sums_ref.shape[0] - left, 8, 128), bf16)


def put_chunks(sums_ref, part, acc):
    down = acc.shape[0] // 8
    for j in range(acc.shape[1] // 128):
        tiles = acc[:, 128 * j : 128 * (j + 1)].reshape(down, 8, 128)
        sums_ref[down * j : down * (j + 1), 8 * part : 8 * part + 8, :] = tiles.astype(bf16)


def take_chunks(got_ref, part, shape):
    down = shape[0] // 8
    return jnp.concatenate(
        [
            got_ref[down * j : down * (j + 1), 8 * part : 8 * part + 8, :].astype(f32).reshape(shape[0], 128)
            for j in range(shape[1] // 128)
        ],
        axis=1,
    )


def decode(rows, got, stk, head, head_t, w_out_t, slope, act_t, xhat_t, chunks):
    nrow, two_cells, ch = stk.shape
    cells = two_cells // 2
    blocks = got.shape[0]
    nv = head.shape[1]
    hid = w_out_t.shape[1]
    n = nrow * cells
    obs_steps, row_steps = blocks // BLOCKS_STEP, nrow // ROWS_STEP
    step = ROWS_STEP * cells

    def at(i):
        return jnp.maximum(i - obs_steps, 0)

    once = pl.Buffered(1)
    return pl.pallas_call(
        functools.partial(decode_kernel, obs_steps=obs_steps, row_steps=row_steps),
        grid=(obs_steps + row_steps,),
        out_shape=(
            jax.ShapeDtypeStruct((n, hid), bf16),
            jax.ShapeDtypeStruct((nrow, cells, ch), f32),
            jax.ShapeDtypeStruct((chunks, 24, 128), bf16),
        ),
        in_specs=[
            pl.BlockSpec(memory_space=pltpu.SMEM),
            pl.BlockSpec((BLOCKS_STEP,) + got.shape[1:], lambda i: (jnp.minimum(i, obs_steps - 1), 0, 0)),
            pl.BlockSpec(stk.shape, lambda i: (0, 0, 0), pipeline_mode=once),
            pl.BlockSpec((ch, nv), lambda i: (0, 0)),
            pl.BlockSpec((nv, ch), lambda i: (0, 0)),
            pl.BlockSpec((ch, hid), lambda i: (0, 0)),
            pl.BlockSpec((step, hid), lambda i: (at(i), 0)),
            pl.BlockSpec((hid, step), lambda i: (0, at(i))),
            pl.BlockSpec((ch, step), lambda i: (0, at(i))),
        ],
        out_specs=(
            pl.BlockSpec((step, hid), lambda i: (at(i), 0)),
            pl.BlockSpec((ROWS_STEP, cells, ch), lambda i: (at(i), 0, 0)),
            pl.BlockSpec((chunks, 24, 128), lambda i: (0, 0, 0)),
        ),
        scratch_shapes=[
            pltpu.VMEM((nrow, cells, ch), f32),
            pltpu.VMEM((nrow, cells, ch), f32),
            pltpu.VMEM((nv, ch), f32),
            pltpu.VMEM((ch, hid), f32),
            pltpu.VMEM((hid, ch), f32),
        ],
        compiler_params=params(),
        cost_estimate=cost(10 * n * ch * hid, 24 * 2**20),
        name="decode",
    )(rows, got, stk, head, head_t, w_out_t, slope, act_t, xhat_t)


def backward_kernel(lat_ref, left_ref, right_ref, gain_ref, w_in_t_ref, pre_grad_ref, both_ref, out_ref, first_ref, last_ref):
    rows, cells, ch = lat_ref.shape
    xhat, inv = normalized(lat_ref[...].astype(f32), left_ref[...], right_ref[...])
    gained = dot(pre_grad_ref[...], w_in_t_ref[...]) * gain_ref[...]
    gained = gained.reshape(rows, cells, ch)
    summed_grad = inv * (gained - xhat * jnp.mean(gained * xhat, axis=-1, keepdims=True))
    out_ref[...] = both_ref[...] + mixed(summed_grad, jnp.zeros((), f32), jnp.zeros((), f32))
    first_ref[...] = summed_grad[:, 0:1, :]
    last_ref[...] = summed_grad[:, cells - 1 : cells, :]


def backward(latent, left, right, gain, w_in_t, pre_grad, both):
    rows, cells, ch = latent.shape
    hid = w_in_t.shape[0]
    step = ROWS_STEP * cells
    edge = pl.BlockSpec((ROWS_STEP, 1, ch), lambda i: (i, 0, 0))
    whole = pl.BlockSpec((ROWS_STEP, cells, ch), lambda i: (i, 0, 0))
    return pl.pallas_call(
        backward_kernel,
        grid=(rows // ROWS_STEP,),
        out_shape=(
            jax.ShapeDtypeStruct((rows, cells, ch), f32),
            jax.ShapeDtypeStruct((rows, 1, ch), f32),
            jax.ShapeDtypeStruct((rows, 1, ch), f32),
        ),
        in_specs=[
            whole,
            edge,
            edge,
            pl.BlockSpec((1, ch), lambda i: (0, 0)),
            pl.BlockSpec((hid, ch), lambda i: (0, 0)),
            pl.BlockSpec((step, hid), lambda i: (i, 0)),
            whole,
        ],
        out_specs=(whole, edge, edge),
        compiler_params=params(),
        cost_estimate=cost(2 * rows * cells * ch * hid, 16 * 2**20),
        name="backward",
    )(latent, left, right, gain, w_in_t, pre_grad, both)


def edges_kernel(left_ref, right_ref, grad_ref, out_ref):
    block = grad_ref[...]
    place = lax.broadcasted_iota(jnp.int32, block.shape, 1)
    at_start = pl.program_id(0) == 0
    add = 0.5 * jnp.where(at_start, left_ref[...], right_ref[...])
    hit = place == jnp.where(at_start, 0, block.shape[1] - 1)
    out_ref[...] = block + jnp.where(hit, add, 0.0)


def add_edges(grad, left, right):
    rows, cells, ch = grad.shape
    ends = pl.BlockSpec((rows, 8, ch), lambda i: (0, i * (cells // 8 - 1), 0))
    edge = pl.BlockSpec((rows, 1, ch), lambda i: (0, 0, 0))
    return pl.pallas_call(
        edges_kernel,
        grid=(2,),
        out_shape=jax.ShapeDtypeStruct(grad.shape, f32),
        in_specs=[edge, edge, ends],
        out_specs=ends,
        input_output_aliases={2: 0},
        compiler_params=params(),
        cost_estimate=cost(rows * 16 * ch, 2**20),
        name="edges",
    )(left, right, grad)


def total_kernel(got_ref, out_ref):
    total = jnp.sum(got_ref[...].astype(f32), axis=0, keepdims=True).astype(bf16)
    out_ref[...] = jnp.broadcast_to(total, out_ref.shape)


def total(got):
    return pl.pallas_call(
        total_kernel,
        out_shape=jax.ShapeDtypeStruct(got.shape, bf16),
        compiler_params=params(),
        cost_estimate=cost(got.size, 2 * got.size * 2),
        name="total",
    )(got)


def finish_kernel(got_ref, gain_ref, w_in_ref, in_ref, out_ref, gain_grad_ref, head_ref, *, devices):
    share = 1.0 / devices
    x = take_chunks(got_ref, 0, in_ref.shape) * share
    in_ref[...] = x * gain_ref[...]
    per_channel = jnp.sum(x * w_in_ref[...].astype(f32), axis=1, keepdims=True)
    gain_grad_ref[...] = jnp.broadcast_to(per_channel, (x.shape[0], 128)).T[0:1, :]
    out_ref[...] = take_chunks(got_ref, 1, out_ref.shape) * share
    head_ref[...] = (take_chunks(got_ref, 2, head_ref.shape[::-1]) * share).T


def finish(got, gain, w_in, head, devices):
    ch, hid = w_in.shape
    return pl.pallas_call(
        functools.partial(finish_kernel, devices=devices),
        out_shape=(
            jax.ShapeDtypeStruct((ch, hid), f32),
            jax.ShapeDtypeStruct((hid, ch), f32),
            jax.ShapeDtypeStruct((1, ch), f32),
            jax.ShapeDtypeStruct(head.shape, f32),
        ),
        compiler_params=params(),
        cost_estimate=cost(4 * ch * hid, 3 * 2**20),
        name="finish",
    )(got, gain.reshape(ch, 1), w_in)


def from_sides(first, last):
    count = lax.axis_size("lon")
    left = lax.ppermute(last, "lon", [(i, (i + 1) % count) for i in range(count)])
    right = lax.ppermute(first, "lon", [((i + 1) % count, i) for i in range(count)])
    return left, right


def body(latent, row_index, weights, slots, counts, targets, gain, w_in, w_out, head):
    both_axes = ("band", "lon")
    devices = lax.axis_size("band") * lax.axis_size("lon")
    cells = latent.shape[1]
    got = lax.all_to_all(pack(weights, targets, slots, counts), "lon", 0, 0, tiled=True)
    left, right = from_sides(latent[:, 0:1, :], latent[:, cells - 1 : cells, :])
    left, right = left.astype(f32), right.astype(f32)
    gain_row = gain.reshape(1, -1)
    stk, slope, act_t, xhat_t = forward(latent, left, right, gain_row, w_in, w_out)
    pre_grad, both, sums = decode(row_index, got, stk, head, head.T, w_out.T, slope, act_t, xhat_t, devices)
    parts = lax.all_to_all(sums, both_axes, 0, 0, tiled=True)
    grad, first, last = backward(latent, left, right, gain_row, w_in.T, pre_grad, both)
    grad_left, grad_right = from_sides(first.astype(bf16), last.astype(bf16))
    grad = add_edges(grad, grad_left.astype(f32), grad_right.astype(f32))
    chunks = lax.all_to_all(total(parts), both_axes, 0, 0, tiled=True)
    grad_in, grad_out, grad_gain, grad_head = finish(chunks, gain, w_in, head, devices)
    return grad, grad_in, grad_out, grad_gain.reshape(-1), grad_head


def solution(mesh):
    return jax.shard_map(
        body,
        mesh=mesh,
        in_specs=(
            P("band", "lon", None),
            P("band", "lon", None),
            P(("band", "lon"), None, None),
            P(("band", "lon"), None),
            P(("band", "lon")),
            P(("band", "lon"), None, None),
            P(),
            P(),
            P(),
            P(),
        ),
        out_specs=(P("band", "lon", None), P(), P(), P(), P()),
        check_vma=False,
    )
```

time: 457 us -> 128 us (0.28)
  waiting for transfers between devices: 251 us -> 30.7 us
  matrix products: 48.9 us -> 0 us
  Pallas kernels: 0 us -> 46 us
  blocking collectives: 67.3 us -> 26 us
  local copies, waits for them, and re-layouts: 34.6 us -> 7.5 us
  other arithmetic: 24.4 us -> 0.19 us
  between operations: 14.3 us -> 0.8 us
    psum x1 -> x0, waiting for transfers between devices: 135 us -> none  [body(): lax.psum((grad_in, grad_out, grad_gain, head_grad), ('band', 'lon'))]
    all_to_all x2, waiting for transfers between devices: 110 us -> 0.3 us  [the longest x1 0.3 us: body(): chunks = lax.all_to_all(total(parts), both_axes, 0, 0, tiled=True)]
    psum x1 -> x0, blocking collectives: 67.3 us -> none  [body(): lax.psum((grad_in, grad_out, grad_gain, head_grad), ('band', 'lon'))]
    dot_general x14 -> x0, matrix products: 48.9 us -> none  [the longest x1 8.91 us: body(): jnp.einsum('lmh,ch->lmc', pre_grad, w_in, preferred_element_type=jnp.floa...]
    pallas_call x0 -> x7, Pallas kernels: none -> 46 us  [the longest x1 23 us: decode(): pl.pallas_call(functools.partial(decode_kernel, obs_steps=obs_steps, row_...]
    all_to_all x0 -> x1, blocking collectives: none -> 26 us  [body(): parts = lax.all_to_all(sums, both_axes, 0, 0, tiled=True)]
    ppermute x4, waiting for transfers between devices: 5.46 us -> 30.4 us  [the longest x2 27.7 us: from_sides(): lax.ppermute(last, 'lon', [(i, (i + 1) % count) for i in range(count)])]
    unnamed x50 -> x27, local copies, waits for them, and re-layouts: 19.3 us -> 7.31 us
  transfers between devices with their start and end apart: 7 -> 6, of which waited for: 6 -> 4; matrix products, arithmetic and copies ran while one was open for 3% -> 1% of each run, Pallas kernels for 0% -> 15%
where the time goes in v1:
time: 128 us; the launch traced here: 126 us
  Pallas kernels  46 us (36%)
  waiting for transfers between devices  30.7 us (24%)
  blocking collectives  26 us (20%)
  starting transfers between devices  14.7 us (11%)
  local copies, waits for them, and re-layouts  7.5 us (6%)
    ppermute x2, waiting for transfers between devices, from_sides(): lax.ppermute(last, 'lon', [(i, (i + 1) % count) for i in range(count)])  27.7 us
    all_to_all x1, blocking collectives, body(): parts = lax.all_to_all(sums, both_axes, 0, 0, tiled=True)  26 us
    pallas_call x1, Pallas kernels, decode(): pl.pallas_call(functools.partial(decode_kernel, obs_steps=obs_steps, row_...  23 us
    pallas_call x1, Pallas kernels, backward(): pl.pallas_call(backward_kernel, grid=(rows // ROWS_STEP,), out_shape=(jax...  9.24 us
    pallas_call x1, Pallas kernels, forward(): pl.pallas_call(forward_kernel, grid=(rows // ROWS_STEP,), out_shape=(jax....  7.83 us
    unnamed x27, local copies, waits for them, and re-layouts  7.31 us
    all_to_all x1, starting transfers between devices, body(): lax.all_to_all(pack(weights, targets, slots, counts), 'lon', 0, 0, tiled=...  7.18 us
    all_to_all x1, starting transfers between devices, body(): chunks = lax.all_to_all(total(parts), both_axes, 0, 0, tiled=True)  4.02 us
  transfers between devices with their start and end apart: 6, of which 4 were waited for; matrix products, arithmetic and copies ran while one was open for 1% of the time, Pallas kernels for 15%

profile of v1, /device:TPU:1, one launch (start us, length us, event | category | flops | bytes accessed | tf_op | source)
XLA Modules:
  0.0 125.9 jit_solution(2141092235107761837)
XLA Ops:
  0.6 0.0 copy-start
  0.6 0.0 copy-start.1
  0.7 1.4 %copy-done.1 = bf16[32,128,128]{2,1,0:T(8,128)(2,1)S(1)} copy-done((bf16[32,128,128]{2,1,0:T(8,128)(2,1)S(1)}, bf16[32,128,128]{2,1,0:T(8,128)(2,1)}, u32[]{:S(2)}) %copy-start.1) | copy-done | bytes 1048600
  2.0 0.0 copy-start.2
  2.0 1.2 copy-done.2
  3.2 0.0 copy-start.6
  3.2 0.7 copy-done.6
  4.0 0.0 copy-start.8
  4.0 0.7 copy-done.8
  4.6 0.0 copy-start.4
  4.6 0.0 copy-start.5
  4.6 0.0 copy-start.3
  4.6 0.0 copy-start.7
  4.6 2.0 %pack.1 = bf16[32,264,128]{2,1,0:T(8,128)(2,1)} custom-call(s32[32]{0:T(128)S(1)} %copy-done.8, s32[32,128]{1,0:T(8,128)S(1)} %copy-done.6, bf16[32,128,128]{2,1,0:T(8,128)(2,1)S(1)} %copy-done.1, bf16[32,128,128]{2,1,0:T(8,128)(2,1)S(1)} %copy-done.2), custom_call_target="tpu_custom_call" | custom-call | flops 1 | bytes 4194304 | tf_op jit(solution)/shard_map/pack/pallas_call | solution.py:62
  6.6 7.2 %all-to-all-start = ((bf16[32,264,128]{2,1,0:T(8,128)(2,1)}), bf16[32,264,128]{2,1,0:T(8,128)(2,1)}, u32[]{:S(2)}, u32[]{:S(2)}) async-start(bf16[32,264,128]{2,1,0:T(8,128)(2,1)} %pack.1), calls=%async_computation | async-start | bytes 4325376 | tf_op jit(solution)/shard_map/all_to_all | solution.py:401
  13.8 0.0 copy-done
  13.8 0.1 fusion
  13.9 1.7 %collective-permute-start = (bf16[32,1,256]{2,1,0:T(2,128)(2,1)S(1)}, bf16[32,1,256]{2,1,0:T(2,128)(2,1)S(1)}, u32[]{:S(2)}, u32[]{:S(2)}) collective-permute-start(bf16[32,1,256]{2,1,0:T(2,128)(2,1)S(1)} %get-tuple-element.34), channel_id=1, source_target_pairs={{0,1},{1,2},{2,3},{3,4},{4,5},{5,6},{6,7},{7,8},{8,9},{9,10},{10,1... | collective-permute-start | bytes 49160 | tf_op jit(solution)/shard_map/ppermute | solution.py:392
  15.6 0.0 collective-permute-start.1
  15.6 0.0 copy-done.4
  15.6 0.1 copy.21
  15.7 0.0 copy-done.5
  15.7 0.0 copy-start.9
  15.7 0.1 copy.20
  15.9 26.9 %collective-permute-done = bf16[32,1,256]{2,1,0:T(2,128)(2,1)S(1)} collective-permute-done((bf16[32,1,256]{2,1,0:T(2,128)(2,1)S(1)}, bf16[32,1,256]{2,1,0:T(2,128)(2,1)S(1)}, u32[]{:S(2)}, u32[]{:S(2)}) %collective-permute-start) | collective-permute-done | bytes 16416 | tf_op jit(solution)/shard_map/ppermute | solution.py:392
  42.8 0.0 collective-permute-done.1
  42.9 0.0 copy-done.3
  42.9 0.0 copy-done.7
  42.9 7.8 %forward.1 = (bf16[32,256,256]{2,1,0:T(8,128)(2,1)}, bf16[4096,512]{1,0:T(8,128)(2,1)}, bf16[512,4096]{1,0:T(8,128)(2,1)}, bf16[256,4096]{1,0:T(8,128)(2,1)S(1)}) custom-call(bf16[32,128,256]{2,1,0:T(8,128)(2,1)S(1)} %copy-done, f32[32,1,256]{2,1,0:T(1,128)S(1)} %convert_element_type.18.left_ref, f32[32,1,256]{2,1,0:T(1,128)S(1)} %convert_element_type.19.right_ref, ...), custom_call_target="tpu_custom_call" | custom-call | flops 2147483648 | bytes 16777216 | tf_op jit(solution)/shard_map/forward/pallas_call | solution.py:116
  50.7 0.0 copy-start.10
  50.7 1.3 %copy-done.10 = bf16[256,4096]{1,0:T(8,128)(2,1)} copy-done((bf16[256,4096]{1,0:T(8,128)(2,1)}, bf16[256,4096]{1,0:T(8,128)(2,1)S(1)}, u32[]{:S(2)}) %copy-start.10) | copy-done | bytes 2097176
  52.1 0.0 all-to-all-done.got_ref
  52.1 0.0 copy-done.9
  52.1 1.6 %copy-done.11 = bf16[256,4096]{1,0:T(8,128)(2,1)S(1)} copy-done((bf16[256,4096]{1,0:T(8,128)(2,1)S(1)}, bf16[256,4096]{1,0:T(8,128)(2,1)}, u32[]{:S(2)}) %copy-start.11) | copy-done | bytes 2097176
  53.7 23.0 %decode.1 = (bf16[4096,512]{1,0:T(8,128)(2,1)}, f32[32,128,256]{2,1,0:T(8,128)}, bf16[128,24,128]{2,1,0:T(8,128)(2,1)S(1)}) custom-call(s32[1,1,32]{2,1,0:T(1,128)S(1)} %copy-done.9, bf16[32,264,128]{2,1,0:T(8,128)(2,1)} %all-to-all-done.got_ref, bf16[32,256,256]{2,1,0:T(8,128)(2,1)} %get-tuple-element.19.stk_ref, bf16[256,128]{1,0:T(8,128)(2,1)S(1)} %copy-done.5, ...), custom_call_target="tpu_custom_call" | custom-call | flops 5368709120 | bytes 25165824 | tf_op jit(solution)/shard_map/decode/pallas_call | solution.py:245
  76.7 26.0 %all_to_all.15.got_ref = bf16[128,24,128]{2,1,0:T(8,128)(2,1)S(1)} all-to-all(bf16[128,24,128]{2,1,0:T(8,128)(2,1)S(1)} %get-tuple-element.28), channel_id=1, replica_groups=mesh['band'=8,'lon'=16] {'band','lon'}, dimensions={0} | all-to-all | bytes 1572864 | tf_op jit(solution)/shard_map/all_to_all | solution.py:407
  102.7 1.1 total.1
  103.8 4.0 %all-to-all-start.2 = ((bf16[128,24,128]{2,1,0:T(8,128)(2,1)}), bf16[128,24,128]{2,1,0:T(8,128)(2,1)S(1)}, u32[]{:S(2)}, u32[]{:S(2)}) async-start(bf16[128,24,128]{2,1,0:T(8,128)(2,1)} %total.1), calls=%async_computation.2 | async-start | bytes 1572864 | tf_op jit(solution)/shard_map/all_to_all | solution.py:411
  107.8 0.1 copy.19
  107.9 9.2 %backward.1 = (f32[32,128,256]{2,1,0:T(8,128)}, f32[32,1,256]{2,1,0:T(1,128)S(1)}, f32[32,1,256]{2,1,0:T(1,128)S(1)}) custom-call(bf16[32,128,256]{2,1,0:T(8,128)(2,1)S(1)} %copy-done, f32[32,1,256]{2,1,0:T(1,128)S(1)} %convert_element_type.18.left_ref, f32[32,1,256]{2,1,0:T(1,128)S(1)} %convert_element_type.19.right_ref, f32[1,256]{1,0:T(1,128)S(1)} %bitcast.10, ...), custom_call_target="tpu_custom_call" | custom-call | flops 1073741824 | bytes 16777216 | tf_op jit(solution)/shard_map/backward/pallas_call | solution.py:299
  117.2 1.7 %collective-permute-start.2 = (bf16[32,1,256]{2,1,0:T(2,128)(2,1)S(1)}, bf16[32,1,256]{2,1,0:T(2,128)(2,1)S(1)}, u32[]{:S(2)}, u32[]{:S(2)}) collective-permute-start(bf16[32,1,256]{2,1,0:T(2,128)(2,1)S(1)} %convert_element_type.20), channel_id=1, source_target_pairs={{0,1},{1,2},{2,3},{3,4},{4,5},{5,6},{6,7},{7,8},{8,9},{9,10},{10,1... | collective-permute-start | bytes 49160 | tf_op jit(solution)/shard_map/ppermute | solution.py:392
  118.9 0.1 collective-permute-start.3
  119.0 0.1 copy.22.gain_ref
  119.2 0.8 collective-permute-done.2
  120.0 2.7 %collective-permute-done.3 = bf16[32,1,256]{2,1,0:T(2,128)(2,1)S(1)} collective-permute-done((bf16[32,1,256]{2,1,0:T(2,128)(2,1)S(1)}, bf16[32,1,256]{2,1,0:T(2,128)(2,1)S(1)}, u32[]{:S(2)}, u32[]{:S(2)}) %collective-permute-start.3) | collective-permute-done | bytes 16416 | tf_op jit(solution)/shard_map/ppermute | solution.py:393
  122.7 1.8 %edges.1 = f32[32,128,256]{2,1,0:T(8,128)} custom-call(f32[32,1,256]{2,1,0:T(1,128)S(1)} %convert_element_type.21.left_ref, f32[32,1,256]{2,1,0:T(1,128)S(1)} %convert_element_type.23.right_ref, f32[32,128,256]{2,1,0:T(8,128)} %get-tuple-element.27.grad_ref), custom_call_target="tpu_custom_call", output_to_operand_aliasing={{}: (2, {})} | custom-call | flops 131072 | bytes 1048576 | tf_op jit(solution)/shard_map/edges/pallas_call | solution.py:336
  124.5 0.3 all-to-all-done.2.got_ref
  124.8 1.1 finish.1
  (7 shorter events, 0.2 us)
Async XLA Ops:
  0.6 13.2 %copy-start = (bf16[32,128,256]{2,1,0:T(8,128)(2,1)S(1)}, bf16[32,128,256]{2,1,0:T(8,128)(2,1)}, u32[]{:S(2)}) copy-start(bf16[32,128,256]{2,1,0:T(8,128)(2,1)} %lat_ref.3) | copy-start | bytes 6291460
  0.6 1.4 %copy-start.1 = (bf16[32,128,128]{2,1,0:T(8,128)(2,1)S(1)}, bf16[32,128,128]{2,1,0:T(8,128)(2,1)}, u32[]{:S(2)}) copy-start(bf16[32,128,128]{2,1,0:T(8,128)(2,1)} %w_hbm.1) | copy-start | bytes 3145732
  2.0 1.2 copy-start.2
  3.2 0.7 copy-start.6
  4.0 0.7 copy-start.8
  4.6 11.0 %copy-start.4 = (bf16[512,256]{1,0:T(8,128)(2,1)S(1)}, bf16[512,256]{1,0:T(8,128)(2,1)}, u32[]{:S(2)}) copy-start(bf16[512,256]{1,0:T(8,128)(2,1)} %w_out_ref.1) | copy-start | bytes 786436
  4.6 11.1 %copy-start.5 = (bf16[256,128]{1,0:T(8,128)(2,1)S(1)}, bf16[256,128]{1,0:T(8,128)(2,1)}, u32[]{:S(2)}) copy-start(bf16[256,128]{1,0:T(8,128)(2,1)} %head_ref.1) | copy-start | bytes 196612
  4.6 38.3 %copy-start.3 = (bf16[256,512]{1,0:T(8,128)(2,1)S(1)}, bf16[256,512]{1,0:T(8,128)(2,1)}, u32[]{:S(2)}) copy-start(bf16[256,512]{1,0:T(8,128)(2,1)} %w_in_ref.3) | copy-start | bytes 786436
  4.6 38.3 %copy-start.7 = (f32[256]{0:T(256)S(1)}, f32[256]{0:T(256)}, u32[]{:S(2)}) copy-start(f32[256]{0:T(256)} %param.16) | copy-start | bytes 3076
  6.6 45.5 %all-to-all-start = ((bf16[32,264,128]{2,1,0:T(8,128)(2,1)}), bf16[32,264,128]{2,1,0:T(8,128)(2,1)}, u32[]{:S(2)}, u32[]{:S(2)}) async-start(bf16[32,264,128]{2,1,0:T(8,128)(2,1)} %pack.1), calls=%async_computation | async-start | bytes 4325376 | tf_op jit(solution)/shard_map/all_to_all | solution.py:401
  13.9 28.9 %collective-permute-start = (bf16[32,1,256]{2,1,0:T(2,128)(2,1)S(1)}, bf16[32,1,256]{2,1,0:T(2,128)(2,1)S(1)}, u32[]{:S(2)}, u32[]{:S(2)}) collective-permute-start(bf16[32,1,256]{2,1,0:T(2,128)(2,1)S(1)} %get-tuple-element.34), channel_id=1, source_target_pairs={{0,1},{1,2},{2,3},{3,4},{4,5},{5,6},{6,7},{7,8},{8,9},{9,10},{10,1... | collective-permute-start | bytes 49160 | tf_op jit(solution)/shard_map/ppermute | solution.py:392
  15.6 27.3 %collective-permute-start.1 = (bf16[32,1,256]{2,1,0:T(2,128)(2,1)S(1)}, bf16[32,1,256]{2,1,0:T(2,128)(2,1)S(1)}, u32[]{:S(2)}, u32[]{:S(2)}) collective-permute-start(bf16[32,1,256]{2,1,0:T(2,128)(2,1)S(1)} %get-tuple-element.33), channel_id=1, source_target_pairs={{1,0},{2,1},{3,2},{4,3},{5,4},{6,5},{7,6},{8,7},{9,8},{10,9},{11,1... | collective-permute-start | bytes 49160 | tf_op jit(solution)/shard_map/ppermute | solution.py:393
  15.7 36.4 %copy-start.9 = (s32[1,1,32]{2,1,0:T(1,128)S(1)}, s32[1,1,32]{2,1,0:T(1,128)}, u32[]{:S(2)}) copy-start(s32[1,1,32]{2,1,0:T(1,128)} %rows_ref.1) | copy-start | bytes 388
  50.7 1.3 %copy-start.10 = (bf16[256,4096]{1,0:T(8,128)(2,1)}, bf16[256,4096]{1,0:T(8,128)(2,1)S(1)}, u32[]{:S(2)}) copy-start(bf16[256,4096]{1,0:T(8,128)(2,1)S(1)} %get-tuple-element.22.xhat_t_ref) | copy-start | bytes 6291460
  52.1 1.6 %copy-start.11 = (bf16[256,4096]{1,0:T(8,128)(2,1)S(1)}, bf16[256,4096]{1,0:T(8,128)(2,1)}, u32[]{:S(2)}) copy-start(bf16[256,4096]{1,0:T(8,128)(2,1)} %copy-done.10) | copy-start | bytes 6291460
  103.8 21.0 %all-to-all-start.2 = ((bf16[128,24,128]{2,1,0:T(8,128)(2,1)}), bf16[128,24,128]{2,1,0:T(8,128)(2,1)S(1)}, u32[]{:S(2)}, u32[]{:S(2)}) async-start(bf16[128,24,128]{2,1,0:T(8,128)(2,1)} %total.1), calls=%async_computation.2 | async-start | bytes 1572864 | tf_op jit(solution)/shard_map/all_to_all | solution.py:411
  117.2 2.7 %collective-permute-start.2 = (bf16[32,1,256]{2,1,0:T(2,128)(2,1)S(1)}, bf16[32,1,256]{2,1,0:T(2,128)(2,1)S(1)}, u32[]{:S(2)}, u32[]{:S(2)}) collective-permute-start(bf16[32,1,256]{2,1,0:T(2,128)(2,1)S(1)} %convert_element_type.20), channel_id=1, source_target_pairs={{0,1},{1,2},{2,3},{3,4},{4,5},{5,6},{6,7},{7,8},{8,9},{9,10},{10,1... | collective-permute-start | bytes 49160 | tf_op jit(solution)/shard_map/ppermute | solution.py:392
  118.9 3.7 %collective-permute-start.3 = (bf16[32,1,256]{2,1,0:T(2,128)(2,1)S(1)}, bf16[32,1,256]{2,1,0:T(2,128)(2,1)S(1)}, u32[]{:S(2)}, u32[]{:S(2)}) collective-permute-start(bf16[32,1,256]{2,1,0:T(2,128)(2,1)S(1)} %convert_element_type.22), channel_id=1, source_target_pairs={{1,0},{2,1},{3,2},{4,3},{5,4},{6,5},{7,6},{8,7},{9,8},{10,9},{11,1... | collective-permute-start | bytes 49160 | tf_op jit(solution)/shard_map/ppermute | solution.py:393

commit v2 on v1

--- a/solution.py
+++ b/solution.py
@@ -11,12 +11,14 @@
 WINDOW_SLOTS = 7
 NORM_EPS = 1e-05
 ROWS_STEP = 4
-BLOCKS_STEP = 4
+BLOCKS_STEP = 8
+PULL_ROWS = 16
 META = 8
-VMEM_LIMIT = 48 * 2**20
 
 f32 = jnp.float32
 bf16 = jnp.bfloat16
+INSIDE = pl.BlockSpec(memory_space=pltpu.VMEM)
+OUTSIDE = pl.BlockSpec(memory_space=pltpu.HBM)
 
 
 def dot(a, b):
@@ -27,32 +29,42 @@
     return lax.dot_general(a, b, (((0,), (0,)), ((), ())), preferred_element_type=f32)
 
 
-def params(**kw):
-    return pltpu.CompilerParams(vmem_limit_bytes=VMEM_LIMIT, **kw)
+def params(mib=48):
+    return pltpu.CompilerParams(vmem_limit_bytes=mib * 2**20)
+
+
+def in_hbm(*arrays):
+    return [pltpu.with_memory_space_constraint(x, pltpu.HBM) for x in arrays]
 
 
 def cost(flops, nbytes, trans=0):
     return pl.CostEstimate(flops=flops, bytes_accessed=nbytes, transcendentals=trans)
 
 
-def pack_kernel(counts, slot_ref, w_hbm, t_hbm, out_hbm, meta, sems):
-    blocks, obs = slot_ref.shape
+def pack_kernel(w_hbm, t_hbm, slot_hbm, count_hbm, out_hbm, slots, counts, meta, sems):
+    blocks, obs = slots.shape
     nv = t_hbm.shape[1]
-    copies = [
-        pltpu.make_async_copy(w_hbm, out_hbm.at[:, pl.ds(0, obs), :], sems.at[0]),
-        pltpu.make_async_copy(t_hbm, out_hbm.at[:, pl.ds(obs, nv), :], sems.at[1]),
+    small = [
+        pltpu.make_async_copy(slot_hbm, slots, sems.at[0]),
+        pltpu.make_async_copy(count_hbm, counts, sems.at[1]),
     ]
-    for c in copies:
+    large = [
+        pltpu.make_async_copy(w_hbm, out_hbm.at[:, pl.ds(0, obs), :], sems.at[2]),
+        pltpu.make_async_copy(t_hbm, out_hbm.at[:, pl.ds(obs, nv), :], sems.at[3]),
+    ]
+    for c in small + large:
         c.start()
-    coef = slot_ref[...].astype(f32) / (WINDOW_SLOTS - 1)
+    for c in small:
+        c.wait()
+    coef = slots[...].astype(f32) / (WINDOW_SLOTS - 1)
     lane = lax.broadcasted_iota(jnp.int32, (META, obs), 1)
     row = lax.broadcasted_iota(jnp.int32, (META, obs), 0)
     for b in range(blocks):
         live = jnp.where(lane < counts[b], 1.0, 0.0)
         meta[b] = jnp.where(row == 0, coef[b : b + 1, :], live).astype(bf16)
-    last = pltpu.make_async_copy(meta, out_hbm.at[:, pl.ds(obs + nv, META), :], sems.at[2])
+    last = pltpu.make_async_copy(meta, out_hbm.at[:, pl.ds(obs + nv, META), :], sems.at[4])
     last.start()
-    for c in copies:
+    for c in large:
         c.wait()
     last.wait()
 
@@ -61,19 +73,19 @@
     blocks, obs, cells = weights.shape
     return pl.pallas_call(
         pack_kernel,
-        out_shape=jax.ShapeDtypeStruct((blocks, 2 * obs + META, cells), bf16),
-        in_specs=[
-            pl.BlockSpec(memory_space=pltpu.SMEM),
-            pl.BlockSpec(memory_space=pltpu.VMEM),
-            pl.BlockSpec(memory_space=pl.ANY),
-            pl.BlockSpec(memory_space=pl.ANY),
+        out_shape=pltpu.HBM((blocks, 2 * obs + META, cells), bf16),
+        in_specs=[OUTSIDE] * 4,
+        out_specs=OUTSIDE,
+        scratch_shapes=[
+            pltpu.VMEM(slots.shape, jnp.int32),
+            pltpu.SMEM(counts.shape, jnp.int32),
+            pltpu.VMEM((blocks, META, obs), bf16),
+            pltpu.SemaphoreType.DMA((5,)),
         ],
-        out_specs=pl.BlockSpec(memory_space=pl.ANY),
-        scratch_shapes=[pltpu.VMEM((blocks, META, obs), bf16), pltpu.SemaphoreType.DMA((3,))],
         compiler_params=params(),
         cost_estimate=cost(1, 4 * 2**20),
         name="pack",
-    )(counts, slots, weights, targets)
+    )(*in_hbm(weights, targets, slots, counts))
 
 
 def mixed(x, left, right):
@@ -117,10 +129,10 @@
         forward_kernel,
         grid=(rows // ROWS_STEP,),
         out_shape=(
-            jax.ShapeDtypeStruct((rows, 2 * cells, ch), bf16),
-            jax.ShapeDtypeStruct((n, hid), bf16),
-            jax.ShapeDtypeStruct((hid, n), bf16),
-            jax.ShapeDtypeStruct((ch, n), bf16),
+            pltpu.HBM((rows, 2 * cells, ch), bf16),
+            pltpu.HBM((n, hid), bf16),
+            pltpu.HBM((hid, n), bf16),
+            pltpu.HBM((ch, n), bf16),
         ),
         in_specs=[
             pl.BlockSpec((ROWS_STEP, cells, ch), lambda i: (i, 0, 0)),
@@ -143,41 +155,61 @@
 
 
 def decode_kernel(
-    rows_ref, got_ref, stk_ref, head_ref, head_t_ref, w_out_t_ref, slope_ref, act_t_ref, xhat_t_ref,
-    pre_grad_ref, both_ref, sums_ref,
-    acc_both, acc_new, acc_head, acc_in, acc_out,
-    *, obs_steps, row_steps,
+    rows_ref, got_hbm, stk_hbm, head_ref, head_t_ref, w_out_t_ref, slope_hbm, act_t_hbm, xhat_t_hbm,
+    pre_grad_hbm, both_hbm, sums_ref,
+    got, stk, slope, act_t, xhat_t, pre_grad_all, acc_both, acc_new, acc_head, acc_in, acc_out,
+    got_sems, stk_sems, in_sems, out_sems,
 ):
-    i = pl.program_id(0)
-    nb = got_ref.shape[0]
+    nb, nr = BLOCKS_STEP, PULL_ROWS
+    blocks = got.shape[0]
     ch, nv = head_ref.shape
-    obs = (got_ref.shape[1] - META) // 2
-    cells = got_ref.shape[2]
+    obs = (got.shape[1] - META) // 2
+    rows, cells, _ = acc_both.shape
     scale = 1.0 / math.sqrt(obs)
-
-    @pl.when(i == 0)
-    def _():
-        acc_both[...] = jnp.zeros_like(acc_both)
-        acc_new[...] = jnp.zeros_like(acc_new)
-        acc_head[...] = jnp.zeros_like(acc_head)
-        acc_in[...] = jnp.zeros_like(acc_in)
-        acc_out[...] = jnp.zeros_like(acc_out)
-
-    @pl.when(i < obs_steps)
-    def _():
-        places = [rows_ref[0, 0, i * nb + j] for j in range(nb)]
+    step = nr * cells
+
+    def got_copy(i):
+        here = pl.ds(i * nb, nb)
+        return pltpu.make_async_copy(got_hbm.at[here], got.at[here], got_sems.at[i])
+
+    def stk_copy(b):
+        return pltpu.make_async_copy(stk_hbm.at[rows_ref[0, 0, b]], stk.at[b], stk_sems.at[b])
+
+    def pre_grad_copy(k):
+        flat = pl.ds(pl.multiple_of(k * step, step), step)
+        return pltpu.make_async_copy(pre_grad_all.at[flat], pre_grad_hbm.at[flat], out_sems.at[k])
+
+    for i in range(blocks // nb):
+        got_copy(i).start()
+        for j in range(nb):
+            stk_copy(i * nb + j).start()
+    later = [
+        pltpu.make_async_copy(src, dst, in_sems.at[i])
+        for i, (src, dst) in enumerate(((slope_hbm, slope), (xhat_t_hbm, xhat_t), (act_t_hbm, act_t)))
+    ]
+    for c in later:
+        c.start()
+    for acc in (acc_both, acc_new, acc_head, acc_in, acc_out):
+        acc[...] = jnp.zeros_like(acc)
+
+    def observe(i, carry):
+        first = i * nb
+        got_copy(i).wait()
+        for j in range(nb):
+            stk_copy(first + j).wait()
+        places = [rows_ref[0, 0, first + j] for j in range(nb)]
         latents, coefs, lives = [], [], []
         for j in range(nb):
-            meta = got_ref[j, 2 * obs : 2 * obs + META, :].astype(f32).T
+            meta = got[first + j, 2 * obs : 2 * obs + META, :].astype(f32).T
             t, live = meta[:, 0:1], meta[:, 1:2]
-            w = got_ref[j, 0:obs, :].astype(f32)
+            w = got[first + j, 0:obs, :].astype(f32)
             pair = jnp.concatenate([(w * (1.0 - t)).astype(bf16), (w * t).astype(bf16)], axis=1)
-            latents.append(dot(pair, stk_ref[places[j]]).astype(bf16))
+            latents.append(dot(pair, stk[first + j]).astype(bf16))
             coefs.append(t)
             lives.append(live)
         obs_latent = jnp.concatenate(latents, axis=0)
         pred = dot(obs_latent, head_ref[...])
-        goals = jnp.concatenate([got_ref[j, obs : 2 * obs, :] for j in range(nb)], axis=0)
+        goals = jnp.concatenate([got[first + j, obs : 2 * obs, :] for j in range(nb)], axis=0)
         live = jnp.concatenate(lives, axis=0)
         residual = jnp.where(live > 0.5, pred - goals.astype(f32), 0.0)
         pred_grad = (residual * scale).astype(bf16)
@@ -185,29 +217,37 @@
         grad = dot(pred_grad, head_t_ref[...])
         for j in range(nb):
             g = grad[j * obs : (j + 1) * obs, :]
-            w = got_ref[j, 0:obs, :]
+            w = got[first + j, 0:obs, :]
             pulled = dot_t(w, jnp.concatenate([g.astype(bf16), (g * coefs[j]).astype(bf16)], axis=1))
             acc_both[places[j]] += pulled[:, :ch]
             acc_new[places[j]] += pulled[:, ch:]
-
-    @pl.when(i >= obs_steps)
-    def _():
-        k = i - obs_steps
-        nr = both_ref.shape[0]
-        both_ref[...] = acc_both[pl.ds(k * nr, nr)]
-        adv = acc_new[pl.ds(k * nr, nr)].reshape(nr * cells, ch).astype(bf16)
-        pre_grad = (dot(adv, w_out_t_ref[...]) * slope_ref[...].astype(f32)).astype(bf16)
-        pre_grad_ref[...] = pre_grad
-        acc_in[...] += dot(xhat_t_ref[...], pre_grad)
-        acc_out[...] += dot(act_t_ref[...], adv)
-
-    @pl.when(i == obs_steps + row_steps - 1)
-    def _():
-        put_chunks(sums_ref, 0, acc_in)
-        put_chunks(sums_ref, 1, acc_out)
-        put_chunks(sums_ref, 2, acc_head)
-        left = acc_head.shape[0] * acc_head.shape[1] // (8 * 128)
-        sums_ref[left:, 16:24, :] = jnp.zeros((sums_ref.shape[0] - left, 8, 128), bf16)
+        return carry
+
+    lax.fori_loop(0, blocks // nb, observe, 0)
+    both_copy = pltpu.make_async_copy(acc_both, both_hbm, out_sems.at[rows // nr])
+    both_copy.start()
+    for c in later:
+        c.wait()
+
+    def pull(k, carry):
+        flat = pl.ds(pl.multiple_of(k * step, step), step)
+        adv = acc_new[pl.ds(k * nr, nr)].reshape(step, ch).astype(bf16)
+        pre_grad = (dot(adv, w_out_t_ref[...]) * slope[flat, :].astype(f32)).astype(bf16)
+        pre_grad_all[flat, :] = pre_grad
+        pre_grad_copy(k).start()
+        acc_in[...] += dot(xhat_t[:, flat], pre_grad)
+        acc_out[...] += dot(act_t[:, flat], adv)
+        return carry
+
+    lax.fori_loop(0, rows // nr, pull, 0)
+    put_chunks(sums_ref, 0, acc_in)
+    put_chunks(sums_ref, 1, acc_out)
+    put_chunks(sums_ref, 2, acc_head)
+    left = acc_head.shape[0] * acc_head.shape[1] // (8 * 128)
+    sums_ref[left:, 16:24, :] = jnp.zeros((sums_ref.shape[0] - left, 8, 128), bf16)
+    both_copy.wait()
+    for k in range(rows // nr):
+        pre_grad_copy(k).wait()
 
 
 def put_chunks(sums_ref, part, acc):
@@ -231,52 +271,36 @@
 def decode(rows, got, stk, head, head_t, w_out_t, slope, act_t, xhat_t, chunks):
     nrow, two_cells, ch = stk.shape
     cells = two_cells // 2
-    blocks = got.shape[0]
     nv = head.shape[1]
     hid = w_out_t.shape[1]
     n = nrow * cells
-    obs_steps, row_steps = blocks // BLOCKS_STEP, nrow // ROWS_STEP
-    step = ROWS_STEP * cells
-
-    def at(i):
-        return jnp.maximum(i - obs_steps, 0)
-
-    once = pl.Buffered(1)
-    return pl.pallas_call(
-        functools.partial(decode_kernel, obs_steps=obs_steps, row_steps=row_steps),
-        grid=(obs_steps + row_steps,),
+    blocks = got.shape[0]
+    dma = pltpu.SemaphoreType.DMA
+    return pl.pallas_call(
+        decode_kernel,
         out_shape=(
-            jax.ShapeDtypeStruct((n, hid), bf16),
-            jax.ShapeDtypeStruct((nrow, cells, ch), f32),
-            jax.ShapeDtypeStruct((chunks, 24, 128), bf16),
-        ),
-        in_specs=[
-            pl.BlockSpec(memory_space=pltpu.SMEM),
-            pl.BlockSpec((BLOCKS_STEP,) + got.shape[1:], lambda i: (jnp.minimum(i, obs_steps - 1), 0, 0)),
-            pl.BlockSpec(stk.shape, lambda i: (0, 0, 0), pipeline_mode=once),
-            pl.BlockSpec((ch, nv), lambda i: (0, 0)),
-            pl.BlockSpec((nv, ch), lambda i: (0, 0)),
-            pl.BlockSpec((ch, hid), lambda i: (0, 0)),
-            pl.BlockSpec((step, hid), lambda i: (at(i), 0)),
-            pl.BlockSpec((hid, step), lambda i: (0, at(i))),
-            pl.BlockSpec((ch, step), lambda i: (0, at(i))),
-        ],
-        out_specs=(
-            pl.BlockSpec((step, hid), lambda i: (at(i), 0)),
-            pl.BlockSpec((ROWS_STEP, cells, ch), lambda i: (at(i), 0, 0)),
-            pl.BlockSpec((chunks, 24, 128), lambda i: (0, 0, 0)),
-        ),
-        scratch_shapes=[
+            pltpu.HBM((n, hid), bf16),
+            pltpu.HBM((nrow, cells, ch), f32),
+            pltpu.HBM((chunks, 24, 128), bf16),
+        ),
+        in_specs=[pl.BlockSpec(memory_space=pltpu.SMEM)] + [OUTSIDE] * 2 + [INSIDE] * 3 + [OUTSIDE] * 3,
+        out_specs=(OUTSIDE, OUTSIDE, INSIDE),
+        scratch_shapes=[pltpu.VMEM(x.shape, bf16) for x in (got, stk, slope, act_t, xhat_t, slope)]
+        + [
             pltpu.VMEM((nrow, cells, ch), f32),
             pltpu.VMEM((nrow, cells, ch), f32),
             pltpu.VMEM((nv, ch), f32),
             pltpu.VMEM((ch, hid), f32),
             pltpu.VMEM((hid, ch), f32),
+            dma((blocks // BLOCKS_STEP,)),
+            dma((blocks,)),
+            dma((3,)),
+            dma((nrow // PULL_ROWS + 1,)),
         ],
         compiler_params=params(),
         cost_estimate=cost(10 * n * ch * hid, 24 * 2**20),
         name="decode",
-    )(rows, got, stk, head, head_t, w_out_t, slope, act_t, xhat_t)
+    )(rows, *in_hbm(got, stk), head, head_t, w_out_t, *in_hbm(slope, act_t, xhat_t))
 
 
 def backward_kernel(lat_ref, left_ref, right_ref, gain_ref, w_in_t_ref, pre_grad_ref, both_ref, out_ref, first_ref, last_ref):
@@ -398,14 +422,17 @@
     both_axes = ("band", "lon")
     devices = lax.axis_size("band") * lax.axis_size("lon")
     cells = latent.shape[1]
-    got = lax.all_to_all(pack(weights, targets, slots, counts), "lon", 0, 0, tiled=True)
+    packed = pack(weights, targets, slots, counts)
     left, right = from_sides(latent[:, 0:1, :], latent[:, cells - 1 : cells, :])
+    packed, left, right = lax.optimization_barrier((packed, left, right))
+    got = lax.all_to_all(packed, "lon", 0, 0, tiled=True)
     left, right = left.astype(f32), right.astype(f32)
     gain_row = gain.reshape(1, -1)
     stk, slope, act_t, xhat_t = forward(latent, left, right, gain_row, w_in, w_out)
     pre_grad, both, sums = decode(row_index, got, stk, head, head.T, w_out.T, slope, act_t, xhat_t, devices)
     parts = lax.all_to_all(sums, both_axes, 0, 0, tiled=True)
     grad, first, last = backward(latent, left, right, gain_row, w_in.T, pre_grad, both)
+    parts, first, last = lax.optimization_barrier((parts, first, last))
     grad_left, grad_right = from_sides(first.astype(bf16), last.astype(bf16))
     grad = add_edges(grad, grad_left.astype(f32), grad_right.astype(f32))
     chunks = lax.all_to_all(total(parts), both_axes, 0, 0, tiled=True)

time: 128 us -> 171 us (1.34)
  Pallas kernels: 46 us -> 101 us
  blocking collectives: 26 us -> 0 us
  starting transfers between devices: 14.7 us -> 25.4 us
  waiting for transfers between devices: 30.7 us -> 40.7 us
  local copies, waits for them, and re-layouts: 7.5 us -> 1.57 us
    pallas_call x3, Pallas kernels: 32.8 us -> 88 us  [the longest x1 64.7 us: pack(): pl.pallas_call(pack_kernel, out_shape=pltpu.HBM((blocks, 2 * obs + META,...]
    all_to_all x1 -> x2, waiting for transfers between devices: 0.01 us -> 27.3 us  [the longest x1 19.8 us: body(): got = lax.all_to_all(packed, 'lon', 0, 0, tiled=True)]
    all_to_all x1 -> x0, blocking collectives: 26 us -> none  [body(): parts = lax.all_to_all(sums, both_axes, 0, 0, tiled=True)]
    ppermute x2, waiting for transfers between devices: 27.7 us -> 5.7 us  [from_sides(): lax.ppermute(last, 'lon', [(i, (i + 1) % count) for i in range(count)])]
    all_to_all x1 -> x2, starting transfers between devices: 7.18 us -> 16.9 us  [the longest x1 10.1 us: body(): parts = lax.all_to_all(sums, both_axes, 0, 0, tiled=True)]
    unnamed x27 -> x15, local copies, waits for them, and re-layouts: 7.31 us -> 0.41 us
    all_to_all x1, waiting for transfers between devices: 0.3 us -> 4.73 us  [body(): chunks = lax.all_to_all(total(parts), both_axes, 0, 0, tiled=True)]
  transfers between devices with their start and end apart: 6 -> 7, of which waited for: 4 -> 5; matrix products, arithmetic and copies ran while one was open for 1% -> 0% of each run, Pallas kernels for 15% -> 49%
where the time goes in v2:
time: 171 us; the launch traced here: 170 us
  Pallas kernels  101 us (59%)
  waiting for transfers between devices  40.7 us (24%)
  starting transfers between devices  25.4 us (15%)
    pallas_call x1, Pallas kernels, pack(): pl.pallas_call(pack_kernel, out_shape=pltpu.HBM((blocks, 2 * obs + META,...  64.7 us
    all_to_all x1, waiting for transfers between devices, body(): got = lax.all_to_all(packed, 'lon', 0, 0, tiled=True)  19.8 us
    pallas_call x1, Pallas kernels, decode(): pl.pallas_call(decode_kernel, out_shape=(pltpu.HBM((n, hid), bf16), pltpu...  15.1 us
    all_to_all x1, starting transfers between devices, body(): parts = lax.all_to_all(sums, both_axes, 0, 0, tiled=True)  10.1 us
    pallas_call x1, Pallas kernels, backward(): pl.pallas_call(backward_kernel, grid=(rows // ROWS_STEP,), out_shape=(jax...  9.26 us
    pallas_call x1, Pallas kernels, forward(): pl.pallas_call(forward_kernel, grid=(rows // ROWS_STEP,), out_shape=(pltp...  8.17 us
    all_to_all x1, waiting for transfers between devices, body(): parts = lax.all_to_all(sums, both_axes, 0, 0, tiled=True)  7.44 us
    all_to_all x1, starting transfers between devices, body(): got = lax.all_to_all(packed, 'lon', 0, 0, tiled=True)  6.83 us
  transfers between devices with their start and end apart: 7, of which 5 were waited for; matrix products, arithmetic and copies ran while one was open for 0% of the time, Pallas kernels for 49%

profile of v2, /device:TPU:1, one launch (start us, length us, event | category | flops | bytes accessed | tf_op | source)
XLA Modules:
  0.0 170.0 jit_solution(14678127964814926125)
XLA Ops:
  0.6 1.0 fusion
  1.7 2.7 %collective-permute-start = (bf16[32,1,256]{2,1,0:T(2,128)(2,1)S(1)}, bf16[32,1,256]{2,1,0:T(2,128)(2,1)S(1)}, u32[]{:S(2)}, u32[]{:S(2)}) collective-permute-start(bf16[32,1,256]{2,1,0:T(2,128)(2,1)S(1)} %get-tuple-element.46), channel_id=1, source_target_pairs={{0,1},{1,2},{2,3},{3,4},{4,5},{5,6},{6,7},{7,8},{8,9},{9,10},{10,1... | collective-permute-start | bytes 49160 | tf_op jit(solution)/shard_map/ppermute | solution.py:416
  4.3 0.0 copy-start.2
  4.3 0.0 copy-start.3
  4.3 0.0 copy-start
  4.3 0.0 copy-start.1
  4.3 0.0 copy-start.4
  4.4 0.1 collective-permute-start.1
  4.4 64.7 %pack.1 = bf16[32,264,128]{2,1,0:T(8,128)(2,1)} custom-call(bf16[32,128,128]{2,1,0:T(8,128)(2,1)} %w_hbm.1, bf16[32,128,128]{2,1,0:T(8,128)(2,1)} %t_hbm.1, s32[32,128]{1,0:T(8,128)} %slot_hbm.1, s32[32]{0:T(128)} %count_hbm.1), custom_call_target="tpu_custom_call" | custom-call | flops 1 | bytes 4194304 | tf_op jit(solution)/shard_map/pack/pallas_call | solution.py:74
  69.1 0.0 collective-permute-done
  69.1 0.0 collective-permute-done.1
  69.1 6.8 %all-to-all-start = ((bf16[32,264,128]{2,1,0:T(8,128)(2,1)}), bf16[32,264,128]{2,1,0:T(8,128)(2,1)}, u32[]{:S(2)}, u32[]{:S(2)}) async-start(bf16[32,264,128]{2,1,0:T(8,128)(2,1)} %pack.1), calls=%async_computation | async-start | bytes 4325376 | tf_op jit(solution)/shard_map/all_to_all | solution.py:428
  76.0 0.0 copy-done.2
  76.0 0.1 copy.20
  76.1 0.0 copy-done.3
  76.1 0.0 copy-start.5
  76.2 0.1 copy.19
  76.4 0.0 copy-done
  76.4 0.0 copy-done.1
  76.4 0.0 copy-done.4
  76.4 8.2 %forward.1 = (bf16[32,256,256]{2,1,0:T(8,128)(2,1)}, bf16[4096,512]{1,0:T(8,128)(2,1)}, bf16[512,4096]{1,0:T(8,128)(2,1)}, bf16[256,4096]{1,0:T(8,128)(2,1)}) custom-call(bf16[32,128,256]{2,1,0:T(8,128)(2,1)S(1)} %copy-done, f32[32,1,256]{2,1,0:T(1,128)S(1)} %convert_element_type.18.left_ref, f32[32,1,256]{2,1,0:T(1,128)S(1)} %convert_element_type.19.right_ref, ...), custom_call_target="tpu_custom_call" | custom-call | flops 2147483648 | bytes 16777216 | tf_op jit(solution)/shard_map/forward/pallas_call | solution.py:128
  84.6 19.8 %all-to-all-done.got_hbm = bf16[32,264,128]{2,1,0:T(8,128)(2,1)} async-done(((bf16[32,264,128]{2,1,0:T(8,128)(2,1)}), bf16[32,264,128]{2,1,0:T(8,128)(2,1)}, u32[]{:S(2)}, u32[]{:S(2)}) %all-to-all-start) | async-done | bytes 2162720 | tf_op jit(solution)/shard_map/all_to_all | solution.py:428
  104.4 0.0 copy-done.5
  104.4 15.1 %decode.1 = (bf16[4096,512]{1,0:T(8,128)(2,1)}, f32[32,128,256]{2,1,0:T(8,128)}, bf16[128,24,128]{2,1,0:T(8,128)(2,1)}) custom-call(s32[1,1,32]{2,1,0:T(1,128)S(1)} %copy-done.5, bf16[32,264,128]{2,1,0:T(8,128)(2,1)} %all-to-all-done.got_hbm, bf16[32,256,256]{2,1,0:T(8,128)(2,1)} %get-tuple-element.28.stk_hbm, bf16[256,128]{1,0:T(8,128)(2,1)S(1)} %copy-done.3, ...), custom_call_target="tpu_custom_call" | custom-call | flops 5368709120 | bytes 25165824 | tf_op jit(solution)/shard_map/decode/pallas_call | solution.py:279
  119.5 10.1 %all-to-all-start.1 = ((bf16[128,24,128]{2,1,0:T(8,128)(2,1)}), bf16[128,24,128]{2,1,0:T(8,128)(2,1)S(1)}, u32[]{:S(2)}, u32[]{:S(2)}) async-start(bf16[128,24,128]{2,1,0:T(8,128)(2,1)} %get-tuple-element.32), calls=%async_computation.1 | async-start | bytes 1572864 | tf_op jit(solution)/shard_map/all_to_all | solution.py:433
  129.6 0.1 copy.21
  129.7 9.3 %backward.1 = (f32[32,128,256]{2,1,0:T(8,128)}, f32[32,1,256]{2,1,0:T(1,128)S(1)}, f32[32,1,256]{2,1,0:T(1,128)S(1)}) custom-call(bf16[32,128,256]{2,1,0:T(8,128)(2,1)S(1)} %copy-done, f32[32,1,256]{2,1,0:T(1,128)S(1)} %convert_element_type.18.left_ref, f32[32,1,256]{2,1,0:T(1,128)S(1)} %convert_element_type.19.right_ref, f32[1,256]{1,0:T(1,128)S(1)} %bitcast.10, ...), custom_call_target="tpu_custom_call" | custom-call | flops 1073741824 | bytes 16777216 | tf_op jit(solution)/shard_map/backward/pallas_call | solution.py:323
  139.0 7.4 %all-to-all-done.1.got_ref = bf16[128,24,128]{2,1,0:T(8,128)(2,1)S(1)} async-done(((bf16[128,24,128]{2,1,0:T(8,128)(2,1)}), bf16[128,24,128]{2,1,0:T(8,128)(2,1)S(1)}, u32[]{:S(2)}, u32[]{:S(2)}) %all-to-all-start.1) | async-done | bytes 786464 | tf_op jit(solution)/shard_map/all_to_all | solution.py:433
  146.4 1.1 total.1
  147.5 4.0 %all-to-all-start.2 = ((bf16[128,24,128]{2,1,0:T(8,128)(2,1)}), bf16[128,24,128]{2,1,0:T(8,128)(2,1)S(1)}, u32[]{:S(2)}, u32[]{:S(2)}) async-start(bf16[128,24,128]{2,1,0:T(8,128)(2,1)} %total.1), calls=%async_computation.2 | async-start | bytes 1572864 | tf_op jit(solution)/shard_map/all_to_all | solution.py:438
  151.6 1.7 %collective-permute-start.2 = (bf16[32,1,256]{2,1,0:T(2,128)(2,1)S(1)}, bf16[32,1,256]{2,1,0:T(2,128)(2,1)S(1)}, u32[]{:S(2)}, u32[]{:S(2)}) collective-permute-start(bf16[32,1,256]{2,1,0:T(2,128)(2,1)S(1)} %convert_element_type.20), channel_id=1, source_target_pairs={{0,1},{1,2},{2,3},{3,4},{4,5},{5,6},{6,7},{7,8},{8,9},{9,10},{10,1... | collective-permute-start | bytes 49160 | tf_op jit(solution)/shard_map/ppermute | solution.py:416
  153.3 0.1 collective-permute-start.3
  153.4 0.1 copy.22.gain_ref
  153.5 5.7 %collective-permute-done.2 = bf16[32,1,256]{2,1,0:T(2,128)(2,1)S(1)} collective-permute-done((bf16[32,1,256]{2,1,0:T(2,128)(2,1)S(1)}, bf16[32,1,256]{2,1,0:T(2,128)(2,1)S(1)}, u32[]{:S(2)}, u32[]{:S(2)}) %collective-permute-start.2) | collective-permute-done | bytes 16416 | tf_op jit(solution)/shard_map/ppermute | solution.py:416
  159.3 3.0 %collective-permute-done.3 = bf16[32,1,256]{2,1,0:T(2,128)(2,1)S(1)} collective-permute-done((bf16[32,1,256]{2,1,0:T(2,128)(2,1)S(1)}, bf16[32,1,256]{2,1,0:T(2,128)(2,1)S(1)}, u32[]{:S(2)}, u32[]{:S(2)}) %collective-permute-start.3) | collective-permute-done | bytes 16416 | tf_op jit(solution)/shard_map/ppermute | solution.py:417
  162.3 1.8 %edges.1 = f32[32,128,256]{2,1,0:T(8,128)} custom-call(f32[32,1,256]{2,1,0:T(1,128)S(1)} %convert_element_type.21.left_ref, f32[32,1,256]{2,1,0:T(1,128)S(1)} %convert_element_type.23.right_ref, f32[32,128,256]{2,1,0:T(8,128)} %get-tuple-element.39.grad_ref), custom_call_target="tpu_custom_call", output_to_operand_aliasing={{}: (2, {})} | custom-call | flops 131072 | bytes 1048576 | tf_op jit(solution)/shard_map/edges/pallas_call | solution.py:360
  164.1 4.7 %all-to-all-done.2.got_ref = bf16[128,24,128]{2,1,0:T(8,128)(2,1)S(1)} async-done(((bf16[128,24,128]{2,1,0:T(8,128)(2,1)}), bf16[128,24,128]{2,1,0:T(8,128)(2,1)S(1)}, u32[]{:S(2)}, u32[]{:S(2)}) %all-to-all-start.2) | async-done | bytes 786464 | tf_op jit(solution)/shard_map/all_to_all | solution.py:438
  168.8 1.1 finish.1
  (6 shorter events, 0.2 us)
Async XLA Ops:
  1.7 67.5 %collective-permute-start = (bf16[32,1,256]{2,1,0:T(2,128)(2,1)S(1)}, bf16[32,1,256]{2,1,0:T(2,128)(2,1)S(1)}, u32[]{:S(2)}, u32[]{:S(2)}) collective-permute-start(bf16[32,1,256]{2,1,0:T(2,128)(2,1)S(1)} %get-tuple-element.46), channel_id=1, source_target_pairs={{0,1},{1,2},{2,3},{3,4},{4,5},{5,6},{6,7},{7,8},{8,9},{9,10},{10,1... | collective-permute-start | bytes 49160 | tf_op jit(solution)/shard_map/ppermute | solution.py:416
  4.3 71.7 %copy-start.2 = (bf16[512,256]{1,0:T(8,128)(2,1)S(1)}, bf16[512,256]{1,0:T(8,128)(2,1)}, u32[]{:S(2)}) copy-start(bf16[512,256]{1,0:T(8,128)(2,1)} %w_out_ref.1) | copy-start | bytes 786436
  4.3 71.8 %copy-start.3 = (bf16[256,128]{1,0:T(8,128)(2,1)S(1)}, bf16[256,128]{1,0:T(8,128)(2,1)}, u32[]{:S(2)}) copy-start(bf16[256,128]{1,0:T(8,128)(2,1)} %head_ref.1) | copy-start | bytes 196612
  4.3 72.0 %copy-start = (bf16[32,128,256]{2,1,0:T(8,128)(2,1)S(1)}, bf16[32,128,256]{2,1,0:T(8,128)(2,1)}, u32[]{:S(2)}) copy-start(bf16[32,128,256]{2,1,0:T(8,128)(2,1)} %lat_ref.3) | copy-start | bytes 6291460
  4.3 72.0 %copy-start.1 = (bf16[256,512]{1,0:T(8,128)(2,1)S(1)}, bf16[256,512]{1,0:T(8,128)(2,1)}, u32[]{:S(2)}) copy-start(bf16[256,512]{1,0:T(8,128)(2,1)} %w_in_ref.3) | copy-start | bytes 786436
  4.3 72.0 %copy-start.4 = (f32[256]{0:T(256)S(1)}, f32[256]{0:T(256)}, u32[]{:S(2)}) copy-start(f32[256]{0:T(256)} %param.16) | copy-start | bytes 3076
  4.4 64.8 %collective-permute-start.1 = (bf16[32,1,256]{2,1,0:T(2,128)(2,1)S(1)}, bf16[32,1,256]{2,1,0:T(2,128)(2,1)S(1)}, u32[]{:S(2)}, u32[]{:S(2)}) collective-permute-start(bf16[32,1,256]{2,1,0:T(2,128)(2,1)S(1)} %get-tuple-element.45), channel_id=1, source_target_pairs={{1,0},{2,1},{3,2},{4,3},{5,4},{6,5},{7,6},{8,7},{9,8},{10,9},{11,1... | collective-permute-start | bytes 49160 | tf_op jit(solution)/shard_map/ppermute | solution.py:417
  69.1 35.2 %all-to-all-start = ((bf16[32,264,128]{2,1,0:T(8,128)(2,1)}), bf16[32,264,128]{2,1,0:T(8,128)(2,1)}, u32[]{:S(2)}, u32[]{:S(2)}) async-start(bf16[32,264,128]{2,1,0:T(8,128)(2,1)} %pack.1), calls=%async_computation | async-start | bytes 4325376 | tf_op jit(solution)/shard_map/all_to_all | solution.py:428
  76.1 28.2 %copy-start.5 = (s32[1,1,32]{2,1,0:T(1,128)S(1)}, s32[1,1,32]{2,1,0:T(1,128)}, u32[]{:S(2)}) copy-start(s32[1,1,32]{2,1,0:T(1,128)} %rows_ref.1) | copy-start | bytes 388
  119.5 26.9 %all-to-all-start.1 = ((bf16[128,24,128]{2,1,0:T(8,128)(2,1)}), bf16[128,24,128]{2,1,0:T(8,128)(2,1)S(1)}, u32[]{:S(2)}, u32[]{:S(2)}) async-start(bf16[128,24,128]{2,1,0:T(8,128)(2,1)} %get-tuple-element.32), calls=%async_computation.1 | async-start | bytes 1572864 | tf_op jit(solution)/shard_map/all_to_all | solution.py:433
  147.5 21.3 %all-to-all-start.2 = ((bf16[128,24,128]{2,1,0:T(8,128)(2,1)}), bf16[128,24,128]{2,1,0:T(8,128)(2,1)S(1)}, u32[]{:S(2)}, u32[]{:S(2)}) async-start(bf16[128,24,128]{2,1,0:T(8,128)(2,1)} %total.1), calls=%async_computation.2 | async-start | bytes 1572864 | tf_op jit(solution)/shard_map/all_to_all | solution.py:438
  151.6 7.7 %collective-permute-start.2 = (bf16[32,1,256]{2,1,0:T(2,128)(2,1)S(1)}, bf16[32,1,256]{2,1,0:T(2,128)(2,1)S(1)}, u32[]{:S(2)}, u32[]{:S(2)}) collective-permute-start(bf16[32,1,256]{2,1,0:T(2,128)(2,1)S(1)} %convert_element_type.20), channel_id=1, source_target_pairs={{0,1},{1,2},{2,3},{3,4},{4,5},{5,6},{6,7},{7,8},{8,9},{9,10},{10,1... | collective-permute-start | bytes 49160 | tf_op jit(solution)/shard_map/ppermute | solution.py:416
  153.3 9.0 %collective-permute-start.3 = (bf16[32,1,256]{2,1,0:T(2,128)(2,1)S(1)}, bf16[32,1,256]{2,1,0:T(2,128)(2,1)S(1)}, u32[]{:S(2)}, u32[]{:S(2)}) collective-permute-start(bf16[32,1,256]{2,1,0:T(2,128)(2,1)S(1)} %convert_element_type.22), channel_id=1, source_target_pairs={{1,0},{2,1},{3,2},{4,3},{5,4},{6,5},{7,6},{8,7},{9,8},{10,9},{11,1... | collective-permute-start | bytes 49160 | tf_op jit(solution)/shard_map/ppermute | solution.py:417

commit v3 on v2

--- a/solution.py
+++ b/solution.py
@@ -13,6 +13,7 @@
 ROWS_STEP = 4
 BLOCKS_STEP = 8
 PULL_ROWS = 16
+PACK_CHUNKS = 4
 META = 8
 
 f32 = jnp.float32
@@ -41,19 +42,29 @@
     return pl.CostEstimate(flops=flops, bytes_accessed=nbytes, transcendentals=trans)
 
 
-def pack_kernel(w_hbm, t_hbm, slot_hbm, count_hbm, out_hbm, slots, counts, meta, sems):
+def pack_kernel(w_hbm, t_hbm, slot_hbm, count_hbm, out_hbm, buf, slots, counts, small_sems, in_sems, out_sems):
     blocks, obs = slots.shape
     nv = t_hbm.shape[1]
+    n = blocks // PACK_CHUNKS
     small = [
-        pltpu.make_async_copy(slot_hbm, slots, sems.at[0]),
-        pltpu.make_async_copy(count_hbm, counts, sems.at[1]),
+        pltpu.make_async_copy(slot_hbm, slots, small_sems.at[0]),
+        pltpu.make_async_copy(count_hbm, counts, small_sems.at[1]),
     ]
-    large = [
-        pltpu.make_async_copy(w_hbm, out_hbm.at[:, pl.ds(0, obs), :], sems.at[2]),
-        pltpu.make_async_copy(t_hbm, out_hbm.at[:, pl.ds(obs, nv), :], sems.at[3]),
-    ]
-    for c in small + large:
+    arrive, leave = [], []
+    for c in range(PACK_CHUNKS):
+        here = pl.ds(c * n, n)
+        arrive.append(
+            (
+                pltpu.make_async_copy(w_hbm.at[here], buf.at[here, pl.ds(0, obs), :], in_sems.at[2 * c]),
+                pltpu.make_async_copy(t_hbm.at[here], buf.at[here, pl.ds(obs, nv), :], in_sems.at[2 * c + 1]),
+            )
+        )
+        leave.append(pltpu.make_async_copy(buf.at[here], out_hbm.at[here], out_sems.at[c]))
+    for c in small:
         c.start()
+    for pair in arrive:
+        for c in pair:
+            c.start()
     for c in small:
         c.wait()
     coef = slots[...].astype(f32) / (WINDOW_SLOTS - 1)
@@ -61,26 +72,31 @@
     row = lax.broadcasted_iota(jnp.int32, (META, obs), 0)
     for b in range(blocks):
         live = jnp.where(lane < counts[b], 1.0, 0.0)
-        meta[b] = jnp.where(row == 0, coef[b : b + 1, :], live).astype(bf16)
-    last = pltpu.make_async_copy(meta, out_hbm.at[:, pl.ds(obs + nv, META), :], sems.at[4])
-    last.start()
-    for c in large:
+        buf[b, obs + nv : obs + nv + META, :] = jnp.where(row == 0, coef[b : b + 1, :], live).astype(bf16)
+    for pair, out in zip(arrive, leave):
+        for c in pair:
+            c.wait()
+        out.start()
+    for c in leave:
         c.wait()
-    last.wait()
 
 
 def pack(weights, targets, slots, counts):
     blocks, obs, cells = weights.shape
+    shape = (blocks, 2 * obs + META, cells)
+    dma = pltpu.SemaphoreType.DMA
     return pl.pallas_call(
         pack_kernel,
-        out_shape=pltpu.HBM((blocks, 2 * obs + META, cells), bf16),
+        out_shape=pltpu.HBM(shape, bf16),
         in_specs=[OUTSIDE] * 4,
         out_specs=OUTSIDE,
         scratch_shapes=[
+            pltpu.VMEM(shape, bf16),
             pltpu.VMEM(slots.shape, jnp.int32),
             pltpu.SMEM(counts.shape, jnp.int32),
-            pltpu.VMEM((blocks, META, obs), bf16),
-            pltpu.SemaphoreType.DMA((5,)),
+            dma((2,)),
+            dma((2 * PACK_CHUNKS,)),
+            dma((PACK_CHUNKS,)),
         ],
         compiler_params=params(),
         cost_estimate=cost(1, 4 * 2**20),

time: 171 us -> 109 us (0.64)
  Pallas kernels: 101 us -> 39.5 us
    pallas_call x1, Pallas kernels: 64.7 us -> 2.92 us  [pack(): pl.pallas_call(pack_kernel, out_shape=pltpu.HBM(shape, bf16), in_specs=[O...]
  transfers between devices with their start and end apart: 7 -> 7, of which waited for: 5 -> 6; matrix products, arithmetic and copies ran while one was open for 0% -> 1% of each run, Pallas kernels for 49% -> 20%
where the time goes in v3:
time: 109 us; the launch traced here: 108 us
  waiting for transfers between devices  41.5 us (38%)
  Pallas kernels  39.5 us (36%)
  starting transfers between devices  24.5 us (22%)
  local copies, waits for them, and re-layouts  1.57 us (1%)
    all_to_all x1, waiting for transfers between devices, body(): got = lax.all_to_all(packed, 'lon', 0, 0, tiled=True)  20 us
    pallas_call x1, Pallas kernels, decode(): pl.pallas_call(decode_kernel, out_shape=(pltpu.HBM((n, hid), bf16), pltpu...  15.1 us
    all_to_all x1, starting transfers between devices, body(): parts = lax.all_to_all(sums, both_axes, 0, 0, tiled=True)  9.63 us
    pallas_call x1, Pallas kernels, backward(): pl.pallas_call(backward_kernel, grid=(rows // ROWS_STEP,), out_shape=(jax...  9.26 us
    pallas_call x1, Pallas kernels, forward(): pl.pallas_call(forward_kernel, grid=(rows // ROWS_STEP,), out_shape=(pltp...  8.17 us
    all_to_all x1, waiting for transfers between devices, body(): parts = lax.all_to_all(sums, both_axes, 0, 0, tiled=True)  7.43 us
    all_to_all x1, starting transfers between devices, body(): got = lax.all_to_all(packed, 'lon', 0, 0, tiled=True)  6.32 us
    ppermute x2, waiting for transfers between devices, from_sides(): lax.ppermute(last, 'lon', [(i, (i + 1) % count) for i in range(count)])  5.7 us
  transfers between devices with their start and end apart: 7, of which 6 were waited for; matrix products, arithmetic and copies ran while one was open for 1% of the time, Pallas kernels for 20%

profile of v3, /device:TPU:1, one launch (start us, length us, event | category | flops | bytes accessed | tf_op | source)
XLA Modules:
  0.0 108.1 jit_solution(7567087958649211323)
XLA Ops:
  0.6 1.0 fusion
  1.7 2.7 %collective-permute-start = (bf16[32,1,256]{2,1,0:T(2,128)(2,1)S(1)}, bf16[32,1,256]{2,1,0:T(2,128)(2,1)S(1)}, u32[]{:S(2)}, u32[]{:S(2)}) collective-permute-start(bf16[32,1,256]{2,1,0:T(2,128)(2,1)S(1)} %get-tuple-element.46), channel_id=1, source_target_pairs={{0,1},{1,2},{2,3},{3,4},{4,5},{5,6},{6,7},{7,8},{8,9},{9,10},{10,1... | collective-permute-start | bytes 49160 | tf_op jit(solution)/shard_map/ppermute | solution.py:432
  4.3 0.0 copy-start.2
  4.3 0.0 copy-start.3
  4.3 0.0 copy-start
  4.3 0.0 copy-start.1
  4.3 0.0 copy-start.4
  4.4 0.1 collective-permute-start.1
  4.4 2.9 %pack.1 = bf16[32,264,128]{2,1,0:T(8,128)(2,1)} custom-call(bf16[32,128,128]{2,1,0:T(8,128)(2,1)} %w_hbm.1, bf16[32,128,128]{2,1,0:T(8,128)(2,1)} %t_hbm.1, s32[32,128]{1,0:T(8,128)} %slot_hbm.1, s32[32]{0:T(128)} %count_hbm.1), custom_call_target="tpu_custom_call" | custom-call | flops 1 | bytes 4194304 | tf_op jit(solution)/shard_map/pack/pallas_call | solution.py:88
  7.4 0.0 collective-permute-done
  7.4 0.7 collective-permute-done.1
  8.1 6.3 %all-to-all-start = ((bf16[32,264,128]{2,1,0:T(8,128)(2,1)}), bf16[32,264,128]{2,1,0:T(8,128)(2,1)}, u32[]{:S(2)}, u32[]{:S(2)}) async-start(bf16[32,264,128]{2,1,0:T(8,128)(2,1)} %pack.1), calls=%async_computation | async-start | bytes 4325376 | tf_op jit(solution)/shard_map/all_to_all | solution.py:444
  14.4 0.0 copy-done.2
  14.4 0.1 copy.20
  14.5 0.0 copy-done.3
  14.5 0.0 copy-start.5
  14.6 0.1 copy.19
  14.8 0.0 copy-done
  14.8 0.0 copy-done.1
  14.8 0.0 copy-done.4
  14.8 8.2 %forward.1 = (bf16[32,256,256]{2,1,0:T(8,128)(2,1)}, bf16[4096,512]{1,0:T(8,128)(2,1)}, bf16[512,4096]{1,0:T(8,128)(2,1)}, bf16[256,4096]{1,0:T(8,128)(2,1)}) custom-call(bf16[32,128,256]{2,1,0:T(8,128)(2,1)S(1)} %copy-done, f32[32,1,256]{2,1,0:T(1,128)S(1)} %convert_element_type.18.left_ref, f32[32,1,256]{2,1,0:T(1,128)S(1)} %convert_element_type.19.right_ref, ...), custom_call_target="tpu_custom_call" | custom-call | flops 2147483648 | bytes 16777216 | tf_op jit(solution)/shard_map/forward/pallas_call | solution.py:144
  23.0 20.0 %all-to-all-done.got_hbm = bf16[32,264,128]{2,1,0:T(8,128)(2,1)} async-done(((bf16[32,264,128]{2,1,0:T(8,128)(2,1)}), bf16[32,264,128]{2,1,0:T(8,128)(2,1)}, u32[]{:S(2)}, u32[]{:S(2)}) %all-to-all-start) | async-done | bytes 2162720 | tf_op jit(solution)/shard_map/all_to_all | solution.py:444
  42.9 0.0 copy-done.5
  42.9 15.1 %decode.1 = (bf16[4096,512]{1,0:T(8,128)(2,1)}, f32[32,128,256]{2,1,0:T(8,128)}, bf16[128,24,128]{2,1,0:T(8,128)(2,1)}) custom-call(s32[1,1,32]{2,1,0:T(1,128)S(1)} %copy-done.5, bf16[32,264,128]{2,1,0:T(8,128)(2,1)} %all-to-all-done.got_hbm, bf16[32,256,256]{2,1,0:T(8,128)(2,1)} %get-tuple-element.28.stk_hbm, bf16[256,128]{1,0:T(8,128)(2,1)S(1)} %copy-done.3, ...), custom_call_target="tpu_custom_call" | custom-call | flops 5368709120 | bytes 25165824 | tf_op jit(solution)/shard_map/decode/pallas_call | solution.py:295
  58.1 9.6 %all-to-all-start.1 = ((bf16[128,24,128]{2,1,0:T(8,128)(2,1)}), bf16[128,24,128]{2,1,0:T(8,128)(2,1)S(1)}, u32[]{:S(2)}, u32[]{:S(2)}) async-start(bf16[128,24,128]{2,1,0:T(8,128)(2,1)} %get-tuple-element.32), calls=%async_computation.1 | async-start | bytes 1572864 | tf_op jit(solution)/shard_map/all_to_all | solution.py:449
  67.7 0.1 copy.21
  67.8 9.3 %backward.1 = (f32[32,128,256]{2,1,0:T(8,128)}, f32[32,1,256]{2,1,0:T(1,128)S(1)}, f32[32,1,256]{2,1,0:T(1,128)S(1)}) custom-call(bf16[32,128,256]{2,1,0:T(8,128)(2,1)S(1)} %copy-done, f32[32,1,256]{2,1,0:T(1,128)S(1)} %convert_element_type.18.left_ref, f32[32,1,256]{2,1,0:T(1,128)S(1)} %convert_element_type.19.right_ref, f32[1,256]{1,0:T(1,128)S(1)} %bitcast.10, ...), custom_call_target="tpu_custom_call" | custom-call | flops 1073741824 | bytes 16777216 | tf_op jit(solution)/shard_map/backward/pallas_call | solution.py:339
  77.1 7.4 %all-to-all-done.1.got_ref = bf16[128,24,128]{2,1,0:T(8,128)(2,1)S(1)} async-done(((bf16[128,24,128]{2,1,0:T(8,128)(2,1)}), bf16[128,24,128]{2,1,0:T(8,128)(2,1)S(1)}, u32[]{:S(2)}, u32[]{:S(2)}) %all-to-all-start.1) | async-done | bytes 786464 | tf_op jit(solution)/shard_map/all_to_all | solution.py:449
  84.5 1.1 total.1
  85.6 4.0 %all-to-all-start.2 = ((bf16[128,24,128]{2,1,0:T(8,128)(2,1)}), bf16[128,24,128]{2,1,0:T(8,128)(2,1)S(1)}, u32[]{:S(2)}, u32[]{:S(2)}) async-start(bf16[128,24,128]{2,1,0:T(8,128)(2,1)} %total.1), calls=%async_computation.2 | async-start | bytes 1572864 | tf_op jit(solution)/shard_map/all_to_all | solution.py:454
  89.7 1.7 %collective-permute-start.2 = (bf16[32,1,256]{2,1,0:T(2,128)(2,1)S(1)}, bf16[32,1,256]{2,1,0:T(2,128)(2,1)S(1)}, u32[]{:S(2)}, u32[]{:S(2)}) collective-permute-start(bf16[32,1,256]{2,1,0:T(2,128)(2,1)S(1)} %convert_element_type.20), channel_id=1, source_target_pairs={{0,1},{1,2},{2,3},{3,4},{4,5},{5,6},{6,7},{7,8},{8,9},{9,10},{10,1... | collective-permute-start | bytes 49160 | tf_op jit(solution)/shard_map/ppermute | solution.py:432
  91.4 0.1 collective-permute-start.3
  91.5 0.1 copy.22.gain_ref
  91.6 5.7 %collective-permute-done.2 = bf16[32,1,256]{2,1,0:T(2,128)(2,1)S(1)} collective-permute-done((bf16[32,1,256]{2,1,0:T(2,128)(2,1)S(1)}, bf16[32,1,256]{2,1,0:T(2,128)(2,1)S(1)}, u32[]{:S(2)}, u32[]{:S(2)}) %collective-permute-start.2) | collective-permute-done | bytes 16416 | tf_op jit(solution)/shard_map/ppermute | solution.py:432
  97.3 3.0 %collective-permute-done.3 = bf16[32,1,256]{2,1,0:T(2,128)(2,1)S(1)} collective-permute-done((bf16[32,1,256]{2,1,0:T(2,128)(2,1)S(1)}, bf16[32,1,256]{2,1,0:T(2,128)(2,1)S(1)}, u32[]{:S(2)}, u32[]{:S(2)}) %collective-permute-start.3) | collective-permute-done | bytes 16416 | tf_op jit(solution)/shard_map/ppermute | solution.py:433
  100.4 1.8 %edges.1 = f32[32,128,256]{2,1,0:T(8,128)} custom-call(f32[32,1,256]{2,1,0:T(1,128)S(1)} %convert_element_type.21.left_ref, f32[32,1,256]{2,1,0:T(1,128)S(1)} %convert_element_type.23.right_ref, f32[32,128,256]{2,1,0:T(8,128)} %get-tuple-element.39.grad_ref), custom_call_target="tpu_custom_call", output_to_operand_aliasing={{}: (2, {})} | custom-call | flops 131072 | bytes 1048576 | tf_op jit(solution)/shard_map/edges/pallas_call | solution.py:376
  102.2 4.7 %all-to-all-done.2.got_ref = bf16[128,24,128]{2,1,0:T(8,128)(2,1)S(1)} async-done(((bf16[128,24,128]{2,1,0:T(8,128)(2,1)}), bf16[128,24,128]{2,1,0:T(8,128)(2,1)S(1)}, u32[]{:S(2)}, u32[]{:S(2)}) %all-to-all-start.2) | async-done | bytes 786464 | tf_op jit(solution)/shard_map/all_to_all | solution.py:454
  106.9 1.1 %finish.1 = (f32[256,512]{1,0:T(8,128)}, f32[512,256]{1,0:T(8,128)}, f32[1,256]{1,0:T(1,128)}, f32[256,128]{1,0:T(8,128)}) custom-call(bf16[128,24,128]{2,1,0:T(8,128)(2,1)S(1)} %all-to-all-done.2.got_ref, f32[256,1]{1,0:T(8,128)S(1)} %copy.22.gain_ref, bf16[256,512]{1,0:T(8,128)(2,1)S(1)} %copy-done.1), custom_call_target="tpu_custom_call" | custom-call | flops 524288 | bytes 3145728 | tf_op jit(solution)/shard_map/finish/pallas_call | solution.py:416
  (6 shorter events, 0.2 us)
Async XLA Ops:
  1.7 5.7 %collective-permute-start = (bf16[32,1,256]{2,1,0:T(2,128)(2,1)S(1)}, bf16[32,1,256]{2,1,0:T(2,128)(2,1)S(1)}, u32[]{:S(2)}, u32[]{:S(2)}) collective-permute-start(bf16[32,1,256]{2,1,0:T(2,128)(2,1)S(1)} %get-tuple-element.46), channel_id=1, source_target_pairs={{0,1},{1,2},{2,3},{3,4},{4,5},{5,6},{6,7},{7,8},{8,9},{9,10},{10,1... | collective-permute-start | bytes 49160 | tf_op jit(solution)/shard_map/ppermute | solution.py:432
  4.3 10.0 %copy-start.2 = (bf16[512,256]{1,0:T(8,128)(2,1)S(1)}, bf16[512,256]{1,0:T(8,128)(2,1)}, u32[]{:S(2)}) copy-start(bf16[512,256]{1,0:T(8,128)(2,1)} %w_out_ref.1) | copy-start | bytes 786436
  4.3 10.2 %copy-start.3 = (bf16[256,128]{1,0:T(8,128)(2,1)S(1)}, bf16[256,128]{1,0:T(8,128)(2,1)}, u32[]{:S(2)}) copy-start(bf16[256,128]{1,0:T(8,128)(2,1)} %head_ref.1) | copy-start | bytes 196612
  4.3 10.4 %copy-start = (bf16[32,128,256]{2,1,0:T(8,128)(2,1)S(1)}, bf16[32,128,256]{2,1,0:T(8,128)(2,1)}, u32[]{:S(2)}) copy-start(bf16[32,128,256]{2,1,0:T(8,128)(2,1)} %lat_ref.3) | copy-start | bytes 6291460
  4.3 10.4 %copy-start.1 = (bf16[256,512]{1,0:T(8,128)(2,1)S(1)}, bf16[256,512]{1,0:T(8,128)(2,1)}, u32[]{:S(2)}) copy-start(bf16[256,512]{1,0:T(8,128)(2,1)} %w_in_ref.3) | copy-start | bytes 786436
  4.3 10.4 %copy-start.4 = (f32[256]{0:T(256)S(1)}, f32[256]{0:T(256)}, u32[]{:S(2)}) copy-start(f32[256]{0:T(256)} %param.16) | copy-start | bytes 3076
  4.4 3.7 %collective-permute-start.1 = (bf16[32,1,256]{2,1,0:T(2,128)(2,1)S(1)}, bf16[32,1,256]{2,1,0:T(2,128)(2,1)S(1)}, u32[]{:S(2)}, u32[]{:S(2)}) collective-permute-start(bf16[32,1,256]{2,1,0:T(2,128)(2,1)S(1)} %get-tuple-element.45), channel_id=1, source_target_pairs={{1,0},{2,1},{3,2},{4,3},{5,4},{6,5},{7,6},{8,7},{9,8},{10,9},{11,1... | collective-permute-start | bytes 49160 | tf_op jit(solution)/shard_map/ppermute | solution.py:433
  8.1 34.8 %all-to-all-start = ((bf16[32,264,128]{2,1,0:T(8,128)(2,1)}), bf16[32,264,128]{2,1,0:T(8,128)(2,1)}, u32[]{:S(2)}, u32[]{:S(2)}) async-start(bf16[32,264,128]{2,1,0:T(8,128)(2,1)} %pack.1), calls=%async_computation | async-start | bytes 4325376 | tf_op jit(solution)/shard_map/all_to_all | solution.py:444
  14.5 28.4 %copy-start.5 = (s32[1,1,32]{2,1,0:T(1,128)S(1)}, s32[1,1,32]{2,1,0:T(1,128)}, u32[]{:S(2)}) copy-start(s32[1,1,32]{2,1,0:T(1,128)} %rows_ref.1) | copy-start | bytes 388
  58.1 26.5 %all-to-all-start.1 = ((bf16[128,24,128]{2,1,0:T(8,128)(2,1)}), bf16[128,24,128]{2,1,0:T(8,128)(2,1)S(1)}, u32[]{:S(2)}, u32[]{:S(2)}) async-start(bf16[128,24,128]{2,1,0:T(8,128)(2,1)} %get-tuple-element.32), calls=%async_computation.1 | async-start | bytes 1572864 | tf_op jit(solution)/shard_map/all_to_all | solution.py:449
  85.6 21.3 %all-to-all-start.2 = ((bf16[128,24,128]{2,1,0:T(8,128)(2,1)}), bf16[128,24,128]{2,1,0:T(8,128)(2,1)S(1)}, u32[]{:S(2)}, u32[]{:S(2)}) async-start(bf16[128,24,128]{2,1,0:T(8,128)(2,1)} %total.1), calls=%async_computation.2 | async-start | bytes 1572864 | tf_op jit(solution)/shard_map/all_to_all | solution.py:454
  89.7 7.7 %collective-permute-start.2 = (bf16[32,1,256]{2,1,0:T(2,128)(2,1)S(1)}, bf16[32,1,256]{2,1,0:T(2,128)(2,1)S(1)}, u32[]{:S(2)}, u32[]{:S(2)}) collective-permute-start(bf16[32,1,256]{2,1,0:T(2,128)(2,1)S(1)} %convert_element_type.20), channel_id=1, source_target_pairs={{0,1},{1,2},{2,3},{3,4},{4,5},{5,6},{6,7},{7,8},{8,9},{9,10},{10,1... | collective-permute-start | bytes 49160 | tf_op jit(solution)/shard_map/ppermute | solution.py:432
  91.4 9.0 %collective-permute-start.3 = (bf16[32,1,256]{2,1,0:T(2,128)(2,1)S(1)}, bf16[32,1,256]{2,1,0:T(2,128)(2,1)S(1)}, u32[]{:S(2)}, u32[]{:S(2)}) collective-permute-start(bf16[32,1,256]{2,1,0:T(2,128)(2,1)S(1)} %convert_element_type.22), channel_id=1, source_target_pairs={{1,0},{2,1},{3,2},{4,3},{5,4},{6,5},{7,6},{8,7},{9,8},{10,9},{11,1... | collective-permute-start | bytes 49160 | tf_op jit(solution)/shard_map/ppermute | solution.py:433

commit v4 on v3

--- a/solution.py
+++ b/solution.py
@@ -171,9 +171,9 @@
 
 
 def decode_kernel(
-    rows_ref, got_hbm, stk_hbm, head_ref, head_t_ref, w_out_t_ref, slope_hbm, act_t_hbm, xhat_t_hbm,
-    pre_grad_hbm, both_hbm, sums_ref,
-    got, stk, slope, act_t, xhat_t, pre_grad_all, acc_both, acc_new, acc_head, acc_in, acc_out,
+    core_ref, rows_ref, got_hbm, stk_hbm, head_ref, head_t_ref, w_out_t_ref, slope_hbm, act_t_hbm, xhat_t_hbm,
+    adv_hbm, both_hbm, keep_ref, send_ref,
+    got, stk, slope, act_t, xhat_t, adv_all, acc_both, acc_new, acc_head, acc_in, acc_out,
     got_sems, stk_sems, in_sems, out_sems,
 ):
     nb, nr = BLOCKS_STEP, PULL_ROWS
@@ -191,20 +191,18 @@
     def stk_copy(b):
         return pltpu.make_async_copy(stk_hbm.at[rows_ref[0, 0, b]], stk.at[b], stk_sems.at[b])
 
-    def pre_grad_copy(k):
+    def adv_copy(k):
         flat = pl.ds(pl.multiple_of(k * step, step), step)
-        return pltpu.make_async_copy(pre_grad_all.at[flat], pre_grad_hbm.at[flat], out_sems.at[k])
-
+        return pltpu.make_async_copy(adv_all.at[flat], adv_hbm.at[flat], out_sems.at[k])
+
+    later = [
+        pltpu.make_async_copy(src, dst, in_sems.at[i])
+        for i, (src, dst) in enumerate(((slope_hbm, slope), (xhat_t_hbm, xhat_t), (act_t_hbm, act_t)))
+    ]
     for i in range(blocks // nb):
         got_copy(i).start()
         for j in range(nb):
             stk_copy(i * nb + j).start()
-    later = [
-        pltpu.make_async_copy(src, dst, in_sems.at[i])
-        for i, (src, dst) in enumerate(((slope_hbm, slope), (xhat_t_hbm, xhat_t), (act_t_hbm, act_t)))
-    ]
-    for c in later:
-        c.start()
     for acc in (acc_both, acc_new, acc_head, acc_in, acc_out):
         acc[...] = jnp.zeros_like(acc)
 
@@ -213,14 +211,20 @@
         got_copy(i).wait()
         for j in range(nb):
             stk_copy(first + j).wait()
+
+        @pl.when(i == 0)
+        def _():
+            for c in later:
+                c.start()
+
         places = [rows_ref[0, 0, first + j] for j in range(nb)]
+        meta = jnp.concatenate([got[first + j, 2 * obs : 2 * obs + META, :].astype(f32) for j in range(nb)], axis=0).T
         latents, coefs, lives = [], [], []
         for j in range(nb):
-            meta = got[first + j, 2 * obs : 2 * obs + META, :].astype(f32).T
-            t, live = meta[:, 0:1], meta[:, 1:2]
-            w = got[first + j, 0:obs, :].astype(f32)
-            pair = jnp.concatenate([(w * (1.0 - t)).astype(bf16), (w * t).astype(bf16)], axis=1)
-            latents.append(dot(pair, stk[first + j]).astype(bf16))
+            t, live = meta[:, META * j : META * j + 1], meta[:, META * j + 1 : META * j + 2]
+            w = got[first + j, 0:obs, :]
+            w_new = w * jnp.broadcast_to(t, w.shape).astype(bf16)
+            latents.append(dot(jnp.concatenate([w - w_new, w_new], axis=1), stk[first + j]).astype(bf16))
             coefs.append(t)
             lives.append(live)
         obs_latent = jnp.concatenate(latents, axis=0)
@@ -248,43 +252,53 @@
     def pull(k, carry):
         flat = pl.ds(pl.multiple_of(k * step, step), step)
         adv = acc_new[pl.ds(k * nr, nr)].reshape(step, ch).astype(bf16)
+        adv_all[flat, :] = adv
+        adv_copy(k).start()
         pre_grad = (dot(adv, w_out_t_ref[...]) * slope[flat, :].astype(f32)).astype(bf16)
-        pre_grad_all[flat, :] = pre_grad
-        pre_grad_copy(k).start()
         acc_in[...] += dot(xhat_t[:, flat], pre_grad)
         acc_out[...] += dot(act_t[:, flat], adv)
         return carry
 
     lax.fori_loop(0, rows // nr, pull, 0)
-    put_chunks(sums_ref, 0, acc_in)
-    put_chunks(sums_ref, 1, acc_out)
-    put_chunks(sums_ref, 2, acc_head)
-    left = acc_head.shape[0] * acc_head.shape[1] // (8 * 128)
-    sums_ref[left:, 16:24, :] = jnp.zeros((sums_ref.shape[0] - left, 8, 128), bf16)
+    for core in range(2):
+
+        @pl.when(core_ref[0] == core)
+        def _(core=core):
+            put_chunks(keep_ref, core, acc_in, acc_out, acc_head)
+            put_chunks(send_ref, 1 - core, acc_in, acc_out, acc_head)
+
     both_copy.wait()
     for k in range(rows // nr):
-        pre_grad_copy(k).wait()
-
-
-def put_chunks(sums_ref, part, acc):
-    down = acc.shape[0] // 8
-    for j in range(acc.shape[1] // 128):
-        tiles = acc[:, 128 * j : 128 * (j + 1)].reshape(down, 8, 128)
-        sums_ref[down * j : down * (j + 1), 8 * part : 8 * part + 8, :] = tiles.astype(bf16)
-
-
-def take_chunks(got_ref, part, shape):
+        adv_copy(k).wait()
+
+
+def put_chunks(ref, half, *accs):
+    for p, acc in enumerate(accs):
+        down = acc.shape[0] // 8
+        across = acc.shape[1] // 256
+        for j in range(across):
+            at = 128 * (half * across + j)
+            tiles = acc[:, at : at + 128].reshape(down, 8, 128)
+            ref[down * j : down * (j + 1), 8 * p : 8 * p + 8, :] = tiles.astype(ref.dtype)
+        if down * across < ref.shape[0]:
+            rest = ref.shape[0] - down * across
+            ref[down * across :, 8 * p : 8 * p + 8, :] = jnp.zeros((rest, 8, 128), ref.dtype)
+
+
+def take_chunks(halves, part, shape):
     down = shape[0] // 8
+    across = shape[1] // 256
     return jnp.concatenate(
         [
-            got_ref[down * j : down * (j + 1), 8 * part : 8 * part + 8, :].astype(f32).reshape(shape[0], 128)
-            for j in range(shape[1] // 128)
+            half[down * j : down * (j + 1), 8 * part : 8 * part + 8, :].reshape(shape[0], 128)
+            for half in halves
+            for j in range(across)
         ],
         axis=1,
     )
 
 
-def decode(rows, got, stk, head, head_t, w_out_t, slope, act_t, xhat_t, chunks):
+def decode(core, rows, got, stk, head, head_t, w_out_t, slope, act_t, xhat_t, chunks):
     nrow, two_cells, ch = stk.shape
     cells = two_cells // 2
     nv = head.shape[1]
@@ -292,17 +306,20 @@
     n = nrow * cells
     blocks = got.shape[0]
     dma = pltpu.SemaphoreType.DMA
+    scalars = pl.BlockSpec(memory_space=pltpu.SMEM)
     return pl.pallas_call(
         decode_kernel,
         out_shape=(
-            pltpu.HBM((n, hid), bf16),
+            pltpu.HBM((n, ch), bf16),
             pltpu.HBM((nrow, cells, ch), f32),
-            pltpu.HBM((chunks, 24, 128), bf16),
+            jax.ShapeDtypeStruct((chunks, 24, 128), f32),
+            jax.ShapeDtypeStruct((chunks, 24, 128), bf16),
         ),
-        in_specs=[pl.BlockSpec(memory_space=pltpu.SMEM)] + [OUTSIDE] * 2 + [INSIDE] * 3 + [OUTSIDE] * 3,
-        out_specs=(OUTSIDE, OUTSIDE, INSIDE),
-        scratch_shapes=[pltpu.VMEM(x.shape, bf16) for x in (got, stk, slope, act_t, xhat_t, slope)]
+        in_specs=[scalars] * 2 + [OUTSIDE] * 2 + [INSIDE] * 3 + [OUTSIDE] * 3,
+        out_specs=(OUTSIDE, OUTSIDE, INSIDE, INSIDE),
+        scratch_shapes=[pltpu.VMEM(x.shape, bf16) for x in (got, stk, slope, act_t, xhat_t)]
         + [
+            pltpu.VMEM((n, ch), bf16),
             pltpu.VMEM((nrow, cells, ch), f32),
             pltpu.VMEM((nrow, cells, ch), f32),
             pltpu.VMEM((nv, ch), f32),
@@ -316,13 +333,16 @@
         compiler_params=params(),
         cost_estimate=cost(10 * n * ch * hid, 24 * 2**20),
         name="decode",
-    )(rows, *in_hbm(got, stk), head, head_t, w_out_t, *in_hbm(slope, act_t, xhat_t))
-
-
-def backward_kernel(lat_ref, left_ref, right_ref, gain_ref, w_in_t_ref, pre_grad_ref, both_ref, out_ref, first_ref, last_ref):
+    )(core, rows, *in_hbm(got, stk), head, head_t, w_out_t, *in_hbm(slope, act_t, xhat_t))
+
+
+def backward_kernel(
+    lat_ref, left_ref, right_ref, gain_ref, w_in_t_ref, w_out_t_ref, adv_ref, slope_ref, both_ref, out_ref, first_ref, last_ref
+):
     rows, cells, ch = lat_ref.shape
     xhat, inv = normalized(lat_ref[...].astype(f32), left_ref[...], right_ref[...])
-    gained = dot(pre_grad_ref[...], w_in_t_ref[...]) * gain_ref[...]
+    pre_grad = (dot(adv_ref[...], w_out_t_ref[...]) * slope_ref[...].astype(f32)).astype(bf16)
+    gained = dot(pre_grad, w_in_t_ref[...]) * gain_ref[...]
     gained = gained.reshape(rows, cells, ch)
     summed_grad = inv * (gained - xhat * jnp.mean(gained * xhat, axis=-1, keepdims=True))
     out_ref[...] = both_ref[...] + mixed(summed_grad, jnp.zeros((), f32), jnp.zeros((), f32))
@@ -330,7 +350,7 @@
     last_ref[...] = summed_grad[:, cells - 1 : cells, :]
 
 
-def backward(latent, left, right, gain, w_in_t, pre_grad, both):
+def backward(latent, left, right, gain, w_in_t, w_out_t, adv, slope, both):
     rows, cells, ch = latent.shape
     hid = w_in_t.shape[0]
     step = ROWS_STEP * cells
@@ -350,14 +370,16 @@
             edge,
             pl.BlockSpec((1, ch), lambda i: (0, 0)),
             pl.BlockSpec((hid, ch), lambda i: (0, 0)),
+            pl.BlockSpec((ch, hid), lambda i: (0, 0)),
+            pl.BlockSpec((step, ch), lambda i: (i, 0)),
             pl.BlockSpec((step, hid), lambda i: (i, 0)),
             whole,
         ],
         out_specs=(whole, edge, edge),
         compiler_params=params(),
-        cost_estimate=cost(2 * rows * cells * ch * hid, 16 * 2**20),
+        cost_estimate=cost(4 * rows * cells * ch * hid, 16 * 2**20),
         name="backward",
-    )(latent, left, right, gain, w_in_t, pre_grad, both)
+    )(latent, left, right, gain, w_in_t, w_out_t, *in_hbm(adv, slope, both))
 
 
 def edges_kernel(left_ref, right_ref, grad_ref, out_ref):
@@ -401,17 +423,37 @@
     )(got)
 
 
-def finish_kernel(got_ref, gain_ref, w_in_ref, in_ref, out_ref, gain_grad_ref, head_ref, *, devices):
+def pair_kernel(keep_ref, came_ref, out_ref):
+    out_ref[...] = (keep_ref[...] + came_ref[...].astype(f32)).astype(bf16)
+
+
+def pair(keep, came):
+    return pl.pallas_call(
+        pair_kernel,
+        out_shape=jax.ShapeDtypeStruct(keep.shape, bf16),
+        compiler_params=params(),
+        cost_estimate=cost(keep.size, 8 * keep.size),
+        name="pair",
+    )(keep, came)
+
+
+def finish_kernel(core_ref, mine_ref, other_ref, gain_ref, w_in_ref, in_ref, out_ref, gain_grad_ref, head_ref, *, devices):
     share = 1.0 / devices
-    x = take_chunks(got_ref, 0, in_ref.shape) * share
-    in_ref[...] = x * gain_ref[...]
-    per_channel = jnp.sum(x * w_in_ref[...].astype(f32), axis=1, keepdims=True)
-    gain_grad_ref[...] = jnp.broadcast_to(per_channel, (x.shape[0], 128)).T[0:1, :]
-    out_ref[...] = take_chunks(got_ref, 1, out_ref.shape) * share
-    head_ref[...] = (take_chunks(got_ref, 2, head_ref.shape[::-1]) * share).T
-
-
-def finish(got, gain, w_in, head, devices):
+    for core in range(2):
+
+        @pl.when(core_ref[0] == core)
+        def _(core=core):
+            pair = (mine_ref, other_ref) if core == 0 else (other_ref, mine_ref)
+            halves = [ref[...].astype(f32) * share for ref in pair]
+            x = take_chunks(halves, 0, in_ref.shape)
+            in_ref[...] = x * gain_ref[...]
+            per_channel = jnp.sum(x * w_in_ref[...].astype(f32), axis=1, keepdims=True)
+            gain_grad_ref[...] = jnp.broadcast_to(per_channel, (x.shape[0], 128)).T[0:1, :]
+            out_ref[...] = take_chunks(halves, 1, out_ref.shape)
+            head_ref[...] = take_chunks(halves, 2, head_ref.shape[::-1]).T
+
+
+def finish(core, mine, other, gain, w_in, head, devices):
     ch, hid = w_in.shape
     return pl.pallas_call(
         functools.partial(finish_kernel, devices=devices),
@@ -421,57 +463,71 @@
             jax.ShapeDtypeStruct((1, ch), f32),
             jax.ShapeDtypeStruct(head.shape, f32),
         ),
+        in_specs=[pl.BlockSpec(memory_space=pltpu.SMEM)] + [INSIDE] * 4,
+        out_specs=(INSIDE,) * 4,
         compiler_params=params(),
         cost_estimate=cost(4 * ch * hid, 3 * 2**20),
         name="finish",
-    )(got, gain.reshape(ch, 1), w_in)
+    )(core, mine, other, gain.reshape(ch, 1), w_in)
+
+
+LON = ("chip", "core")
 
 
 def from_sides(first, last):
-    count = lax.axis_size("lon")
-    left = lax.ppermute(last, "lon", [(i, (i + 1) % count) for i in range(count)])
-    right = lax.ppermute(first, "lon", [((i + 1) % count, i) for i in range(count)])
+    count = lax.axis_size("chip") * lax.axis_size("core")
+    left = lax.ppermute(last, LON, [(i, (i + 1) % count) for i in range(count)])
+    right = lax.ppermute(first, LON, [((i + 1) % count, i) for i in range(count)])
     return left, right
 
 
 def body(latent, row_index, weights, slots, counts, targets, gain, w_in, w_out, head):
-    both_axes = ("band", "lon")
-    devices = lax.axis_size("band") * lax.axis_size("lon")
+    chips = ("band", "chip")
+    swap = [(0, 1), (1, 0)]
+    groups = lax.axis_size("band") * lax.axis_size("chip")
+    core = lax.axis_index("core").astype(jnp.int32).reshape(1)
     cells = latent.shape[1]
     packed = pack(weights, targets, slots, counts)
     left, right = from_sides(latent[:, 0:1, :], latent[:, cells - 1 : cells, :])
     packed, left, right = lax.optimization_barrier((packed, left, right))
-    got = lax.all_to_all(packed, "lon", 0, 0, tiled=True)
+    got = lax.all_to_all(packed, LON, 0, 0, tiled=True)
     left, right = left.astype(f32), right.astype(f32)
     gain_row = gain.reshape(1, -1)
+    w_out_t = w_out.T
     stk, slope, act_t, xhat_t = forward(latent, left, right, gain_row, w_in, w_out)
-    pre_grad, both, sums = decode(row_index, got, stk, head, head.T, w_out.T, slope, act_t, xhat_t, devices)
-    parts = lax.all_to_all(sums, both_axes, 0, 0, tiled=True)
-    grad, first, last = backward(latent, left, right, gain_row, w_in.T, pre_grad, both)
+    adv, both, keep, send = decode(core, row_index, got, stk, head, head.T, w_out_t, slope, act_t, xhat_t, groups)
+    came = lax.ppermute(send, "core", swap)
+    parts = lax.all_to_all(pair(keep, came), chips, 0, 0, tiled=True)
+    grad, first, last = backward(latent, left, right, gain_row, w_in.T, w_out_t, adv, slope, both)
     parts, first, last = lax.optimization_barrier((parts, first, last))
     grad_left, grad_right = from_sides(first.astype(bf16), last.astype(bf16))
     grad = add_edges(grad, grad_left.astype(f32), grad_right.astype(f32))
-    chunks = lax.all_to_all(total(parts), both_axes, 0, 0, tiled=True)
-    grad_in, grad_out, grad_gain, grad_head = finish(chunks, gain, w_in, head, devices)
+    mine = lax.all_to_all(total(parts), chips, 0, 0, tiled=True)
+    mine, grad = lax.optimization_barrier((mine, grad))
+    other = lax.ppermute(mine, "core", swap)
+    grad_in, grad_out, grad_gain, grad_head = finish(core, mine, other, gain, w_in, head, 2 * groups)
     return grad, grad_in, grad_out, grad_gain.reshape(-1), grad_head
 
 
 def solution(mesh):
+    bands, lons = mesh.devices.shape
+    by_core = jax.sharding.Mesh(mesh.devices.reshape(bands, lons // 2, 2), ("band", "chip", "core"))
+    every = ("band", "chip", "core")
     return jax.shard_map(
         body,
-        mesh=mesh,
+        mesh=by_core,
         in_specs=(
-            P("band", "lon", None),
-            P("band", "lon", None),
-            P(("band", "lon"), None, None),
-            P(("band", "lon"), None),
-            P(("band", "lon")),
-            P(("band", "lon"), None, None),
+            P("band", LON, None),
+            P("band", LON, None),
+            P(every, None, None),
+            P(every, None),
+            P(every),
+            P(every, None, None),
             P(),
             P(),
             P(),
             P(),
         ),
-        out_specs=(P("band", "lon", None), P(), P(), P(), P()),
+        out_specs=(P("band", LON, None), P(), P(), P(), P()),
         check_vma=False,
     )

time: 109 us -> 107 us (0.982)
  waiting for transfers between devices: 41.5 us -> 29.6 us
  starting transfers between devices: 24.5 us -> 34.6 us
    all_to_all x3, waiting for transfers between devices: 32.1 us -> 22.3 us  [the longest x1 20 us: body(): got = lax.all_to_all(packed, LON, 0, 0, tiled=True)]
    all_to_all x3, starting transfers between devices: 20 us -> 26 us  [the longest x1 10.2 us: body(): parts = lax.all_to_all(pair(keep, came), chips, 0, 0, tiled=True)]
    ppermute x4 -> x6, starting transfers between devices: 4.53 us -> 8.69 us  [the longest x2 5.13 us: from_sides(): left = lax.ppermute(last, LON, [(i, (i + 1) % count) for i in range(count)])]
    ppermute x4 -> x6, waiting for transfers between devices: 9.4 us -> 7.25 us  [the longest x2 3.54 us: from_sides(): lax.ppermute(first, LON, [((i + 1) % count, i) for i in range(count)])]
    pallas_call x1, Pallas kernels: 9.26 us -> 10.7 us  [backward(): pl.pallas_call(backward_kernel, grid=(rows // ROWS_STEP,), out_shape=(jax...]
    pallas_call x1 -> x2, Pallas kernels: 15.1 us -> 14 us  [the longest x1 13.2 us: decode(): pl.pallas_call(decode_kernel, out_shape=(pltpu.HBM((n, ch), bf16), pltpu....]
  transfers between devices with their start and end apart: 7 -> 9, of which waited for: 6 -> 8; matrix products, arithmetic and copies ran while one was open for 1% -> 1% of each run, Pallas kernels for 20% -> 22%
where the time goes in v4:
time: 107 us
  Pallas kernels  39.8 us (37%)
  starting transfers between devices  34.6 us (32%)
  waiting for transfers between devices  29.6 us (28%)
  local copies, waits for them, and re-layouts  1.57 us (1%)
    all_to_all x1, waiting for transfers between devices, body(): got = lax.all_to_all(packed, LON, 0, 0, tiled=True)  20 us
    pallas_call x1, Pallas kernels, decode(): pl.pallas_call(decode_kernel, out_shape=(pltpu.HBM((n, ch), bf16), pltpu....  13.2 us
    pallas_call x1, Pallas kernels, backward(): pl.pallas_call(backward_kernel, grid=(rows // ROWS_STEP,), out_shape=(jax...  10.7 us
    all_to_all x1, starting transfers between devices, body(): parts = lax.all_to_all(pair(keep, came), chips, 0, 0, tiled=True)  10.2 us
    all_to_all x1, starting transfers between devices, body(): mine = lax.all_to_all(total(parts), chips, 0, 0, tiled=True)  9.43 us
    pallas_call x1, Pallas kernels, forward(): pl.pallas_call(forward_kernel, grid=(rows // ROWS_STEP,), out_shape=(pltp...  8.16 us
    all_to_all x1, starting transfers between devices, body(): got = lax.all_to_all(packed, LON, 0, 0, tiled=True)  6.32 us
    ppermute x2, starting transfers between devices, from_sides(): left = lax.ppermute(last, LON, [(i, (i + 1) % count) for i in range(count)])  5.13 us
  transfers between devices with their start and end apart: 9, of which 8 were waited for; matrix products, arithmetic and copies ran while one was open for 1% of the time, Pallas kernels for 22%

profile of v4, /device:TPU:1, one launch (start us, length us, event | category | flops | bytes accessed | tf_op | source)
XLA Modules:
  0.0 106.6 jit_solution(3323502342242737065)
XLA Ops:
  0.6 1.0 fusion
  1.7 2.7 %collective-permute-start = (bf16[32,1,256]{2,1,0:T(2,128)(2,1)S(1)}, bf16[32,1,256]{2,1,0:T(2,128)(2,1)S(1)}, u32[]{:S(2)}, u32[]{:S(2)}) collective-permute-start(bf16[32,1,256]{2,1,0:T(2,128)(2,1)S(1)} %get-tuple-element.52), channel_id=1, source_target_pairs={{0,1},{1,2},{2,3},{3,4},{4,5},{5,6},{6,7},{7,8},{8,9},{9,10},{10,1... | collective-permute-start | bytes 49160 | tf_op jit(solution)/shard_map/ppermute | solution.py:479
  4.3 0.0 copy-start.2
  4.3 0.0 copy-start.3
  4.3 0.0 copy-start
  4.3 0.0 copy-start.1
  4.3 0.0 copy-start.4
  4.4 0.1 collective-permute-start.1
  4.4 2.9 %pack.1 = bf16[32,264,128]{2,1,0:T(8,128)(2,1)} custom-call(bf16[32,128,128]{2,1,0:T(8,128)(2,1)} %w_hbm.1, bf16[32,128,128]{2,1,0:T(8,128)(2,1)} %t_hbm.1, s32[32,128]{1,0:T(8,128)} %slot_hbm.1, s32[32]{0:T(128)} %count_hbm.1), custom_call_target="tpu_custom_call" | custom-call | flops 1 | bytes 4194304 | tf_op jit(solution)/shard_map/pack/pallas_call | solution.py:88
  7.4 0.0 collective-permute-done
  7.4 0.7 collective-permute-done.1
  8.1 6.3 %all-to-all-start = ((bf16[32,264,128]{2,1,0:T(8,128)(2,1)}), bf16[32,264,128]{2,1,0:T(8,128)(2,1)}, u32[]{:S(2)}, u32[]{:S(2)}) async-start(bf16[32,264,128]{2,1,0:T(8,128)(2,1)} %pack.1), calls=%async_computation | async-start | bytes 4325376 | tf_op jit(solution)/shard_map/all_to_all | solution.py:493
  14.4 0.0 copy-done.2
  14.4 0.1 copy.20
  14.5 0.0 copy-start.5
  14.5 0.0 copy-done.3
  14.6 0.1 copy.19
  14.8 0.0 copy-done
  14.8 0.0 copy-done.1
  14.8 0.0 copy-done.4
  14.8 8.2 %forward.1 = (bf16[32,256,256]{2,1,0:T(8,128)(2,1)}, bf16[4096,512]{1,0:T(8,128)(2,1)}, bf16[512,4096]{1,0:T(8,128)(2,1)}, bf16[256,4096]{1,0:T(8,128)(2,1)}) custom-call(bf16[32,128,256]{2,1,0:T(8,128)(2,1)S(1)} %copy-done, f32[32,1,256]{2,1,0:T(1,128)S(1)} %convert_element_type.18.left_ref, f32[32,1,256]{2,1,0:T(1,128)S(1)} %convert_element_type.19.right_ref, ...), custom_call_target="tpu_custom_call" | custom-call | flops 2147483648 | bytes 16777216 | tf_op jit(solution)/shard_map/forward/pallas_call | solution.py:144
  22.9 20.0 %all-to-all-done.got_hbm = bf16[32,264,128]{2,1,0:T(8,128)(2,1)} async-done(((bf16[32,264,128]{2,1,0:T(8,128)(2,1)}), bf16[32,264,128]{2,1,0:T(8,128)(2,1)}, u32[]{:S(2)}, u32[]{:S(2)}) %all-to-all-start) | async-done | bytes 2162720 | tf_op jit(solution)/shard_map/all_to_all | solution.py:493
  42.9 0.0 copy-done.5
  42.9 13.2 %decode.1 = (bf16[4096,256]{1,0:T(8,128)(2,1)}, f32[32,128,256]{2,1,0:T(8,128)}, f32[64,24,128]{2,1,0:T(8,128)S(1)}, bf16[64,24,128]{2,1,0:T(8,128)(2,1)S(1)}) custom-call(s32[1]{0:T(128)} %bitcast.core_ref, s32[1,1,32]{2,1,0:T(1,128)S(1)} %copy-done.5, bf16[32,264,128]{2,1,0:T(8,128)(2,1)} %all-to-all-done.got_hbm, ...), custom_call_target="tpu_custom_call" | custom-call | flops 5368709120 | bytes 25165824 | tf_op jit(solution)/shard_map/decode/pallas_call | solution.py:310
  56.1 0.6 collective-permute-start.2
  56.7 1.3 %collective-permute-done.2.came_ref = bf16[64,24,128]{2,1,0:T(8,128)(2,1)S(1)} collective-permute-done((bf16[64,24,128]{2,1,0:T(8,128)(2,1)S(1)}, bf16[64,24,128]{2,1,0:T(8,128)(2,1)S(1)}, u32[]{:S(2)}, u32[]{:S(2)}) %collective-permute-start.2) | collective-permute-done | bytes 393248 | tf_op jit(solution)/shard_map/ppermute | solution.py:499
  58.1 0.8 pair.1
  58.9 10.2 %all-to-all-start.1 = ((bf16[64,24,128]{2,1,0:T(8,128)(2,1)}), bf16[64,24,128]{2,1,0:T(8,128)(2,1)S(1)}, u32[]{:S(2)}, u32[]{:S(2)}) async-start(bf16[64,24,128]{2,1,0:T(8,128)(2,1)} %pair.1), calls=%async_computation.1 | async-start | bytes 786432 | tf_op jit(solution)/shard_map/all_to_all | solution.py:500
  69.1 0.1 copy.21
  69.2 10.7 %backward.1 = (f32[32,128,256]{2,1,0:T(8,128)}, f32[32,1,256]{2,1,0:T(1,128)S(1)}, f32[32,1,256]{2,1,0:T(1,128)S(1)}) custom-call(bf16[32,128,256]{2,1,0:T(8,128)(2,1)S(1)} %copy-done, f32[32,1,256]{2,1,0:T(1,128)S(1)} %convert_element_type.18.left_ref, f32[32,1,256]{2,1,0:T(1,128)S(1)} %convert_element_type.19.right_ref, f32[1,256]{1,0:T(1,128)S(1)} %bitcast.12, ...), custom_call_target="tpu_custom_call" | custom-call | flops 2147483648 | bytes 16777216 | tf_op jit(solution)/shard_map/backward/pallas_call | solution.py:359
  80.0 0.4 all-to-all-done.1.got_ref
  80.4 0.8 total.1
  81.2 9.4 %all-to-all-start.2 = ((bf16[64,24,128]{2,1,0:T(8,128)(2,1)}), bf16[64,24,128]{2,1,0:T(8,128)(2,1)S(1)}, u32[]{:S(2)}, u32[]{:S(2)}) async-start(bf16[64,24,128]{2,1,0:T(8,128)(2,1)} %total.1), calls=%async_computation.2 | async-start | bytes 786432 | tf_op jit(solution)/shard_map/all_to_all | solution.py:505
  90.7 2.5 %collective-permute-start.3 = (bf16[32,1,256]{2,1,0:T(2,128)(2,1)S(1)}, bf16[32,1,256]{2,1,0:T(2,128)(2,1)S(1)}, u32[]{:S(2)}, u32[]{:S(2)}) collective-permute-start(bf16[32,1,256]{2,1,0:T(2,128)(2,1)S(1)} %convert_element_type.20), channel_id=1, source_target_pairs={{0,1},{1,2},{2,3},{3,4},{4,5},{5,6},{6,7},{7,8},{8,9},{9,10},{10,1... | collective-permute-start | bytes 49160 | tf_op jit(solution)/shard_map/ppermute | solution.py:479
  93.2 0.1 collective-permute-start.4
  93.3 1.1 %collective-permute-done.3 = bf16[32,1,256]{2,1,0:T(2,128)(2,1)S(1)} collective-permute-done((bf16[32,1,256]{2,1,0:T(2,128)(2,1)S(1)}, bf16[32,1,256]{2,1,0:T(2,128)(2,1)S(1)}, u32[]{:S(2)}, u32[]{:S(2)}) %collective-permute-start.3) | collective-permute-done | bytes 16416 | tf_op jit(solution)/shard_map/ppermute | solution.py:479
  94.4 2.9 %collective-permute-done.4 = bf16[32,1,256]{2,1,0:T(2,128)(2,1)S(1)} collective-permute-done((bf16[32,1,256]{2,1,0:T(2,128)(2,1)S(1)}, bf16[32,1,256]{2,1,0:T(2,128)(2,1)S(1)}, u32[]{:S(2)}, u32[]{:S(2)}) %collective-permute-start.4) | collective-permute-done | bytes 16416 | tf_op jit(solution)/shard_map/ppermute | solution.py:480
  97.4 1.8 %edges.1 = f32[32,128,256]{2,1,0:T(8,128)} custom-call(f32[32,1,256]{2,1,0:T(1,128)S(1)} %convert_element_type.21.left_ref, f32[32,1,256]{2,1,0:T(1,128)S(1)} %convert_element_type.23.right_ref, f32[32,128,256]{2,1,0:T(8,128)} %get-tuple-element.44.grad_ref), custom_call_target="tpu_custom_call", output_to_operand_aliasing={{}: (2, {})} | custom-call | flops 131072 | bytes 1048576 | tf_op jit(solution)/shard_map/edges/pallas_call | solution.py:398
  99.2 2.0 %all-to-all-done.2.mine_ref = bf16[64,24,128]{2,1,0:T(8,128)(2,1)S(1)} async-done(((bf16[64,24,128]{2,1,0:T(8,128)(2,1)}), bf16[64,24,128]{2,1,0:T(8,128)(2,1)S(1)}, u32[]{:S(2)}, u32[]{:S(2)}) %all-to-all-start.2) | async-done | bytes 393248 | tf_op jit(solution)/shard_map/all_to_all | solution.py:505
  101.1 2.8 %collective-permute-start.5 = (bf16[64,24,128]{2,1,0:T(8,128)(2,1)S(1)}, bf16[64,24,128]{2,1,0:T(8,128)(2,1)S(1)}, u32[]{:S(2)}, u32[]{:S(2)}) collective-permute-start(bf16[64,24,128]{2,1,0:T(8,128)(2,1)S(1)} %all-to-all-done.2.mine_ref), channel_id=1, source_target_pairs={{0,1},{1,0},{2,3},{3,2},{4,5},{5,4},{6,7},{7,6},{8,9},{9,8},{10,11... | collective-permute-start | bytes 1179656 | tf_op jit(solution)/shard_map/ppermute | solution.py:507
  103.9 0.1 copy.22.gain_ref
  104.1 1.2 %collective-permute-done.5.other_ref = bf16[64,24,128]{2,1,0:T(8,128)(2,1)S(1)} collective-permute-done((bf16[64,24,128]{2,1,0:T(8,128)(2,1)S(1)}, bf16[64,24,128]{2,1,0:T(8,128)(2,1)S(1)}, u32[]{:S(2)}, u32[]{:S(2)}) %collective-permute-start.5) | collective-permute-done | bytes 393248 | tf_op jit(solution)/shard_map/ppermute | solution.py:507
  105.3 1.3 %finish.1 = (f32[256,512]{1,0:T(8,128)}, f32[512,256]{1,0:T(8,128)}, f32[1,256]{1,0:T(1,128)}, f32[256,128]{1,0:T(8,128)}) custom-call(s32[1]{0:T(128)} %bitcast.core_ref, bf16[64,24,128]{2,1,0:T(8,128)(2,1)S(1)} %all-to-all-done.2.mine_ref, bf16[64,24,128]{2,1,0:T(8,128)(2,1)S(1)} %collective-permute-done.5.other_ref, f32[256,1]{1,0:T(8,128)S(1)} %copy.22.gain_ref, ...), custom_call_target="tpu_custom_call" | custom-call | flops 524288 | bytes 3145728 | tf_op jit(solution)/shard_map/finish/pallas_call | solution.py:458
  (6 shorter events, 0.2 us)
Async XLA Ops:
  1.7 5.7 %collective-permute-start = (bf16[32,1,256]{2,1,0:T(2,128)(2,1)S(1)}, bf16[32,1,256]{2,1,0:T(2,128)(2,1)S(1)}, u32[]{:S(2)}, u32[]{:S(2)}) collective-permute-start(bf16[32,1,256]{2,1,0:T(2,128)(2,1)S(1)} %get-tuple-element.52), channel_id=1, source_target_pairs={{0,1},{1,2},{2,3},{3,4},{4,5},{5,6},{6,7},{7,8},{8,9},{9,10},{10,1... | collective-permute-start | bytes 49160 | tf_op jit(solution)/shard_map/ppermute | solution.py:479
  4.3 10.0 %copy-start.2 = (bf16[512,256]{1,0:T(8,128)(2,1)S(1)}, bf16[512,256]{1,0:T(8,128)(2,1)}, u32[]{:S(2)}) copy-start(bf16[512,256]{1,0:T(8,128)(2,1)} %w_out_ref.1) | copy-start | bytes 786436
  4.3 10.2 %copy-start.3 = (bf16[256,128]{1,0:T(8,128)(2,1)S(1)}, bf16[256,128]{1,0:T(8,128)(2,1)}, u32[]{:S(2)}) copy-start(bf16[256,128]{1,0:T(8,128)(2,1)} %head_ref.1) | copy-start | bytes 196612
  4.3 10.4 %copy-start = (bf16[32,128,256]{2,1,0:T(8,128)(2,1)S(1)}, bf16[32,128,256]{2,1,0:T(8,128)(2,1)}, u32[]{:S(2)}) copy-start(bf16[32,128,256]{2,1,0:T(8,128)(2,1)} %lat_ref.3) | copy-start | bytes 6291460
  4.3 10.4 %copy-start.1 = (bf16[256,512]{1,0:T(8,128)(2,1)S(1)}, bf16[256,512]{1,0:T(8,128)(2,1)}, u32[]{:S(2)}) copy-start(bf16[256,512]{1,0:T(8,128)(2,1)} %w_in_ref.3) | copy-start | bytes 786436
  4.3 10.4 %copy-start.4 = (f32[256]{0:T(256)S(1)}, f32[256]{0:T(256)}, u32[]{:S(2)}) copy-start(f32[256]{0:T(256)} %param.16) | copy-start | bytes 3076
  4.4 3.7 %collective-permute-start.1 = (bf16[32,1,256]{2,1,0:T(2,128)(2,1)S(1)}, bf16[32,1,256]{2,1,0:T(2,128)(2,1)S(1)}, u32[]{:S(2)}, u32[]{:S(2)}) collective-permute-start(bf16[32,1,256]{2,1,0:T(2,128)(2,1)S(1)} %get-tuple-element.51), channel_id=1, source_target_pairs={{1,0},{2,1},{3,2},{4,3},{5,4},{6,5},{7,6},{8,7},{9,8},{10,9},{11,1... | collective-permute-start | bytes 49160 | tf_op jit(solution)/shard_map/ppermute | solution.py:480
  8.1 34.8 %all-to-all-start = ((bf16[32,264,128]{2,1,0:T(8,128)(2,1)}), bf16[32,264,128]{2,1,0:T(8,128)(2,1)}, u32[]{:S(2)}, u32[]{:S(2)}) async-start(bf16[32,264,128]{2,1,0:T(8,128)(2,1)} %pack.1), calls=%async_computation | async-start | bytes 4325376 | tf_op jit(solution)/shard_map/all_to_all | solution.py:493
  14.5 28.4 %copy-start.5 = (s32[1,1,32]{2,1,0:T(1,128)S(1)}, s32[1,1,32]{2,1,0:T(1,128)}, u32[]{:S(2)}) copy-start(s32[1,1,32]{2,1,0:T(1,128)} %rows_ref.1) | copy-start | bytes 388
  56.1 1.9 %collective-permute-start.2 = (bf16[64,24,128]{2,1,0:T(8,128)(2,1)S(1)}, bf16[64,24,128]{2,1,0:T(8,128)(2,1)S(1)}, u32[]{:S(2)}, u32[]{:S(2)}) collective-permute-start(bf16[64,24,128]{2,1,0:T(8,128)(2,1)S(1)} %get-tuple-element.36), channel_id=1, source_target_pairs={{0,1},{1,0},{2,3},{3,2},{4,5},{5,4},{6,7},{7,6},{8,9},{9,8},{10,11... | collective-permute-start | bytes 1179656 | tf_op jit(solution)/shard_map/ppermute | solution.py:499
  58.9 21.5 %all-to-all-start.1 = ((bf16[64,24,128]{2,1,0:T(8,128)(2,1)}), bf16[64,24,128]{2,1,0:T(8,128)(2,1)S(1)}, u32[]{:S(2)}, u32[]{:S(2)}) async-start(bf16[64,24,128]{2,1,0:T(8,128)(2,1)} %pair.1), calls=%async_computation.1 | async-start | bytes 786432 | tf_op jit(solution)/shard_map/all_to_all | solution.py:500
  81.2 19.9 %all-to-all-start.2 = ((bf16[64,24,128]{2,1,0:T(8,128)(2,1)}), bf16[64,24,128]{2,1,0:T(8,128)(2,1)S(1)}, u32[]{:S(2)}, u32[]{:S(2)}) async-start(bf16[64,24,128]{2,1,0:T(8,128)(2,1)} %total.1), calls=%async_computation.2 | async-start | bytes 786432 | tf_op jit(solution)/shard_map/all_to_all | solution.py:505
  90.7 3.7 %collective-permute-start.3 = (bf16[32,1,256]{2,1,0:T(2,128)(2,1)S(1)}, bf16[32,1,256]{2,1,0:T(2,128)(2,1)S(1)}, u32[]{:S(2)}, u32[]{:S(2)}) collective-permute-start(bf16[32,1,256]{2,1,0:T(2,128)(2,1)S(1)} %convert_element_type.20), channel_id=1, source_target_pairs={{0,1},{1,2},{2,3},{3,4},{4,5},{5,6},{6,7},{7,8},{8,9},{9,10},{10,1... | collective-permute-start | bytes 49160 | tf_op jit(solution)/shard_map/ppermute | solution.py:479
  93.2 4.1 %collective-permute-start.4 = (bf16[32,1,256]{2,1,0:T(2,128)(2,1)S(1)}, bf16[32,1,256]{2,1,0:T(2,128)(2,1)S(1)}, u32[]{:S(2)}, u32[]{:S(2)}) collective-permute-start(bf16[32,1,256]{2,1,0:T(2,128)(2,1)S(1)} %convert_element_type.22), channel_id=1, source_target_pairs={{1,0},{2,1},{3,2},{4,3},{5,4},{6,5},{7,6},{8,7},{9,8},{10,9},{11,1... | collective-permute-start | bytes 49160 | tf_op jit(solution)/shard_map/ppermute | solution.py:480
  101.1 4.2 %collective-permute-start.5 = (bf16[64,24,128]{2,1,0:T(8,128)(2,1)S(1)}, bf16[64,24,128]{2,1,0:T(8,128)(2,1)S(1)}, u32[]{:S(2)}, u32[]{:S(2)}) collective-permute-start(bf16[64,24,128]{2,1,0:T(8,128)(2,1)S(1)} %all-to-all-done.2.mine_ref), channel_id=1, source_target_pairs={{0,1},{1,0},{2,3},{3,2},{4,5},{5,4},{6,7},{7,6},{8,9},{9,8},{10,11... | collective-permute-start | bytes 1179656 | tf_op jit(solution)/shard_map/ppermute | solution.py:507

commit v5 on v4

--- a/solution.py
+++ b/solution.py
@@ -10,7 +10,7 @@
 
 WINDOW_SLOTS = 7
 NORM_EPS = 1e-05
-ROWS_STEP = 4
+ROWS_STEP = 8
 BLOCKS_STEP = 8
 PULL_ROWS = 16
 PACK_CHUNKS = 4
@@ -118,22 +118,32 @@
     return summed * inv, inv
 
 
-def forward_kernel(lat_ref, left_ref, right_ref, gain_ref, w_in_ref, w_out_ref, stk_ref, slope_ref, act_t_ref, xhat_t_ref):
+def forward_kernel(
+    lat_ref, left_ref, right_ref, gain_ref, w_in_ref, w_out_ref,
+    stk_ref, slope_ref, act_t_ref, xhat_t_ref, xhat_ref, inv_slope_ref, ends_ref,
+):
     rows, cells, ch = lat_ref.shape
     lat_b = lat_ref[...]
     lat = lat_b.astype(f32)
-    xhat, _ = normalized(lat, left_ref[...], right_ref[...])
-    xhat = xhat.reshape(rows * cells, ch)
+    xhat3, inv3 = normalized(lat, left_ref[...], right_ref[...])
+    for k, cell in enumerate((0, cells - 1)):
+        ends_ref[2 * k] = xhat3[:, cell, :]
+        ends_ref[2 * k + 1] = jnp.broadcast_to(inv3[:, cell, :], (rows, ch))
+    xhat = xhat3.reshape(rows * cells, ch)
     pre = dot((xhat * gain_ref[...]).astype(bf16), w_in_ref[...])
     sig = jax.nn.sigmoid(pre)
     act = pre * sig
     act_b = act.astype(bf16)
-    slope_ref[...] = (sig * (1.0 + pre * (1.0 - sig))).astype(bf16)
+    slope = sig * (1.0 + pre * (1.0 - sig))
+    slope_ref[...] = slope.astype(bf16)
+    inv_slope_ref[...] = (slope * inv3.reshape(rows * cells, 1)).astype(bf16)
     new = lat.reshape(rows * cells, ch) + dot(act_b, w_out_ref[...])
     stk_ref[:, 0:cells, :] = lat_b
     stk_ref[:, cells : 2 * cells, :] = new.astype(bf16).reshape(rows, cells, ch)
+    xhat_b = xhat.astype(bf16)
+    xhat_ref[...] = xhat_b
     act_t_ref[...] = act_b.T
-    xhat_t_ref[...] = xhat.astype(bf16).T
+    xhat_t_ref[...] = xhat_b.T
 
 
 def forward(latent, left, right, gain, w_in, w_out):
@@ -149,6 +159,9 @@
             pltpu.HBM((n, hid), bf16),
             pltpu.HBM((hid, n), bf16),
             pltpu.HBM((ch, n), bf16),
+            pltpu.HBM((n, ch), bf16),
+            pltpu.HBM((n, hid), bf16),
+            jax.ShapeDtypeStruct((4, rows, ch), f32),
         ),
         in_specs=[
             pl.BlockSpec((ROWS_STEP, cells, ch), lambda i: (i, 0, 0)),
@@ -163,6 +176,9 @@
             pl.BlockSpec((step, hid), lambda i: (i, 0)),
             pl.BlockSpec((hid, step), lambda i: (0, i)),
             pl.BlockSpec((ch, step), lambda i: (0, i)),
+            pl.BlockSpec((step, ch), lambda i: (i, 0)),
+            pl.BlockSpec((step, hid), lambda i: (i, 0)),
+            pl.BlockSpec((4, ROWS_STEP, ch), lambda i: (0, i, 0)),
         ),
         compiler_params=params(),
         cost_estimate=cost(4 * n * ch * hid, 16 * 2**20, 2 * n * hid),
@@ -171,9 +187,10 @@
 
 
 def decode_kernel(
-    core_ref, rows_ref, got_hbm, stk_hbm, head_ref, head_t_ref, w_out_t_ref, slope_hbm, act_t_hbm, xhat_t_hbm,
-    adv_hbm, both_hbm, keep_ref, send_ref,
-    got, stk, slope, act_t, xhat_t, adv_all, acc_both, acc_new, acc_head, acc_in, acc_out,
+    core_ref, rows_ref, got_hbm, stk_hbm, head_ref, head_t_ref, w_out_t_ref, w_in_t_ref, gain_ref, ends_ref,
+    slope_hbm, act_t_hbm, xhat_t_hbm,
+    adv_hbm, both_hbm, keep_ref, send_ref, first_ref, last_ref,
+    got, stk, slope, act_t, xhat_t, adv_all, both_all, ends, acc_both, acc_new, acc_head, acc_in, acc_out,
     got_sems, stk_sems, in_sems, out_sems,
 ):
     nb, nr = BLOCKS_STEP, PULL_ROWS
@@ -244,7 +261,8 @@
         return carry
 
     lax.fori_loop(0, blocks // nb, observe, 0)
-    both_copy = pltpu.make_async_copy(acc_both, both_hbm, out_sems.at[rows // nr])
+    both_all[...] = acc_both[...].astype(bf16)
+    both_copy = pltpu.make_async_copy(both_all, both_hbm, out_sems.at[rows // nr])
     both_copy.start()
     for c in later:
         c.wait()
@@ -255,11 +273,19 @@
         adv_all[flat, :] = adv
         adv_copy(k).start()
         pre_grad = (dot(adv, w_out_t_ref[...]) * slope[flat, :].astype(f32)).astype(bf16)
+        here = pl.ds(pl.multiple_of(k * nr, nr), nr)
+        by_row = pre_grad.reshape(nr, cells, pre_grad.shape[1])
+        ends[0, here, :] = by_row[:, 0, :].astype(f32)
+        ends[1, here, :] = by_row[:, cells - 1, :].astype(f32)
         acc_in[...] += dot(xhat_t[:, flat], pre_grad)
         acc_out[...] += dot(act_t[:, flat], adv)
         return carry
 
     lax.fori_loop(0, rows // nr, pull, 0)
+    for k, ref in enumerate((first_ref, last_ref)):
+        gained = dot(ends[k].astype(bf16), w_in_t_ref[...]) * gain_ref[...]
+        xhat, inv = ends_ref[2 * k], ends_ref[2 * k + 1]
+        ref[...] = (inv * (gained - xhat * jnp.mean(gained * xhat, axis=-1, keepdims=True))).astype(bf16)
     for core in range(2):
 
         @pl.when(core_ref[0] == core)
@@ -298,7 +324,7 @@
     )
 
 
-def decode(core, rows, got, stk, head, head_t, w_out_t, slope, act_t, xhat_t, chunks):
+def decode(core, rows, got, stk, head, head_t, w_out_t, w_in_t, gain, ends, slope, act_t, xhat_t, chunks):
     nrow, two_cells, ch = stk.shape
     cells = two_cells // 2
     nv = head.shape[1]
@@ -311,15 +337,19 @@
         decode_kernel,
         out_shape=(
             pltpu.HBM((n, ch), bf16),
-            pltpu.HBM((nrow, cells, ch), f32),
+            pltpu.HBM((nrow, cells, ch), bf16),
             jax.ShapeDtypeStruct((chunks, 24, 128), f32),
             jax.ShapeDtypeStruct((chunks, 24, 128), bf16),
+            jax.ShapeDtypeStruct((nrow, ch), bf16),
+            jax.ShapeDtypeStruct((nrow, ch), bf16),
         ),
-        in_specs=[scalars] * 2 + [OUTSIDE] * 2 + [INSIDE] * 3 + [OUTSIDE] * 3,
-        out_specs=(OUTSIDE, OUTSIDE, INSIDE, INSIDE),
+        in_specs=[scalars] * 2 + [OUTSIDE] * 2 + [INSIDE] * 6 + [OUTSIDE] * 3,
+        out_specs=(OUTSIDE, OUTSIDE) + (INSIDE,) * 4,
         scratch_shapes=[pltpu.VMEM(x.shape, bf16) for x in (got, stk, slope, act_t, xhat_t)]
         + [
             pltpu.VMEM((n, ch), bf16),
+            pltpu.VMEM((nrow, cells, ch), bf16),
+            pltpu.VMEM((2, nrow, hid), f32),
             pltpu.VMEM((nrow, cells, ch), f32),
             pltpu.VMEM((nrow, cells, ch), f32),
             pltpu.VMEM((nv, ch), f32),
@@ -333,25 +363,20 @@
         compiler_params=params(),
         cost_estimate=cost(10 * n * ch * hid, 24 * 2**20),
         name="decode",
-    )(core, rows, *in_hbm(got, stk), head, head_t, w_out_t, *in_hbm(slope, act_t, xhat_t))
-
-
-def backward_kernel(
-    lat_ref, left_ref, right_ref, gain_ref, w_in_t_ref, w_out_t_ref, adv_ref, slope_ref, both_ref, out_ref, first_ref, last_ref
-):
-    rows, cells, ch = lat_ref.shape
-    xhat, inv = normalized(lat_ref[...].astype(f32), left_ref[...], right_ref[...])
+    )(core, rows, *in_hbm(got, stk), head, head_t, w_out_t, w_in_t, gain, ends, *in_hbm(slope, act_t, xhat_t))
+
+
+def backward_kernel(left_ref, right_ref, gain_ref, w_in_t_ref, w_out_t_ref, adv_ref, slope_ref, xhat_ref, both_ref, out_ref):
+    rows, cells, ch = out_ref.shape
     pre_grad = (dot(adv_ref[...], w_out_t_ref[...]) * slope_ref[...].astype(f32)).astype(bf16)
     gained = dot(pre_grad, w_in_t_ref[...]) * gain_ref[...]
-    gained = gained.reshape(rows, cells, ch)
-    summed_grad = inv * (gained - xhat * jnp.mean(gained * xhat, axis=-1, keepdims=True))
-    out_ref[...] = both_ref[...] + mixed(summed_grad, jnp.zeros((), f32), jnp.zeros((), f32))
-    first_ref[...] = summed_grad[:, 0:1, :]
-    last_ref[...] = summed_grad[:, cells - 1 : cells, :]
-
-
-def backward(latent, left, right, gain, w_in_t, w_out_t, adv, slope, both):
-    rows, cells, ch = latent.shape
+    xhat = xhat_ref[...].astype(f32)
+    summed_grad = gained - xhat * jnp.mean(gained * xhat, axis=-1, keepdims=True)
+    out_ref[...] = both_ref[...].astype(f32) + mixed(summed_grad.reshape(rows, cells, ch), left_ref[...], right_ref[...])
+
+
+def backward(left, right, gain, w_in_t, w_out_t, adv, inv_slope, xhat, both):
+    rows, cells, ch = both.shape
     hid = w_in_t.shape[0]
     step = ROWS_STEP * cells
     edge = pl.BlockSpec((ROWS_STEP, 1, ch), lambda i: (i, 0, 0))
@@ -359,13 +384,8 @@
     return pl.pallas_call(
         backward_kernel,
         grid=(rows // ROWS_STEP,),
-        out_shape=(
-            jax.ShapeDtypeStruct((rows, cells, ch), f32),
-            jax.ShapeDtypeStruct((rows, 1, ch), f32),
-            jax.ShapeDtypeStruct((rows, 1, ch), f32),
-        ),
+        out_shape=jax.ShapeDtypeStruct((rows, cells, ch), f32),
         in_specs=[
-            whole,
             edge,
             edge,
             pl.BlockSpec((1, ch), lambda i: (0, 0)),
@@ -373,39 +393,14 @@
             pl.BlockSpec((ch, hid), lambda i: (0, 0)),
             pl.BlockSpec((step, ch), lambda i: (i, 0)),
             pl.BlockSpec((step, hid), lambda i: (i, 0)),
+            pl.BlockSpec((step, ch), lambda i: (i, 0)),
             whole,
         ],
-        out_specs=(whole, edge, edge),
+        out_specs=whole,
         compiler_params=params(),
         cost_estimate=cost(4 * rows * cells * ch * hid, 16 * 2**20),
         name="backward",
-    )(latent, left, right, gain, w_in_t, w_out_t, *in_hbm(adv, slope, both))
-
-
-def edges_kernel(left_ref, right_ref, grad_ref, out_ref):
-    block = grad_ref[...]
-    place = lax.broadcasted_iota(jnp.int32, block.shape, 1)
-    at_start = pl.program_id(0) == 0
-    add = 0.5 * jnp.where(at_start, left_ref[...], right_ref[...])
-    hit = place == jnp.where(at_start, 0, block.shape[1] - 1)
-    out_ref[...] = block + jnp.where(hit, add, 0.0)
-
-
-def add_edges(grad, left, right):
-    rows, cells, ch = grad.shape
-    ends = pl.BlockSpec((rows, 8, ch), lambda i: (0, i * (cells // 8 - 1), 0))
-    edge = pl.BlockSpec((rows, 1, ch), lambda i: (0, 0, 0))
-    return pl.pallas_call(
-        edges_kernel,
-        grid=(2,),
-        out_shape=jax.ShapeDtypeStruct(grad.shape, f32),
-        in_specs=[edge, edge, ends],
-        out_specs=ends,
-        input_output_aliases={2: 0},
-        compiler_params=params(),
-        cost_estimate=cost(rows * 16 * ch, 2**20),
-        name="edges",
-    )(left, right, grad)
+    )(left, right, gain, w_in_t, w_out_t, *in_hbm(adv, inv_slope, xhat, both))
 
 
 def total_kernel(got_ref, out_ref):
@@ -494,16 +489,19 @@
     left, right = left.astype(f32), right.astype(f32)
     gain_row = gain.reshape(1, -1)
     w_out_t = w_out.T
-    stk, slope, act_t, xhat_t = forward(latent, left, right, gain_row, w_in, w_out)
-    adv, both, keep, send = decode(core, row_index, got, stk, head, head.T, w_out_t, slope, act_t, xhat_t, groups)
+    w_in_t = w_in.T
+    stk, slope, act_t, xhat_t, xhat, inv_slope, ends = forward(latent, left, right, gain_row, w_in, w_out)
+    adv, both, keep, send, first, last = decode(
+        core, row_index, got, stk, head, head.T, w_out_t, w_in_t, gain_row, ends, slope, act_t, xhat_t, groups
+    )
+    grad_left, grad_right = from_sides(first, last)
     came = lax.ppermute(send, "core", swap)
-    parts = lax.all_to_all(pair(keep, came), chips, 0, 0, tiled=True)
-    grad, first, last = backward(latent, left, right, gain_row, w_in.T, w_out_t, adv, slope, both)
-    parts, first, last = lax.optimization_barrier((parts, first, last))
-    grad_left, grad_right = from_sides(first.astype(bf16), last.astype(bf16))
-    grad = add_edges(grad, grad_left.astype(f32), grad_right.astype(f32))
+    summed, grad_left, grad_right = lax.optimization_barrier((pair(keep, came), grad_left, grad_right))
+    parts = lax.all_to_all(summed, chips, 0, 0, tiled=True)
+    grad_left, grad_right = (x.astype(f32)[:, None, :] for x in (grad_left, grad_right))
+    grad = backward(grad_left, grad_right, gain_row, w_in_t, w_out_t, adv, inv_slope, xhat, both)
+    parts, grad = lax.optimization_barrier((parts, grad))
     mine = lax.all_to_all(total(parts), chips, 0, 0, tiled=True)
-    mine, grad = lax.optimization_barrier((mine, grad))
     other = lax.ppermute(mine, "core", swap)
     grad_in, grad_out, grad_gain, grad_head = finish(core, mine, other, gain, w_in, head, 2 * groups)
     return grad, grad_in, grad_out, grad_gain.reshape(-1), grad_head

time: 107 us -> 106 us (level)
  blocking collectives: 0 us -> 18.7 us
  starting transfers between devices: 34.6 us -> 23.3 us
  waiting for transfers between devices: 29.6 us -> 25.3 us
  Pallas kernels: 39.8 us -> 35.7 us
    all_to_all x0 -> x1, blocking collectives: none -> 18.7 us  [body(): mine = lax.all_to_all(total(parts), chips, 0, 0, tiled=True)]
    all_to_all x2 -> x1, starting transfers between devices: 19.6 us -> 11.5 us  [body(): parts = lax.all_to_all(summed, chips, 0, 0, tiled=True)]
    pallas_call x2 -> x1, Pallas kernels: 12.5 us -> 8.55 us  [backward(): pl.pallas_call(backward_kernel, grid=(rows // ROWS_STEP,), out_shape=jax....]
    ppermute x1, starting transfers between devices: 2.82 us -> 0.01 us  [body(): other = lax.ppermute(mine, 'core', swap)]
    ppermute x1, waiting for transfers between devices: 1.35 us -> 0.01 us  [body(): came = lax.ppermute(send, 'core', swap)]
    ppermute x2, waiting for transfers between devices: 1.15 us -> 0.04 us  [from_sides(): left = lax.ppermute(last, LON, [(i, (i + 1) % count) for i in range(count)])]
    all_to_all x2 -> x1, waiting for transfers between devices: 2.37 us -> 1.53 us  [body(): parts = lax.all_to_all(summed, chips, 0, 0, tiled=True)]
  transfers between devices with their start and end apart: 9 -> 8, of which waited for: 8 -> 5; matrix products, arithmetic and copies ran while one was open for 1% -> 1% of each run, Pallas kernels for 22% -> 20%
where the time goes in v5:
time: 106 us
  Pallas kernels  35.7 us (34%)
  waiting for transfers between devices  25.3 us (24%)
  starting transfers between devices  23.3 us (22%)
  blocking collectives  18.7 us (18%)
  local copies, waits for them, and re-layouts  1.62 us (2%)
    all_to_all x1, waiting for transfers between devices, body(): got = lax.all_to_all(packed, LON, 0, 0, tiled=True)  19 us
    all_to_all x1, blocking collectives, body(): mine = lax.all_to_all(total(parts), chips, 0, 0, tiled=True)  18.7 us
    pallas_call x1, Pallas kernels, decode(): pl.pallas_call(decode_kernel, out_shape=(pltpu.HBM((n, ch), bf16), pltpu....  13.2 us
    all_to_all x1, starting transfers between devices, body(): parts = lax.all_to_all(summed, chips, 0, 0, tiled=True)  11.5 us
    pallas_call x1, Pallas kernels, forward(): pl.pallas_call(forward_kernel, grid=(rows // ROWS_STEP,), out_shape=(pltp...  9.01 us
    pallas_call x1, Pallas kernels, backward(): pl.pallas_call(backward_kernel, grid=(rows // ROWS_STEP,), out_shape=jax....  8.55 us
    all_to_all x1, starting transfers between devices, body(): got = lax.all_to_all(packed, LON, 0, 0, tiled=True)  6.32 us
    ppermute x2, starting transfers between devices, from_sides(): left = lax.ppermute(last, LON, [(i, (i + 1) % count) for i in range(count)])  4.84 us
  transfers between devices with their start and end apart: 8, of which 5 were waited for; matrix products, arithmetic and copies ran while one was open for 1% of the time, Pallas kernels for 20%

profile of v5, /device:TPU:1, one launch (start us, length us, event | category | flops | bytes accessed | tf_op | source)
XLA Modules:
  0.0 105.5 jit_solution(16315891212136688013)
XLA Ops:
  0.6 1.0 fusion
  1.7 2.7 %collective-permute-start = (bf16[32,1,256]{2,1,0:T(2,128)(2,1)S(1)}, bf16[32,1,256]{2,1,0:T(2,128)(2,1)S(1)}, u32[]{:S(2)}, u32[]{:S(2)}) collective-permute-start(bf16[32,1,256]{2,1,0:T(2,128)(2,1)S(1)} %get-tuple-element.56), channel_id=1, source_target_pairs={{0,1},{1,2},{2,3},{3,4},{4,5},{5,6},{6,7},{7,8},{8,9},{9,10},{10,1... | collective-permute-start | bytes 49160 | tf_op jit(solution)/shard_map/ppermute | solution.py:474
  4.3 0.0 collective-permute-start.1
  4.3 2.7 %pack.1 = bf16[32,264,128]{2,1,0:T(8,128)(2,1)} custom-call(bf16[32,128,128]{2,1,0:T(8,128)(2,1)} %w_hbm.1, bf16[32,128,128]{2,1,0:T(8,128)(2,1)} %t_hbm.1, s32[32,128]{1,0:T(8,128)} %slot_hbm.1, s32[32]{0:T(128)} %count_hbm.1), custom_call_target="tpu_custom_call" | custom-call | flops 1 | bytes 4194304 | tf_op jit(solution)/shard_map/pack/pallas_call | solution.py:88
  7.0 0.0 copy-start.1
  7.0 0.0 copy-start
  7.0 0.0 copy-start.2
  7.1 0.0 copy-start.3
  7.1 0.0 copy-start.4
  7.1 0.0 collective-permute-done
  7.1 0.9 collective-permute-done.1
  8.0 6.3 %all-to-all-start = ((bf16[32,264,128]{2,1,0:T(8,128)(2,1)}), bf16[32,264,128]{2,1,0:T(8,128)(2,1)}, u32[]{:S(2)}, u32[]{:S(2)}) async-start(bf16[32,264,128]{2,1,0:T(8,128)(2,1)} %pack.1), calls=%async_computation | async-start | bytes 4325376 | tf_op jit(solution)/shard_map/all_to_all | solution.py:488
  14.3 0.0 copy-done.1
  14.3 0.1 copy.19
  14.4 0.0 copy-done
  14.4 0.1 copy.20
  14.6 0.0 copy-done.2
  14.6 0.1 copy.18
  14.8 0.0 copy-done.3
  14.8 0.0 copy-done.4
  14.8 0.0 copy-start.5
  14.8 9.0 %forward.1 = (bf16[32,256,256]{2,1,0:T(8,128)(2,1)}, bf16[4096,512]{1,0:T(8,128)(2,1)}, bf16[512,4096]{1,0:T(8,128)(2,1)}, bf16[256,4096]{1,0:T(8,128)(2,1)}, bf...) custom-call(bf16[32,128,256]{2,1,0:T(8,128)(2,1)S(1)} %copy-done.4, ...), custom_call_target="tpu_custom_call" | custom-call | flops 2147483648 | bytes 16777216 | tf_op jit(solution)/shard_map/forward/pallas_call | solution.py:154
  23.8 19.0 %all-to-all-done.got_hbm = bf16[32,264,128]{2,1,0:T(8,128)(2,1)} async-done(((bf16[32,264,128]{2,1,0:T(8,128)(2,1)}), bf16[32,264,128]{2,1,0:T(8,128)(2,1)}, u32[]{:S(2)}, u32[]{:S(2)}) %all-to-all-start) | async-done | bytes 2162720 | tf_op jit(solution)/shard_map/all_to_all | solution.py:488
  42.8 0.0 copy-done.5
  42.8 13.2 %decode.1 = (bf16[4096,256]{1,0:T(8,128)(2,1)}, bf16[32,128,256]{2,1,0:T(8,128)(2,1)}, f32[64,24,128]{2,1,0:T(8,128)S(1)}, bf16[64,24,128]{2,1,0:T(8,128)(2,1)S(...) custom-call(s32[1]{0:T(128)} %bitcast.core_ref, s32[1,1,32]{2,1,0:T(1,128)S(1)} %copy-done.5, ...), custom_call_target="tpu_custom_call" | custom-call | flops 5368709120 | bytes 25165824 | tf_op jit(solution)/shard_map/decode/pallas_call | solution.py:336
  56.0 0.7 collective-permute-start.2
  56.7 2.2 %collective-permute-start.3 = (bf16[32,256]{1,0:T(8,128)(2,1)S(1)}, bf16[32,256]{1,0:T(8,128)(2,1)S(1)}, u32[]{:S(2)}, u32[]{:S(2)}) collective-permute-start(bf16[32,256]{1,0:T(8,128)(2,1)S(1)} %get-tuple-element.40), channel_id=1, source_target_pairs={{0,1},{1,2},{2,3},{3,4},{4,5},{5,6},{6,7},{7,8},{8,9},{9,10},{10,1... | collective-permute-start | bytes 49160 | tf_op jit(solution)/shard_map/ppermute | solution.py:474
  58.9 0.0 collective-permute-start.4
  58.9 0.0 collective-permute-done.2.came_ref
  58.9 0.8 pair.1
  59.7 0.0 collective-permute-done.3
  59.7 2.3 %collective-permute-done.4 = bf16[32,256]{1,0:T(8,128)(2,1)S(1)} collective-permute-done((bf16[32,256]{1,0:T(8,128)(2,1)S(1)}, bf16[32,256]{1,0:T(8,128)(2,1)S(1)}, u32[]{:S(2)}, u32[]{:S(2)}) %collective-permute-start.4) | collective-permute-done | bytes 16416 | tf_op jit(solution)/shard_map/ppermute | solution.py:475
  62.0 11.5 %all-to-all-start.1 = ((bf16[64,24,128]{2,1,0:T(8,128)(2,1)}), bf16[64,24,128]{2,1,0:T(8,128)(2,1)S(1)}, u32[]{:S(2)}, u32[]{:S(2)}) async-start(bf16[64,24,128]{2,1,0:T(8,128)(2,1)} %pair.1), calls=%async_computation.1 | async-start | bytes 786432 | tf_op jit(solution)/shard_map/all_to_all | solution.py:500
  73.6 8.5 %backward.1 = f32[32,128,256]{2,1,0:T(8,128)} custom-call(f32[32,1,256]{2,1,0:T(1,128)S(1)} %reshape.26.left_ref, f32[32,1,256]{2,1,0:T(1,128)S(1)} %reshape.27.right_ref, f32[1,256]{1,0:T(1,128)S(1)} %bitcast.14, bf16[512,256]{1,0:T(8,128)(2,1)S(1)} %bitcast.10, bf16[256,512]{1,0:T(8,128)(2,1)S(1)} %bitcast.8, bf16[4096,256]{1,0:T(8,128)(2,1)} %get-tuple-element.45.adv_ref, ...), custom_call_target="tpu_custom_call" | custom-call | flops 2147483648 | bytes 16777216 | tf_op jit(solution)/shard_map/backward/pallas_call | solution.py:384
  82.2 1.5 %all-to-all-done.1.got_ref = bf16[64,24,128]{2,1,0:T(8,128)(2,1)S(1)} async-done(((bf16[64,24,128]{2,1,0:T(8,128)(2,1)}), bf16[64,24,128]{2,1,0:T(8,128)(2,1)S(1)}, u32[]{:S(2)}, u32[]{:S(2)}) %all-to-all-start.1) | async-done | bytes 393248 | tf_op jit(solution)/shard_map/all_to_all | solution.py:500
  83.7 0.1 total.1
  83.8 18.7 %all_to_all.15.mine_ref = bf16[64,24,128]{2,1,0:T(8,128)(2,1)S(1)} all-to-all(bf16[64,24,128]{2,1,0:T(8,128)(2,1)S(1)} %total.1), channel_id=1, replica_groups=mesh['band'=8,'chip'=8,'core'=2] {'band','chip'}, dimensions={0} | all-to-all | bytes 786432 | tf_op jit(solution)/shard_map/all_to_all | solution.py:504
  102.5 0.0 collective-permute-start.5
  102.5 0.1 copy.21.gain_ref
  102.7 1.6 %collective-permute-done.5.other_ref = bf16[64,24,128]{2,1,0:T(8,128)(2,1)S(1)} collective-permute-done((bf16[64,24,128]{2,1,0:T(8,128)(2,1)S(1)}, bf16[64,24,128]{2,1,0:T(8,128)(2,1)S(1)}, u32[]{:S(2)}, u32[]{:S(2)}) %collective-permute-start.5) | collective-permute-done | bytes 393248 | tf_op jit(solution)/shard_map/ppermute | solution.py:505
  104.2 1.3 %finish.1 = (f32[256,512]{1,0:T(8,128)}, f32[512,256]{1,0:T(8,128)}, f32[1,256]{1,0:T(1,128)}, f32[256,128]{1,0:T(8,128)}) custom-call(s32[1]{0:T(128)} %bitcast.core_ref, bf16[64,24,128]{2,1,0:T(8,128)(2,1)S(1)} %all_to_all.15.mine_ref, bf16[64,24,128]{2,1,0:T(8,128)(2,1)S(1)} %collective-permute-done.5.other_ref, f32[256,1]{1,0:T(8,128)S(1)} %copy.21.gain_ref, ...), custom_call_target="tpu_custom_call" | custom-call | flops 524288 | bytes 3145728 | tf_op jit(solution)/shard_map/finish/pallas_call | solution.py:453
  (4 shorter events, 0.1 us)
Async XLA Ops:
  1.7 5.4 %collective-permute-start = (bf16[32,1,256]{2,1,0:T(2,128)(2,1)S(1)}, bf16[32,1,256]{2,1,0:T(2,128)(2,1)S(1)}, u32[]{:S(2)}, u32[]{:S(2)}) collective-permute-start(bf16[32,1,256]{2,1,0:T(2,128)(2,1)S(1)} %get-tuple-element.56), channel_id=1, source_target_pairs={{0,1},{1,2},{2,3},{3,4},{4,5},{5,6},{6,7},{7,8},{8,9},{9,10},{10,1... | collective-permute-start | bytes 49160 | tf_op jit(solution)/shard_map/ppermute | solution.py:474
  4.3 3.6 %collective-permute-start.1 = (bf16[32,1,256]{2,1,0:T(2,128)(2,1)S(1)}, bf16[32,1,256]{2,1,0:T(2,128)(2,1)S(1)}, u32[]{:S(2)}, u32[]{:S(2)}) collective-permute-start(bf16[32,1,256]{2,1,0:T(2,128)(2,1)S(1)} %get-tuple-element.55), channel_id=1, source_target_pairs={{1,0},{2,1},{3,2},{4,3},{5,4},{6,5},{7,6},{8,7},{9,8},{10,9},{11,1... | collective-permute-start | bytes 49160 | tf_op jit(solution)/shard_map/ppermute | solution.py:475
  7.0 7.3 %copy-start.1 = (bf16[512,256]{1,0:T(8,128)(2,1)S(1)}, bf16[512,256]{1,0:T(8,128)(2,1)}, u32[]{:S(2)}) copy-start(bf16[512,256]{1,0:T(8,128)(2,1)} %w_out_ref.1) | copy-start | bytes 786436
  7.0 7.4 %copy-start = (bf16[256,512]{1,0:T(8,128)(2,1)S(1)}, bf16[256,512]{1,0:T(8,128)(2,1)}, u32[]{:S(2)}) copy-start(bf16[256,512]{1,0:T(8,128)(2,1)} %w_in_ref.3) | copy-start | bytes 786436
  7.0 7.5 %copy-start.2 = (bf16[256,128]{1,0:T(8,128)(2,1)S(1)}, bf16[256,128]{1,0:T(8,128)(2,1)}, u32[]{:S(2)}) copy-start(bf16[256,128]{1,0:T(8,128)(2,1)} %head_ref.1) | copy-start | bytes 196612
  7.1 7.7 %copy-start.3 = (f32[256]{0:T(256)S(1)}, f32[256]{0:T(256)}, u32[]{:S(2)}) copy-start(f32[256]{0:T(256)} %param.16) | copy-start | bytes 3076
  7.1 7.7 %copy-start.4 = (bf16[32,128,256]{2,1,0:T(8,128)(2,1)S(1)}, bf16[32,128,256]{2,1,0:T(8,128)(2,1)}, u32[]{:S(2)}) copy-start(bf16[32,128,256]{2,1,0:T(8,128)(2,1)} %lat_ref.1) | copy-start | bytes 6291460
  8.0 34.8 %all-to-all-start = ((bf16[32,264,128]{2,1,0:T(8,128)(2,1)}), bf16[32,264,128]{2,1,0:T(8,128)(2,1)}, u32[]{:S(2)}, u32[]{:S(2)}) async-start(bf16[32,264,128]{2,1,0:T(8,128)(2,1)} %pack.1), calls=%async_computation | async-start | bytes 4325376 | tf_op jit(solution)/shard_map/all_to_all | solution.py:488
  14.8 28.0 %copy-start.5 = (s32[1,1,32]{2,1,0:T(1,128)S(1)}, s32[1,1,32]{2,1,0:T(1,128)}, u32[]{:S(2)}) copy-start(s32[1,1,32]{2,1,0:T(1,128)} %rows_ref.1) | copy-start | bytes 388
  56.0 2.8 %collective-permute-start.2 = (bf16[64,24,128]{2,1,0:T(8,128)(2,1)S(1)}, bf16[64,24,128]{2,1,0:T(8,128)(2,1)S(1)}, u32[]{:S(2)}, u32[]{:S(2)}) collective-permute-start(bf16[64,24,128]{2,1,0:T(8,128)(2,1)S(1)} %get-tuple-element.39), channel_id=1, source_target_pairs={{0,1},{1,0},{2,3},{3,2},{4,5},{5,4},{6,7},{7,6},{8,9},{9,8},{10,11... | collective-permute-start | bytes 1179656 | tf_op jit(solution)/shard_map/ppermute | solution.py:498
  56.7 3.0 %collective-permute-start.3 = (bf16[32,256]{1,0:T(8,128)(2,1)S(1)}, bf16[32,256]{1,0:T(8,128)(2,1)S(1)}, u32[]{:S(2)}, u32[]{:S(2)}) collective-permute-start(bf16[32,256]{1,0:T(8,128)(2,1)S(1)} %get-tuple-element.40), channel_id=1, source_target_pairs={{0,1},{1,2},{2,3},{3,4},{4,5},{5,6},{6,7},{7,8},{8,9},{9,10},{10,1... | collective-permute-start | bytes 49160 | tf_op jit(solution)/shard_map/ppermute | solution.py:474
  58.9 3.2 %collective-permute-start.4 = (bf16[32,256]{1,0:T(8,128)(2,1)S(1)}, bf16[32,256]{1,0:T(8,128)(2,1)S(1)}, u32[]{:S(2)}, u32[]{:S(2)}) collective-permute-start(bf16[32,256]{1,0:T(8,128)(2,1)S(1)} %get-tuple-element.41), channel_id=1, source_target_pairs={{1,0},{2,1},{3,2},{4,3},{5,4},{6,5},{7,6},{8,7},{9,8},{10,9},{11,1... | collective-permute-start | bytes 49160 | tf_op jit(solution)/shard_map/ppermute | solution.py:475
  62.0 21.7 %all-to-all-start.1 = ((bf16[64,24,128]{2,1,0:T(8,128)(2,1)}), bf16[64,24,128]{2,1,0:T(8,128)(2,1)S(1)}, u32[]{:S(2)}, u32[]{:S(2)}) async-start(bf16[64,24,128]{2,1,0:T(8,128)(2,1)} %pair.1), calls=%async_computation.1 | async-start | bytes 786432 | tf_op jit(solution)/shard_map/all_to_all | solution.py:500
  102.5 1.7 %collective-permute-start.5 = (bf16[64,24,128]{2,1,0:T(8,128)(2,1)S(1)}, bf16[64,24,128]{2,1,0:T(8,128)(2,1)S(1)}, u32[]{:S(2)}, u32[]{:S(2)}) collective-permute-start(bf16[64,24,128]{2,1,0:T(8,128)(2,1)S(1)} %all_to_all.15.mine_ref), channel_id=1, source_target_pairs={{0,1},{1,0},{2,3},{3,2},{4,5},{5,4},{6,7},{7,6},{8,9},{9,8},{10,11... | collective-permute-start | bytes 1179656 | tf_op jit(solution)/shard_map/ppermute | solution.py:505

commit v6 on v5

--- a/solution.py
+++ b/solution.py
@@ -14,6 +14,7 @@
 BLOCKS_STEP = 8
 PULL_ROWS = 16
 PACK_CHUNKS = 4
+BACK_ROWS = 8
 META = 8
 
 f32 = jnp.float32
@@ -189,7 +190,7 @@
 def decode_kernel(
     core_ref, rows_ref, got_hbm, stk_hbm, head_ref, head_t_ref, w_out_t_ref, w_in_t_ref, gain_ref, ends_ref,
     slope_hbm, act_t_hbm, xhat_t_hbm,
-    adv_hbm, both_hbm, keep_ref, send_ref, first_ref, last_ref,
+    adv_hbm, both_hbm, keep_ref, send_ref, outer_ref,
     got, stk, slope, act_t, xhat_t, adv_all, both_all, ends, acc_both, acc_new, acc_head, acc_in, acc_out,
     got_sems, stk_sems, in_sems, out_sems,
 ):
@@ -282,16 +283,19 @@
         return carry
 
     lax.fori_loop(0, rows // nr, pull, 0)
-    for k, ref in enumerate((first_ref, last_ref)):
+    edges = []
+    for k in range(2):
         gained = dot(ends[k].astype(bf16), w_in_t_ref[...]) * gain_ref[...]
         xhat, inv = ends_ref[2 * k], ends_ref[2 * k + 1]
-        ref[...] = (inv * (gained - xhat * jnp.mean(gained * xhat, axis=-1, keepdims=True))).astype(bf16)
+        edges.append(inv * (gained - xhat * jnp.mean(gained * xhat, axis=-1, keepdims=True)))
     for core in range(2):
 
         @pl.when(core_ref[0] == core)
         def _(core=core):
             put_chunks(keep_ref, core, acc_in, acc_out, acc_head)
             put_chunks(send_ref, 1 - core, acc_in, acc_out, acc_head)
+            outer_ref[...] = edges[core].astype(bf16)
+            put_edge(send_ref, edges[1 - core])
 
     both_copy.wait()
     for k in range(rows // nr):
@@ -311,6 +315,16 @@
             ref[down * across :, 8 * p : 8 * p + 8, :] = jnp.zeros((rest, 8, 128), ref.dtype)
 
 
+def edge_tiles(shape):
+    first = 16
+    return [(first + k, 8 * (k % (shape[0] // 8)), 128 * (k // (shape[0] // 8))) for k in range(shape[0] * shape[1] // 1024)]
+
+
+def put_edge(ref, edge):
+    for chunk, row, lane in edge_tiles(edge.shape):
+        ref[chunk, 16:24, :] = edge[row : row + 8, lane : lane + 128].astype(ref.dtype)
+
+
 def take_chunks(halves, part, shape):
     down = shape[0] // 8
     across = shape[1] // 256
@@ -341,10 +355,9 @@
             jax.ShapeDtypeStruct((chunks, 24, 128), f32),
             jax.ShapeDtypeStruct((chunks, 24, 128), bf16),
             jax.ShapeDtypeStruct((nrow, ch), bf16),
-            jax.ShapeDtypeStruct((nrow, ch), bf16),
         ),
         in_specs=[scalars] * 2 + [OUTSIDE] * 2 + [INSIDE] * 6 + [OUTSIDE] * 3,
-        out_specs=(OUTSIDE, OUTSIDE) + (INSIDE,) * 4,
+        out_specs=(OUTSIDE, OUTSIDE) + (INSIDE,) * 3,
         scratch_shapes=[pltpu.VMEM(x.shape, bf16) for x in (got, stk, slope, act_t, xhat_t)]
         + [
             pltpu.VMEM((n, ch), bf16),
@@ -366,7 +379,10 @@
     )(core, rows, *in_hbm(got, stk), head, head_t, w_out_t, w_in_t, gain, ends, *in_hbm(slope, act_t, xhat_t))
 
 
-def backward_kernel(left_ref, right_ref, gain_ref, w_in_t_ref, w_out_t_ref, adv_ref, slope_ref, xhat_ref, both_ref, out_ref):
+def backward_kernel(
+    left_ref, right_ref, gain_ref, w_in_t_ref, w_out_t_ref, adv_ref, slope_ref, xhat_ref, both_ref, *rest
+):
+    out_ref = rest[-1]
     rows, cells, ch = out_ref.shape
     pre_grad = (dot(adv_ref[...], w_out_t_ref[...]) * slope_ref[...].astype(f32)).astype(bf16)
     gained = dot(pre_grad, w_in_t_ref[...]) * gain_ref[...]
@@ -375,32 +391,37 @@
     out_ref[...] = both_ref[...].astype(f32) + mixed(summed_grad.reshape(rows, cells, ch), left_ref[...], right_ref[...])
 
 
-def backward(left, right, gain, w_in_t, w_out_t, adv, inv_slope, xhat, both):
+def backward(left, right, gain, w_in_t, w_out_t, adv, inv_slope, xhat, both, begin, end, *before):
     rows, cells, ch = both.shape
     hid = w_in_t.shape[0]
-    step = ROWS_STEP * cells
-    edge = pl.BlockSpec((ROWS_STEP, 1, ch), lambda i: (i, 0, 0))
-    whole = pl.BlockSpec((ROWS_STEP, cells, ch), lambda i: (i, 0, 0))
+    nr = BACK_ROWS
+    step = nr * cells
+    base = begin // nr
+    edge = pl.BlockSpec((nr, 1, ch), lambda i: (i + base, 0, 0))
+    whole = pl.BlockSpec((nr, cells, ch), lambda i: (i + base, 0, 0))
+    share = (end - begin) * cells
     return pl.pallas_call(
         backward_kernel,
-        grid=(rows // ROWS_STEP,),
-        out_shape=jax.ShapeDtypeStruct((rows, cells, ch), f32),
+        grid=((end - begin) // nr,),
+        out_shape=pltpu.HBM((rows, cells, ch), f32),
         in_specs=[
             edge,
             edge,
             pl.BlockSpec((1, ch), lambda i: (0, 0)),
             pl.BlockSpec((hid, ch), lambda i: (0, 0)),
             pl.BlockSpec((ch, hid), lambda i: (0, 0)),
-            pl.BlockSpec((step, ch), lambda i: (i, 0)),
-            pl.BlockSpec((step, hid), lambda i: (i, 0)),
-            pl.BlockSpec((step, ch), lambda i: (i, 0)),
+            pl.BlockSpec((step, ch), lambda i: (i + base, 0)),
+            pl.BlockSpec((step, hid), lambda i: (i + base, 0)),
+            pl.BlockSpec((step, ch), lambda i: (i + base, 0)),
             whole,
-        ],
+        ]
+        + [OUTSIDE] * len(before),
         out_specs=whole,
-        compiler_params=params(),
-        cost_estimate=cost(4 * rows * cells * ch * hid, 16 * 2**20),
+        input_output_aliases={9: 0} if before else {},
+        compiler_params=params(),
+        cost_estimate=cost(4 * share * ch * hid, 3584 * share),
         name="backward",
-    )(left, right, gain, w_in_t, w_out_t, *in_hbm(adv, inv_slope, xhat, both))
+    )(left, right, gain, w_in_t, w_out_t, *in_hbm(adv, inv_slope, xhat, both, *before))
 
 
 def total_kernel(got_ref, out_ref):
@@ -418,14 +439,16 @@
     )(got)
 
 
-def pair_kernel(keep_ref, came_ref, out_ref):
+def pair_kernel(keep_ref, came_ref, out_ref, edge_ref):
     out_ref[...] = (keep_ref[...] + came_ref[...].astype(f32)).astype(bf16)
-
-
-def pair(keep, came):
+    for chunk, row, lane in edge_tiles(edge_ref.shape):
+        edge_ref[row : row + 8, lane : lane + 128] = came_ref[chunk, 16:24, :].astype(f32)
+
+
+def pair(keep, came, edge):
     return pl.pallas_call(
         pair_kernel,
-        out_shape=jax.ShapeDtypeStruct(keep.shape, bf16),
+        out_shape=(jax.ShapeDtypeStruct(keep.shape, bf16), jax.ShapeDtypeStruct(edge.shape, f32)),
         compiler_params=params(),
         cost_estimate=cost(keep.size, 8 * keep.size),
         name="pair",
@@ -491,17 +514,24 @@
     w_out_t = w_out.T
     w_in_t = w_in.T
     stk, slope, act_t, xhat_t, xhat, inv_slope, ends = forward(latent, left, right, gain_row, w_in, w_out)
-    adv, both, keep, send, first, last = decode(
+    adv, both, keep, send, outer = decode(
         core, row_index, got, stk, head, head.T, w_out_t, w_in_t, gain_row, ends, slope, act_t, xhat_t, groups
     )
-    grad_left, grad_right = from_sides(first, last)
-    came = lax.ppermute(send, "core", swap)
-    summed, grad_left, grad_right = lax.optimization_barrier((pair(keep, came), grad_left, grad_right))
+    lons = 2 * lax.axis_size("chip")
+    outer = lax.ppermute(outer, LON, [(i, (i + (1 if i % 2 else -1)) % lons) for i in range(lons)])
+    summed, inner = pair(keep, lax.ppermute(send, "core", swap), outer)
+    summed, outer, inner = lax.optimization_barrier((summed, outer, inner))
     parts = lax.all_to_all(summed, chips, 0, 0, tiled=True)
-    grad_left, grad_right = (x.astype(f32)[:, None, :] for x in (grad_left, grad_right))
-    grad = backward(grad_left, grad_right, gain_row, w_in_t, w_out_t, adv, inv_slope, xhat, both)
+    outer = outer.astype(f32)
+    grad_left = jnp.where(core == 0, outer, inner)[:, None, :]
+    grad_right = jnp.where(core == 0, inner, outer)[:, None, :]
+    rest = (grad_left, grad_right, gain_row, w_in_t, w_out_t, adv, inv_slope, xhat, both)
+    rows = latent.shape[0]
+    grad = backward(*rest, 0, rows // 2)
     parts, grad = lax.optimization_barrier((parts, grad))
     mine = lax.all_to_all(total(parts), chips, 0, 0, tiled=True)
+    grad = backward(*rest, rows // 2, rows, grad)
+    mine, grad = lax.optimization_barrier((mine, grad))
     other = lax.ppermute(mine, "core", swap)
     grad_in, grad_out, grad_gain, grad_head = finish(core, mine, other, gain, w_in, head, 2 * groups)
     return grad, grad_in, grad_out, grad_gain.reshape(-1), grad_head

time: 106 us -> 104 us (0.981)
  blocking collectives: 18.7 us -> 0 us
  waiting for transfers between devices: 25.3 us -> 33.9 us
  starting transfers between devices: 23.3 us -> 28.8 us
  Pallas kernels: 35.7 us -> 38.2 us
    all_to_all x1 -> x0, blocking collectives: 18.7 us -> none  [body(): mine = lax.all_to_all(total(parts), chips, 0, 0, tiled=True)]
    all_to_all x0 -> x1, waiting for transfers between devices: none -> 5.4 us  [body(): mine = lax.all_to_all(total(parts), chips, 0, 0, tiled=True)]
    all_to_all x1, waiting for transfers between devices: 1.53 us -> 6.5 us  [body(): parts = lax.all_to_all(summed, chips, 0, 0, tiled=True)]
    all_to_all x0 -> x1, starting transfers between devices: none -> 4.63 us  [body(): mine = lax.all_to_all(total(parts), chips, 0, 0, tiled=True)]
    ppermute x1, starting transfers between devices: 0.01 us -> 2.45 us  [body(): other = lax.ppermute(mine, 'core', swap)]
    ppermute x1 -> x2, starting transfers between devices: 0.66 us -> 2.99 us  [the longest x1 2.32 us: body(): lax.ppermute(outer, LON, [(i, (i + (1 if i % 2 else -1)) % lons) for i in...]
    ppermute x2 -> x1, waiting for transfers between devices: 3.17 us -> 0.87 us  [from_sides(): lax.ppermute(first, LON, [((i + 1) % count, i) for i in range(count)])]
    ppermute x2 -> x1, starting transfers between devices: 4.84 us -> 2.67 us  [from_sides(): left = lax.ppermute(last, LON, [(i, (i + 1) % count) for i in range(count)])]
  transfers between devices with their start and end apart: 8 -> 8, of which waited for: 5 -> 6; matrix products, arithmetic and copies ran while one was open for 1% -> 1% of each run, Pallas kernels for 20% -> 22%
where the time goes in v6:
time: 104 us; the launch traced here: 103 us
  Pallas kernels  38.2 us (37%)
  waiting for transfers between devices  33.9 us (33%)
  starting transfers between devices  28.8 us (28%)
  local copies, waits for them, and re-layouts  1.64 us (2%)
    all_to_all x1, waiting for transfers between devices, body(): got = lax.all_to_all(packed, LON, 0, 0, tiled=True)  19 us
    pallas_call x1, Pallas kernels, decode(): pl.pallas_call(decode_kernel, out_shape=(pltpu.HBM((n, ch), bf16), pltpu....  13.4 us
    pallas_call x2, Pallas kernels, backward(): pl.pallas_call(backward_kernel, grid=((end - begin) // nr,), out_shape=pl...  10.2 us
    all_to_all x1, starting transfers between devices, body(): parts = lax.all_to_all(summed, chips, 0, 0, tiled=True)  9.79 us
    pallas_call x1, Pallas kernels, forward(): pl.pallas_call(forward_kernel, grid=(rows // ROWS_STEP,), out_shape=(pltp...  9 us
    all_to_all x1, waiting for transfers between devices, body(): parts = lax.all_to_all(summed, chips, 0, 0, tiled=True)  6.5 us
    all_to_all x1, starting transfers between devices, body(): got = lax.all_to_all(packed, LON, 0, 0, tiled=True)  6.32 us
    all_to_all x1, waiting for transfers between devices, body(): mine = lax.all_to_all(total(parts), chips, 0, 0, tiled=True)  5.4 us
  transfers between devices with their start and end apart: 8, of which 6 were waited for; matrix products, arithmetic and copies ran while one was open for 1% of the time, Pallas kernels for 22%

profile of v6, /device:TPU:1, one launch (start us, length us, event | category | flops | bytes accessed | tf_op | source)
XLA Modules:
  0.0 103.5 jit_solution(9554576118285096382)
XLA Ops:
  0.6 1.0 fusion.1
  1.7 2.7 %collective-permute-start = (bf16[32,1,256]{2,1,0:T(2,128)(2,1)S(1)}, bf16[32,1,256]{2,1,0:T(2,128)(2,1)S(1)}, u32[]{:S(2)}, u32[]{:S(2)}) collective-permute-start(bf16[32,1,256]{2,1,0:T(2,128)(2,1)S(1)} %get-tuple-element.62), channel_id=1, source_target_pairs={{0,1},{1,2},{2,3},{3,4},{4,5},{5,6},{6,7},{7,8},{8,9},{9,10},{10,1... | collective-permute-start | bytes 49160 | tf_op jit(solution)/shard_map/ppermute | solution.py:497
  4.3 0.0 collective-permute-start.1
  4.3 2.7 %pack.1 = bf16[32,264,128]{2,1,0:T(8,128)(2,1)} custom-call(bf16[32,128,128]{2,1,0:T(8,128)(2,1)} %w_hbm.1, bf16[32,128,128]{2,1,0:T(8,128)(2,1)} %t_hbm.1, s32[32,128]{1,0:T(8,128)} %slot_hbm.1, s32[32]{0:T(128)} %count_hbm.1), custom_call_target="tpu_custom_call" | custom-call | flops 1 | bytes 4194304 | tf_op jit(solution)/shard_map/pack/pallas_call | solution.py:89
  7.0 0.0 copy-start.1
  7.0 0.0 copy-start
  7.0 0.0 copy-start.2
  7.1 0.0 copy-start.3
  7.1 0.0 copy-start.4
  7.1 0.0 collective-permute-done
  7.1 0.9 collective-permute-done.1
  8.0 6.3 %all-to-all-start = ((bf16[32,264,128]{2,1,0:T(8,128)(2,1)}), bf16[32,264,128]{2,1,0:T(8,128)(2,1)}, u32[]{:S(2)}, u32[]{:S(2)}) async-start(bf16[32,264,128]{2,1,0:T(8,128)(2,1)} %pack.1), calls=%async_computation | async-start | bytes 4325376 | tf_op jit(solution)/shard_map/all_to_all | solution.py:511
  14.3 0.0 copy-done.1
  14.3 0.1 copy.22
  14.4 0.0 copy-done
  14.4 0.1 copy.23
  14.6 0.0 copy-done.2
  14.6 0.1 copy.21
  14.8 0.0 copy-done.3
  14.8 0.0 copy-done.4
  14.8 0.0 copy-start.5
  14.8 9.0 %forward.1 = (bf16[32,256,256]{2,1,0:T(8,128)(2,1)}, bf16[4096,512]{1,0:T(8,128)(2,1)}, bf16[512,4096]{1,0:T(8,128)(2,1)}, bf16[256,4096]{1,0:T(8,128)(2,1)}, bf...) custom-call(bf16[32,128,256]{2,1,0:T(8,128)(2,1)S(1)} %copy-done.4, ...), custom_call_target="tpu_custom_call" | custom-call | flops 2147483648 | bytes 16777216 | tf_op jit(solution)/shard_map/forward/pallas_call | solution.py:155
  23.8 19.0 %all-to-all-done.got_hbm = bf16[32,264,128]{2,1,0:T(8,128)(2,1)} async-done(((bf16[32,264,128]{2,1,0:T(8,128)(2,1)}), bf16[32,264,128]{2,1,0:T(8,128)(2,1)}, u32[]{:S(2)}, u32[]{:S(2)}) %all-to-all-start) | async-done | bytes 2162720 | tf_op jit(solution)/shard_map/all_to_all | solution.py:511
  42.8 0.0 copy-done.5
  42.8 13.4 %decode.1 = (bf16[4096,256]{1,0:T(8,128)(2,1)}, bf16[32,128,256]{2,1,0:T(8,128)(2,1)}, f32[64,24,128]{2,1,0:T(8,128)S(1)}, bf16[64,24,128]{2,1,0:T(8,128)(2,1)S(1)}, bf16[32,256]{1,0:T(8,128)(2,1)S(1)}) custom-call(s32[1]{0:T(128)} %bitcast.core_ref, s32[1,1,32]{2,1,0:T(1,128)S(1)} %copy-done.5, bf16[32,264,128]{2,1,0:T(8,128)(2,1)} %all-to-all-done.got_hbm, ...), custom_call_target="tpu_custom_call" | custom-call | flops 5368709120 | bytes 25165824 | tf_op jit(solution)/shard_map/decode/pallas_call | solution.py:350
  56.2 0.7 collective-permute-start.2
  56.9 2.3 %collective-permute-start.3 = (bf16[32,256]{1,0:T(8,128)(2,1)S(1)}, bf16[32,256]{1,0:T(8,128)(2,1)S(1)}, u32[]{:S(2)}, u32[]{:S(2)}) collective-permute-start(bf16[32,256]{1,0:T(8,128)(2,1)S(1)} %get-tuple-element.44), channel_id=1, source_target_pairs={{0,15},{1,2},{2,1},{3,4},{4,3},{5,6},{6,5},{7,8},{8,7},{9,10},{10,... | collective-permute-start | bytes 49160 | tf_op jit(solution)/shard_map/ppermute | solution.py:521
  59.2 0.0 collective-permute-done.2.came_ref
  59.2 0.8 pair.1
  60.0 0.9 collective-permute-done.3
  60.9 9.8 %all-to-all-start.1 = ((bf16[64,24,128]{2,1,0:T(8,128)(2,1)}), bf16[64,24,128]{2,1,0:T(8,128)(2,1)S(1)}, u32[]{:S(2)}, u32[]{:S(2)}) async-start(bf16[64,24,128]{2,1,0:T(8,128)(2,1)} %get-tuple-element.46), calls=%async_computation.1 | async-start | bytes 786432 | tf_op jit(solution)/shard_map/all_to_all | solution.py:524
  70.8 5.1 %backward.2.rest_0_ = f32[32,128,256]{2,1,0:T(8,128)} custom-call(f32[32,1,256]{2,1,0:T(1,128)S(1)} %copy.24.left_ref, f32[32,1,256]{2,1,0:T(1,128)S(1)} %broadcast_in_dim.19.right_ref, f32[1,256]{1,0:T(1,128)S(1)} %bitcast.19, bf16[512,256]{1,0:T(8,128)(2,1)S(1)} %bitcast.14, bf16[256,512]{1,0:T(8,128)(2,1)S(1)} %bitcast.11, ...), custom_call_target="tpu_custom_call" | custom-call | flops 1073741824 | bytes 7340032 | tf_op jit(solution)/shard_map/backward/pallas_call | solution.py:403
  75.9 6.5 %all-to-all-done.1.got_ref = bf16[64,24,128]{2,1,0:T(8,128)(2,1)S(1)} async-done(((bf16[64,24,128]{2,1,0:T(8,128)(2,1)}), bf16[64,24,128]{2,1,0:T(8,128)(2,1)S(1)}, u32[]{:S(2)}, u32[]{:S(2)}) %all-to-all-start.1) | async-done | bytes 393248 | tf_op jit(solution)/shard_map/all_to_all | solution.py:524
  82.4 0.8 total.1
  83.2 4.6 %all-to-all-start.2 = ((bf16[64,24,128]{2,1,0:T(8,128)(2,1)}), bf16[64,24,128]{2,1,0:T(8,128)(2,1)S(1)}, u32[]{:S(2)}, u32[]{:S(2)}) async-start(bf16[64,24,128]{2,1,0:T(8,128)(2,1)} %total.1), calls=%async_computation.2 | async-start | bytes 786432 | tf_op jit(solution)/shard_map/all_to_all | solution.py:532
  87.9 5.1 %backward.3 = f32[32,128,256]{2,1,0:T(8,128)} custom-call(f32[32,1,256]{2,1,0:T(1,128)S(1)} %copy.24.left_ref, f32[32,1,256]{2,1,0:T(1,128)S(1)} %broadcast_in_dim.19.right_ref, f32[1,256]{1,0:T(1,128)S(1)} %bitcast.20, bf16[512,256]{1,0:T(8,128)(2,1)S(1)} %bitcast.15, bf16[256,512]{1,0:T(8,128)(2,1)S(1)} %bitcast.12, ...), custom_call_target="tpu_custom_call", output_to_operand_aliasing={{}: (9, {})} | custom-call | flops 1073741824 | bytes 7340032 | tf_op jit(solution)/shard_map/backward/pallas_call | solution.py:403
  92.9 5.4 %all-to-all-done.2.mine_ref = bf16[64,24,128]{2,1,0:T(8,128)(2,1)S(1)} async-done(((bf16[64,24,128]{2,1,0:T(8,128)(2,1)}), bf16[64,24,128]{2,1,0:T(8,128)(2,1)S(1)}, u32[]{:S(2)}, u32[]{:S(2)}) %all-to-all-start.2) | async-done | bytes 393248 | tf_op jit(solution)/shard_map/all_to_all | solution.py:532
  98.3 2.4 %collective-permute-start.4 = (bf16[64,24,128]{2,1,0:T(8,128)(2,1)S(1)}, bf16[64,24,128]{2,1,0:T(8,128)(2,1)S(1)}, u32[]{:S(2)}, u32[]{:S(2)}) collective-permute-start(bf16[64,24,128]{2,1,0:T(8,128)(2,1)S(1)} %all-to-all-done.2.mine_ref), channel_id=1, source_target_pairs={{0,1},{1,0},{2,3},{3,2},{4,5},{5,4},{6,7},{7,6},{8,9},{9,8},{10,11... | collective-permute-start | bytes 1179656 | tf_op jit(solution)/shard_map/ppermute | solution.py:535
  100.8 0.1 copy.26.gain_ref
  100.9 1.2 %collective-permute-done.4.other_ref = bf16[64,24,128]{2,1,0:T(8,128)(2,1)S(1)} collective-permute-done((bf16[64,24,128]{2,1,0:T(8,128)(2,1)S(1)}, bf16[64,24,128]{2,1,0:T(8,128)(2,1)S(1)}, u32[]{:S(2)}, u32[]{:S(2)}) %collective-permute-start.4) | collective-permute-done | bytes 393248 | tf_op jit(solution)/shard_map/ppermute | solution.py:535
  102.1 1.3 %finish.1 = (f32[256,512]{1,0:T(8,128)}, f32[512,256]{1,0:T(8,128)}, f32[1,256]{1,0:T(1,128)}, f32[256,128]{1,0:T(8,128)}) custom-call(s32[1]{0:T(128)} %bitcast.core_ref, bf16[64,24,128]{2,1,0:T(8,128)(2,1)S(1)} %all-to-all-done.2.mine_ref, bf16[64,24,128]{2,1,0:T(8,128)(2,1)S(1)} %collective-permute-done.4.other_ref, f32[256,1]{1,0:T(8,128)S(1)} %copy.26.gain_ref, ...), custom_call_target="tpu_custom_call" | custom-call | flops 524288 | bytes 3145728 | tf_op jit(solution)/shard_map/finish/pallas_call | solution.py:476
  (5 shorter events, 0.1 us)
Async XLA Ops:
  1.7 5.4 %collective-permute-start = (bf16[32,1,256]{2,1,0:T(2,128)(2,1)S(1)}, bf16[32,1,256]{2,1,0:T(2,128)(2,1)S(1)}, u32[]{:S(2)}, u32[]{:S(2)}) collective-permute-start(bf16[32,1,256]{2,1,0:T(2,128)(2,1)S(1)} %get-tuple-element.62), channel_id=1, source_target_pairs={{0,1},{1,2},{2,3},{3,4},{4,5},{5,6},{6,7},{7,8},{8,9},{9,10},{10,1... | collective-permute-start | bytes 49160 | tf_op jit(solution)/shard_map/ppermute | solution.py:497
  4.3 3.6 %collective-permute-start.1 = (bf16[32,1,256]{2,1,0:T(2,128)(2,1)S(1)}, bf16[32,1,256]{2,1,0:T(2,128)(2,1)S(1)}, u32[]{:S(2)}, u32[]{:S(2)}) collective-permute-start(bf16[32,1,256]{2,1,0:T(2,128)(2,1)S(1)} %get-tuple-element.61), channel_id=1, source_target_pairs={{1,0},{2,1},{3,2},{4,3},{5,4},{6,5},{7,6},{8,7},{9,8},{10,9},{11,1... | collective-permute-start | bytes 49160 | tf_op jit(solution)/shard_map/ppermute | solution.py:498
  7.0 7.3 %copy-start.1 = (bf16[512,256]{1,0:T(8,128)(2,1)S(1)}, bf16[512,256]{1,0:T(8,128)(2,1)}, u32[]{:S(2)}) copy-start(bf16[512,256]{1,0:T(8,128)(2,1)} %w_out_ref.1) | copy-start | bytes 786436
  7.0 7.4 %copy-start = (bf16[256,512]{1,0:T(8,128)(2,1)S(1)}, bf16[256,512]{1,0:T(8,128)(2,1)}, u32[]{:S(2)}) copy-start(bf16[256,512]{1,0:T(8,128)(2,1)} %w_in_ref.3) | copy-start | bytes 786436
  7.0 7.5 %copy-start.2 = (bf16[256,128]{1,0:T(8,128)(2,1)S(1)}, bf16[256,128]{1,0:T(8,128)(2,1)}, u32[]{:S(2)}) copy-start(bf16[256,128]{1,0:T(8,128)(2,1)} %head_ref.1) | copy-start | bytes 196612
  7.1 7.7 %copy-start.3 = (f32[256]{0:T(256)S(1)}, f32[256]{0:T(256)}, u32[]{:S(2)}) copy-start(f32[256]{0:T(256)} %param.16) | copy-start | bytes 3076
  7.1 7.7 %copy-start.4 = (bf16[32,128,256]{2,1,0:T(8,128)(2,1)S(1)}, bf16[32,128,256]{2,1,0:T(8,128)(2,1)}, u32[]{:S(2)}) copy-start(bf16[32,128,256]{2,1,0:T(8,128)(2,1)} %lat_ref.1) | copy-start | bytes 6291460
  8.0 34.8 %all-to-all-start = ((bf16[32,264,128]{2,1,0:T(8,128)(2,1)}), bf16[32,264,128]{2,1,0:T(8,128)(2,1)}, u32[]{:S(2)}, u32[]{:S(2)}) async-start(bf16[32,264,128]{2,1,0:T(8,128)(2,1)} %pack.1), calls=%async_computation | async-start | bytes 4325376 | tf_op jit(solution)/shard_map/all_to_all | solution.py:511
  14.8 28.0 %copy-start.5 = (s32[1,1,32]{2,1,0:T(1,128)S(1)}, s32[1,1,32]{2,1,0:T(1,128)}, u32[]{:S(2)}) copy-start(s32[1,1,32]{2,1,0:T(1,128)} %rows_ref.1) | copy-start | bytes 388
  56.2 3.0 %collective-permute-start.2 = (bf16[64,24,128]{2,1,0:T(8,128)(2,1)S(1)}, bf16[64,24,128]{2,1,0:T(8,128)(2,1)S(1)}, u32[]{:S(2)}, u32[]{:S(2)}) collective-permute-start(bf16[64,24,128]{2,1,0:T(8,128)(2,1)S(1)} %get-tuple-element.42), channel_id=1, source_target_pairs={{0,1},{1,0},{2,3},{3,2},{4,5},{5,4},{6,7},{7,6},{8,9},{9,8},{10,11... | collective-permute-start | bytes 1179656 | tf_op jit(solution)/shard_map/ppermute | solution.py:522
  56.9 4.0 %collective-permute-start.3 = (bf16[32,256]{1,0:T(8,128)(2,1)S(1)}, bf16[32,256]{1,0:T(8,128)(2,1)S(1)}, u32[]{:S(2)}, u32[]{:S(2)}) collective-permute-start(bf16[32,256]{1,0:T(8,128)(2,1)S(1)} %get-tuple-element.44), channel_id=1, source_target_pairs={{0,15},{1,2},{2,1},{3,4},{4,3},{5,6},{6,5},{7,8},{8,7},{9,10},{10,... | collective-permute-start | bytes 49160 | tf_op jit(solution)/shard_map/ppermute | solution.py:521
  60.9 21.5 %all-to-all-start.1 = ((bf16[64,24,128]{2,1,0:T(8,128)(2,1)}), bf16[64,24,128]{2,1,0:T(8,128)(2,1)S(1)}, u32[]{:S(2)}, u32[]{:S(2)}) async-start(bf16[64,24,128]{2,1,0:T(8,128)(2,1)} %get-tuple-element.46), calls=%async_computation.1 | async-start | bytes 786432 | tf_op jit(solution)/shard_map/all_to_all | solution.py:524
  83.2 15.1 %all-to-all-start.2 = ((bf16[64,24,128]{2,1,0:T(8,128)(2,1)}), bf16[64,24,128]{2,1,0:T(8,128)(2,1)S(1)}, u32[]{:S(2)}, u32[]{:S(2)}) async-start(bf16[64,24,128]{2,1,0:T(8,128)(2,1)} %total.1), calls=%async_computation.2 | async-start | bytes 786432 | tf_op jit(solution)/shard_map/all_to_all | solution.py:532
  98.3 3.8 %collective-permute-start.4 = (bf16[64,24,128]{2,1,0:T(8,128)(2,1)S(1)}, bf16[64,24,128]{2,1,0:T(8,128)(2,1)S(1)}, u32[]{:S(2)}, u32[]{:S(2)}) collective-permute-start(bf16[64,24,128]{2,1,0:T(8,128)(2,1)S(1)} %all-to-all-done.2.mine_ref), channel_id=1, source_target_pairs={{0,1},{1,0},{2,3},{3,2},{4,5},{5,4},{6,7},{7,6},{8,9},{9,8},{10,11... | collective-permute-start | bytes 1179656 | tf_op jit(solution)/shard_map/ppermute | solution.py:535

commit v7 on v6

--- a/solution.py
+++ b/solution.py
@@ -15,6 +15,7 @@
 PULL_ROWS = 16
 PACK_CHUNKS = 4
 BACK_ROWS = 8
+AHEAD = 2
 META = 8
 
 f32 = jnp.float32
@@ -217,10 +218,13 @@
         pltpu.make_async_copy(src, dst, in_sems.at[i])
         for i, (src, dst) in enumerate(((slope_hbm, slope), (xhat_t_hbm, xhat_t), (act_t_hbm, act_t)))
     ]
-    for i in range(blocks // nb):
+    def start(i):
         got_copy(i).start()
         for j in range(nb):
             stk_copy(i * nb + j).start()
+
+    for i in range(AHEAD):
+        start(i)
     for acc in (acc_both, acc_new, acc_head, acc_in, acc_out):
         acc[...] = jnp.zeros_like(acc)
 
@@ -230,7 +234,11 @@
         for j in range(nb):
             stk_copy(first + j).wait()
 
-        @pl.when(i == 0)
+        @pl.when(i + AHEAD < blocks // nb)
+        def _():
+            start(i + AHEAD)
+
+        @pl.when(i == blocks // nb - 1 - AHEAD)
         def _():
             for c in later:
                 c.start()
@@ -424,6 +432,31 @@
     )(left, right, gain, w_in_t, w_out_t, *in_hbm(adv, inv_slope, xhat, both, *before))
 
 
+def edge_kernel(core_ref, outer_ref, grad_ref, out_ref):
+    block = grad_ref[...]
+    place = lax.broadcasted_iota(jnp.int32, block.shape, 1)
+    out_ref[...] = block + jnp.where(place == core_ref[0] * (block.shape[1] - 1), 0.5 * outer_ref[...].astype(f32), 0.0)
+
+
+def add_outer(core, outer, grad):
+    rows, cells, ch = grad.shape
+    ends = pl.BlockSpec((rows, 8, ch), lambda i, core: (0, core[0] * (cells // 8 - 1), 0))
+    return pl.pallas_call(
+        edge_kernel,
+        grid_spec=pltpu.PrefetchScalarGridSpec(
+            num_scalar_prefetch=1,
+            grid=(1,),
+            in_specs=[pl.BlockSpec((rows, 1, ch), lambda i, core: (0, 0, 0)), ends],
+            out_specs=ends,
+        ),
+        out_shape=pltpu.HBM(grad.shape, f32),
+        input_output_aliases={2: 0},
+        compiler_params=params(),
+        cost_estimate=cost(rows * 8 * ch, 2**19),
+        name="edge",
+    )(core, outer, *in_hbm(grad))
+
+
 def total_kernel(got_ref, out_ref):
     total = jnp.sum(got_ref[...].astype(f32), axis=0, keepdims=True).astype(bf16)
     out_ref[...] = jnp.broadcast_to(total, out_ref.shape)
@@ -520,17 +553,16 @@
     lons = 2 * lax.axis_size("chip")
     outer = lax.ppermute(outer, LON, [(i, (i + (1 if i % 2 else -1)) % lons) for i in range(lons)])
     summed, inner = pair(keep, lax.ppermute(send, "core", swap), outer)
-    summed, outer, inner = lax.optimization_barrier((summed, outer, inner))
     parts = lax.all_to_all(summed, chips, 0, 0, tiled=True)
-    outer = outer.astype(f32)
-    grad_left = jnp.where(core == 0, outer, inner)[:, None, :]
-    grad_right = jnp.where(core == 0, inner, outer)[:, None, :]
+    grad_left = jnp.where(core == 1, inner, 0.0)[:, None, :]
+    grad_right = jnp.where(core == 0, inner, 0.0)[:, None, :]
     rest = (grad_left, grad_right, gain_row, w_in_t, w_out_t, adv, inv_slope, xhat, both)
     rows = latent.shape[0]
     grad = backward(*rest, 0, rows // 2)
-    parts, grad = lax.optimization_barrier((parts, grad))
+    parts, grad, outer = lax.optimization_barrier((parts, grad, outer))
+    outer = outer.astype(f32)[:, None, :]
     mine = lax.all_to_all(total(parts), chips, 0, 0, tiled=True)
-    grad = backward(*rest, rows // 2, rows, grad)
+    grad = add_outer(core, outer, backward(*rest, rows // 2, rows, grad))
     mine, grad = lax.optimization_barrier((mine, grad))
     other = lax.ppermute(mine, "core", swap)
     grad_in, grad_out, grad_gain, grad_head = finish(core, mine, other, gain, w_in, head, 2 * groups)

time: 104 us -> 103 us (level)
  waiting for transfers between devices: 33.9 us -> 30.6 us
  Pallas kernels: 38.2 us -> 39.7 us
    all_to_all x1, waiting for transfers between devices: 6.5 us -> 4.01 us  [body(): parts = lax.all_to_all(summed, chips, 0, 0, tiled=True)]
    pallas_call x0 -> x1, Pallas kernels: none -> 1.7 us  [add_outer(): pl.pallas_call(edge_kernel, grid_spec=pltpu.PrefetchScalarGridSpec(num_sc...]
    ppermute x1, waiting for transfers between devices: 0.01 us -> 1.35 us  [body(): summed, inner = pair(keep, lax.ppermute(send, 'core', swap), outer)]
    all_to_all x1, waiting for transfers between devices: 5.4 us -> 4.17 us  [body(): mine = lax.all_to_all(total(parts), chips, 0, 0, tiled=True)]
    all_to_all x1, starting transfers between devices: 4.63 us -> 5.72 us  [body(): mine = lax.all_to_all(total(parts), chips, 0, 0, tiled=True)]
  transfers between devices with their start and end apart: 8 -> 8, of which waited for: 6 -> 6; matrix products, arithmetic and copies ran while one was open for 1% -> 1% of each run, Pallas kernels for 22% -> 23%
where the time goes in v7:
time: 103 us; the launch traced here: 102 us
  Pallas kernels  39.7 us (39%)
  waiting for transfers between devices  30.6 us (30%)
  starting transfers between devices  29.5 us (29%)
  local copies, waits for them, and re-layouts  1.65 us (2%)
    all_to_all x1, waiting for transfers between devices, body(): got = lax.all_to_all(packed, LON, 0, 0, tiled=True)  19 us
    pallas_call x1, Pallas kernels, decode(): pl.pallas_call(decode_kernel, out_shape=(pltpu.HBM((n, ch), bf16), pltpu....  13.2 us
    all_to_all x1, starting transfers between devices, body(): parts = lax.all_to_all(summed, chips, 0, 0, tiled=True)  10.3 us
    pallas_call x2, Pallas kernels, backward(): pl.pallas_call(backward_kernel, grid=((end - begin) // nr,), out_shape=pl...  10.2 us
    pallas_call x1, Pallas kernels, forward(): pl.pallas_call(forward_kernel, grid=(rows // ROWS_STEP,), out_shape=(pltp...  9 us
    all_to_all x1, starting transfers between devices, body(): got = lax.all_to_all(packed, LON, 0, 0, tiled=True)  6.32 us
    all_to_all x1, starting transfers between devices, body(): mine = lax.all_to_all(total(parts), chips, 0, 0, tiled=True)  5.72 us
    all_to_all x1, waiting for transfers between devices, body(): mine = lax.all_to_all(total(parts), chips, 0, 0, tiled=True)  4.17 us
  transfers between devices with their start and end apart: 8, of which 6 were waited for; matrix products, arithmetic and copies ran while one was open for 1% of the time, Pallas kernels for 23%

profile of v7, /device:TPU:1, one launch (start us, length us, event | category | flops | bytes accessed | tf_op | source)
XLA Modules:
  0.0 102.4 jit_solution(13544545241827727999)
XLA Ops:
  0.6 1.0 %fusion = (bf16[32,1,256]{2,1,0:T(2,128)(2,1)S(1)}, bf16[32,1,256]{2,1,0:T(2,128)(2,1)S(1)}) fusion(bf16[32,128,256]{2,1,0:T(8,128)(2,1)} %lat_ref.1), kind=kLoop, calls=%fused_computation.2 | loop fusion | bytes 65536 | tf_op jit(solution)/shard_map/slice | solution.py:542
  1.7 2.7 %collective-permute-start = (bf16[32,1,256]{2,1,0:T(2,128)(2,1)S(1)}, bf16[32,1,256]{2,1,0:T(2,128)(2,1)S(1)}, u32[]{:S(2)}, u32[]{:S(2)}) collective-permute-start(bf16[32,1,256]{2,1,0:T(2,128)(2,1)S(1)} %get-tuple-element.58), channel_id=1, source_target_pairs={{0,1},{1,2},{2,3},{3,4},{4,5},{5,6},{6,7},{7,8},{8,9},{9,10},{10,1... | collective-permute-start | bytes 49160 | tf_op jit(solution)/shard_map/ppermute | solution.py:530
  4.3 0.0 collective-permute-start.1
  4.3 2.7 %pack.1 = bf16[32,264,128]{2,1,0:T(8,128)(2,1)} custom-call(bf16[32,128,128]{2,1,0:T(8,128)(2,1)} %w_hbm.1, bf16[32,128,128]{2,1,0:T(8,128)(2,1)} %t_hbm.1, s32[32,128]{1,0:T(8,128)} %slot_hbm.1, s32[32]{0:T(128)} %count_hbm.1), custom_call_target="tpu_custom_call" | custom-call | flops 1 | bytes 4194304 | tf_op jit(solution)/shard_map/pack/pallas_call | solution.py:90
  7.0 0.0 copy-start.1
  7.0 0.0 copy-start
  7.0 0.0 copy-start.2
  7.1 0.0 copy-start.3
  7.1 0.0 copy-start.4
  7.1 0.0 collective-permute-done
  7.1 0.9 collective-permute-done.1
  8.0 6.3 %all-to-all-start = ((bf16[32,264,128]{2,1,0:T(8,128)(2,1)}), bf16[32,264,128]{2,1,0:T(8,128)(2,1)}, u32[]{:S(2)}, u32[]{:S(2)}) async-start(bf16[32,264,128]{2,1,0:T(8,128)(2,1)} %pack.1), calls=%async_computation | async-start | bytes 4325376 | tf_op jit(solution)/shard_map/all_to_all | solution.py:544
  14.3 0.0 copy-done.1
  14.3 0.1 copy.23
  14.4 0.0 copy-done
  14.4 0.1 copy.24
  14.6 0.0 copy-done.2
  14.6 0.1 copy.22
  14.8 0.0 copy-done.3
  14.8 0.0 copy-done.4
  14.8 0.0 copy-start.5
  14.8 9.0 %forward.1 = (bf16[32,256,256]{2,1,0:T(8,128)(2,1)}, bf16[4096,512]{1,0:T(8,128)(2,1)}, bf16[512,4096]{1,0:T(8,128)(2,1)}, bf16[256,4096]{1,0:T(8,128)(2,1)}, bf...) custom-call(bf16[32,128,256]{2,1,0:T(8,128)(2,1)S(1)} %copy-done.4, ...), custom_call_target="tpu_custom_call" | custom-call | flops 2147483648 | bytes 16777216 | tf_op jit(solution)/shard_map/forward/pallas_call | solution.py:156
  23.8 19.0 %all-to-all-done.got_hbm = bf16[32,264,128]{2,1,0:T(8,128)(2,1)} async-done(((bf16[32,264,128]{2,1,0:T(8,128)(2,1)}), bf16[32,264,128]{2,1,0:T(8,128)(2,1)}, u32[]{:S(2)}, u32[]{:S(2)}) %all-to-all-start) | async-done | bytes 2162720 | tf_op jit(solution)/shard_map/all_to_all | solution.py:544
  42.8 0.0 copy-done.5
  42.8 13.2 %decode.1 = (bf16[4096,256]{1,0:T(8,128)(2,1)}, bf16[32,128,256]{2,1,0:T(8,128)(2,1)}, f32[64,24,128]{2,1,0:T(8,128)S(1)}, bf16[64,24,128]{2,1,0:T(8,128)(2,1)S(1)}, bf16[32,256]{1,0:T(8,128)(2,1)S(1)}) custom-call(s32[1]{0:T(128)} %bitcast.core_ref, s32[1,1,32]{2,1,0:T(1,128)S(1)} %copy-done.5, bf16[32,264,128]{2,1,0:T(8,128)(2,1)} %all-to-all-done.got_hbm, ...), custom_call_target="tpu_custom_call" | custom-call | flops 5368709120 | bytes 25165824 | tf_op jit(solution)/shard_map/decode/pallas_call | solution.py:358
  56.0 0.7 collective-permute-start.2
  56.6 1.3 %collective-permute-done.2.came_ref = bf16[64,24,128]{2,1,0:T(8,128)(2,1)S(1)} collective-permute-done((bf16[64,24,128]{2,1,0:T(8,128)(2,1)S(1)}, bf16[64,24,128]{2,1,0:T(8,128)(2,1)S(1)}, u32[]{:S(2)}, u32[]{:S(2)}) %collective-permute-start.2) | collective-permute-done | bytes 393248 | tf_op jit(solution)/shard_map/ppermute | solution.py:555
  58.0 0.8 pair.1
  58.8 10.3 %all-to-all-start.1 = ((bf16[64,24,128]{2,1,0:T(8,128)(2,1)}), bf16[64,24,128]{2,1,0:T(8,128)(2,1)S(1)}, u32[]{:S(2)}, u32[]{:S(2)}) async-start(bf16[64,24,128]{2,1,0:T(8,128)(2,1)} %get-tuple-element.41), calls=%async_computation.1 | async-start | bytes 786432 | tf_op jit(solution)/shard_map/all_to_all | solution.py:556
  69.1 1.9 %collective-permute-start.3 = (bf16[32,256]{1,0:T(8,128)(2,1)S(1)}, bf16[32,256]{1,0:T(8,128)(2,1)S(1)}, u32[]{:S(2)}, u32[]{:S(2)}) collective-permute-start(bf16[32,256]{1,0:T(8,128)(2,1)S(1)} %get-tuple-element.47), channel_id=1, source_target_pairs={{0,15},{1,2},{2,1},{3,4},{4,3},{5,6},{6,5},{7,8},{8,7},{9,10},{10,... | collective-permute-start | bytes 49160 | tf_op jit(solution)/shard_map/ppermute | solution.py:554
  71.1 5.1 %backward.2.rest_0_ = f32[32,128,256]{2,1,0:T(8,128)} custom-call(f32[32,1,256]{2,1,0:T(1,128)S(1)} %copy.25.left_ref, f32[32,1,256]{2,1,0:T(1,128)S(1)} %broadcast_in_dim.33.right_ref, f32[1,256]{1,0:T(1,128)S(1)} %bitcast.20, bf16[512,256]{1,0:T(8,128)(2,1)S(1)} %bitcast.15, bf16[256,512]{1,0:T(8,128)(2,1)S(1)} %bitcast.12, ...), custom_call_target="tpu_custom_call" | custom-call | flops 1073741824 | bytes 7340032 | tf_op jit(solution)/shard_map/backward/pallas_call | solution.py:411
  76.2 0.0 collective-permute-done.3
  76.2 4.0 %all-to-all-done.1.got_ref = bf16[64,24,128]{2,1,0:T(8,128)(2,1)S(1)} async-done(((bf16[64,24,128]{2,1,0:T(8,128)(2,1)}), bf16[64,24,128]{2,1,0:T(8,128)(2,1)S(1)}, u32[]{:S(2)}, u32[]{:S(2)}) %all-to-all-start.1) | async-done | bytes 393248 | tf_op jit(solution)/shard_map/all_to_all | solution.py:556
  80.2 0.8 total.1
  81.0 5.7 %all-to-all-start.2 = ((bf16[64,24,128]{2,1,0:T(8,128)(2,1)}), bf16[64,24,128]{2,1,0:T(8,128)(2,1)S(1)}, u32[]{:S(2)}, u32[]{:S(2)}) async-start(bf16[64,24,128]{2,1,0:T(8,128)(2,1)} %total.1), calls=%async_computation.2 | async-start | bytes 786432 | tf_op jit(solution)/shard_map/all_to_all | solution.py:564
  86.8 5.1 %backward.3.grad_ref = f32[32,128,256]{2,1,0:T(8,128)} custom-call(f32[32,1,256]{2,1,0:T(1,128)S(1)} %copy.25.left_ref, f32[32,1,256]{2,1,0:T(1,128)S(1)} %broadcast_in_dim.33.right_ref, f32[1,256]{1,0:T(1,128)S(1)} %bitcast.21, bf16[512,256]{1,0:T(8,128)(2,1)S(1)} %bitcast.16, bf16[256,512]{1,0:T(8,128)(2,1)S(1)} %bitcast.13, ...), custom_call_target="tpu_custom_call", output_to_operand_aliasing={{}: (9, {})} | custom-call | flops 1073741824 | bytes 7340032 | tf_op jit(solution)/shard_map/backward/pallas_call | solution.py:411
  91.9 1.7 %edge.1 = f32[32,128,256]{2,1,0:T(8,128)} custom-call(s32[1]{0:T(128)} %bitcast.core_ref, f32[32,1,256]{2,1,0:T(1,128)S(1)} %reshape.28.outer_ref, f32[32,128,256]{2,1,0:T(8,128)} %backward.3.grad_ref), custom_call_target="tpu_custom_call", output_to_operand_aliasing={{}: (2, {})} | custom-call | flops 65536 | bytes 524288 | tf_op jit(solution)/shard_map/edge/pallas_call | solution.py:444
  93.6 4.2 %all-to-all-done.2.mine_ref = bf16[64,24,128]{2,1,0:T(8,128)(2,1)S(1)} async-done(((bf16[64,24,128]{2,1,0:T(8,128)(2,1)}), bf16[64,24,128]{2,1,0:T(8,128)(2,1)S(1)}, u32[]{:S(2)}, u32[]{:S(2)}) %all-to-all-start.2) | async-done | bytes 393248 | tf_op jit(solution)/shard_map/all_to_all | solution.py:564
  97.8 2.0 %collective-permute-start.4 = (bf16[64,24,128]{2,1,0:T(8,128)(2,1)S(1)}, bf16[64,24,128]{2,1,0:T(8,128)(2,1)S(1)}, u32[]{:S(2)}, u32[]{:S(2)}) collective-permute-start(bf16[64,24,128]{2,1,0:T(8,128)(2,1)S(1)} %all-to-all-done.2.mine_ref), channel_id=1, source_target_pairs={{0,1},{1,0},{2,3},{3,2},{4,5},{5,4},{6,7},{7,6},{8,9},{9,8},{10,11... | collective-permute-start | bytes 1179656 | tf_op jit(solution)/shard_map/ppermute | solution.py:567
  99.7 0.1 copy.27.gain_ref
  99.8 1.2 %collective-permute-done.4.other_ref = bf16[64,24,128]{2,1,0:T(8,128)(2,1)S(1)} collective-permute-done((bf16[64,24,128]{2,1,0:T(8,128)(2,1)S(1)}, bf16[64,24,128]{2,1,0:T(8,128)(2,1)S(1)}, u32[]{:S(2)}, u32[]{:S(2)}) %collective-permute-start.4) | collective-permute-done | bytes 393248 | tf_op jit(solution)/shard_map/ppermute | solution.py:567
  101.1 1.3 %finish.1 = (f32[256,512]{1,0:T(8,128)}, f32[512,256]{1,0:T(8,128)}, f32[1,256]{1,0:T(1,128)}, f32[256,128]{1,0:T(8,128)}) custom-call(s32[1]{0:T(128)} %bitcast.core_ref, bf16[64,24,128]{2,1,0:T(8,128)(2,1)S(1)} %all-to-all-done.2.mine_ref, bf16[64,24,128]{2,1,0:T(8,128)(2,1)S(1)} %collective-permute-done.4.other_ref, f32[256,1]{1,0:T(8,128)S(1)} %copy.27.gain_ref, ...), custom_call_target="tpu_custom_call" | custom-call | flops 524288 | bytes 3145728 | tf_op jit(solution)/shard_map/finish/pallas_call | solution.py:509
  (6 shorter events, 0.2 us)
Async XLA Ops:
  1.7 5.4 %collective-permute-start = (bf16[32,1,256]{2,1,0:T(2,128)(2,1)S(1)}, bf16[32,1,256]{2,1,0:T(2,128)(2,1)S(1)}, u32[]{:S(2)}, u32[]{:S(2)}) collective-permute-start(bf16[32,1,256]{2,1,0:T(2,128)(2,1)S(1)} %get-tuple-element.58), channel_id=1, source_target_pairs={{0,1},{1,2},{2,3},{3,4},{4,5},{5,6},{6,7},{7,8},{8,9},{9,10},{10,1... | collective-permute-start | bytes 49160 | tf_op jit(solution)/shard_map/ppermute | solution.py:530
  4.3 3.6 %collective-permute-start.1 = (bf16[32,1,256]{2,1,0:T(2,128)(2,1)S(1)}, bf16[32,1,256]{2,1,0:T(2,128)(2,1)S(1)}, u32[]{:S(2)}, u32[]{:S(2)}) collective-permute-start(bf16[32,1,256]{2,1,0:T(2,128)(2,1)S(1)} %get-tuple-element.57), channel_id=1, source_target_pairs={{1,0},{2,1},{3,2},{4,3},{5,4},{6,5},{7,6},{8,7},{9,8},{10,9},{11,1... | collective-permute-start | bytes 49160 | tf_op jit(solution)/shard_map/ppermute | solution.py:531
  7.0 7.3 %copy-start.1 = (bf16[512,256]{1,0:T(8,128)(2,1)S(1)}, bf16[512,256]{1,0:T(8,128)(2,1)}, u32[]{:S(2)}) copy-start(bf16[512,256]{1,0:T(8,128)(2,1)} %w_out_ref.1) | copy-start | bytes 786436
  7.0 7.4 %copy-start = (bf16[256,512]{1,0:T(8,128)(2,1)S(1)}, bf16[256,512]{1,0:T(8,128)(2,1)}, u32[]{:S(2)}) copy-start(bf16[256,512]{1,0:T(8,128)(2,1)} %w_in_ref.3) | copy-start | bytes 786436
  7.0 7.5 %copy-start.2 = (bf16[256,128]{1,0:T(8,128)(2,1)S(1)}, bf16[256,128]{1,0:T(8,128)(2,1)}, u32[]{:S(2)}) copy-start(bf16[256,128]{1,0:T(8,128)(2,1)} %head_ref.1) | copy-start | bytes 196612
  7.1 7.7 %copy-start.3 = (f32[256]{0:T(256)S(1)}, f32[256]{0:T(256)}, u32[]{:S(2)}) copy-start(f32[256]{0:T(256)} %param.16) | copy-start | bytes 3076
  7.1 7.7 %copy-start.4 = (bf16[32,128,256]{2,1,0:T(8,128)(2,1)S(1)}, bf16[32,128,256]{2,1,0:T(8,128)(2,1)}, u32[]{:S(2)}) copy-start(bf16[32,128,256]{2,1,0:T(8,128)(2,1)} %lat_ref.1) | copy-start | bytes 6291460
  8.0 34.8 %all-to-all-start = ((bf16[32,264,128]{2,1,0:T(8,128)(2,1)}), bf16[32,264,128]{2,1,0:T(8,128)(2,1)}, u32[]{:S(2)}, u32[]{:S(2)}) async-start(bf16[32,264,128]{2,1,0:T(8,128)(2,1)} %pack.1), calls=%async_computation | async-start | bytes 4325376 | tf_op jit(solution)/shard_map/all_to_all | solution.py:544
  14.8 28.0 %copy-start.5 = (s32[1,1,32]{2,1,0:T(1,128)S(1)}, s32[1,1,32]{2,1,0:T(1,128)}, u32[]{:S(2)}) copy-start(s32[1,1,32]{2,1,0:T(1,128)} %rows_ref.1) | copy-start | bytes 388
  56.0 2.0 %collective-permute-start.2 = (bf16[64,24,128]{2,1,0:T(8,128)(2,1)S(1)}, bf16[64,24,128]{2,1,0:T(8,128)(2,1)S(1)}, u32[]{:S(2)}, u32[]{:S(2)}) collective-permute-start(bf16[64,24,128]{2,1,0:T(8,128)(2,1)S(1)} %get-tuple-element.40), channel_id=1, source_target_pairs={{0,1},{1,0},{2,3},{3,2},{4,5},{5,4},{6,7},{7,6},{8,9},{9,8},{10,11... | collective-permute-start | bytes 1179656 | tf_op jit(solution)/shard_map/ppermute | solution.py:555
  58.8 21.4 %all-to-all-start.1 = ((bf16[64,24,128]{2,1,0:T(8,128)(2,1)}), bf16[64,24,128]{2,1,0:T(8,128)(2,1)S(1)}, u32[]{:S(2)}, u32[]{:S(2)}) async-start(bf16[64,24,128]{2,1,0:T(8,128)(2,1)} %get-tuple-element.41), calls=%async_computation.1 | async-start | bytes 786432 | tf_op jit(solution)/shard_map/all_to_all | solution.py:556
  69.1 7.1 %collective-permute-start.3 = (bf16[32,256]{1,0:T(8,128)(2,1)S(1)}, bf16[32,256]{1,0:T(8,128)(2,1)S(1)}, u32[]{:S(2)}, u32[]{:S(2)}) collective-permute-start(bf16[32,256]{1,0:T(8,128)(2,1)S(1)} %get-tuple-element.47), channel_id=1, source_target_pairs={{0,15},{1,2},{2,1},{3,4},{4,3},{5,6},{6,5},{7,8},{8,7},{9,10},{10,... | collective-permute-start | bytes 49160 | tf_op jit(solution)/shard_map/ppermute | solution.py:554
  81.0 16.7 %all-to-all-start.2 = ((bf16[64,24,128]{2,1,0:T(8,128)(2,1)}), bf16[64,24,128]{2,1,0:T(8,128)(2,1)S(1)}, u32[]{:S(2)}, u32[]{:S(2)}) async-start(bf16[64,24,128]{2,1,0:T(8,128)(2,1)} %total.1), calls=%async_computation.2 | async-start | bytes 786432 | tf_op jit(solution)/shard_map/all_to_all | solution.py:564
  97.8 3.3 %collective-permute-start.4 = (bf16[64,24,128]{2,1,0:T(8,128)(2,1)S(1)}, bf16[64,24,128]{2,1,0:T(8,128)(2,1)S(1)}, u32[]{:S(2)}, u32[]{:S(2)}) collective-permute-start(bf16[64,24,128]{2,1,0:T(8,128)(2,1)S(1)} %all-to-all-done.2.mine_ref), channel_id=1, source_target_pairs={{0,1},{1,0},{2,3},{3,2},{4,5},{5,4},{6,7},{7,6},{8,9},{9,8},{10,11... | collective-permute-start | bytes 1179656 | tf_op jit(solution)/shard_map/ppermute | solution.py:567

commit v8 on v7

--- a/solution.py
+++ b/solution.py
@@ -12,10 +12,11 @@
 NORM_EPS = 1e-05
 ROWS_STEP = 8
 BLOCKS_STEP = 8
-PULL_ROWS = 16
+PULL_ROWS = 8
 PACK_CHUNKS = 4
 BACK_ROWS = 8
-AHEAD = 2
+AHEAD = 3
+LATER_AT = 0
 META = 8
 
 f32 = jnp.float32
@@ -121,8 +122,8 @@
 
 
 def forward_kernel(
-    lat_ref, left_ref, right_ref, gain_ref, w_in_ref, w_out_ref,
-    stk_ref, slope_ref, act_t_ref, xhat_t_ref, xhat_ref, inv_slope_ref, ends_ref,
+    lat_ref, left_ref, right_ref, gain_ref, w_in_ref, w_out_ref, head_ref,
+    shown_ref, lat_t_ref, slope_ref, act_t_ref, xhat_t_ref, xhat_ref, inv_slope_ref, ends_ref,
 ):
     rows, cells, ch = lat_ref.shape
     lat_b = lat_ref[...]
@@ -139,25 +140,30 @@
     slope = sig * (1.0 + pre * (1.0 - sig))
     slope_ref[...] = slope.astype(bf16)
     inv_slope_ref[...] = (slope * inv3.reshape(rows * cells, 1)).astype(bf16)
-    new = lat.reshape(rows * cells, ch) + dot(act_b, w_out_ref[...])
-    stk_ref[:, 0:cells, :] = lat_b
-    stk_ref[:, cells : 2 * cells, :] = new.astype(bf16).reshape(rows, cells, ch)
+    new = (lat.reshape(rows * cells, ch) + dot(act_b, w_out_ref[...])).astype(bf16)
+    old = lat_b.reshape(rows * cells, ch)
+    for k, tile in enumerate((old, new)):
+        shown = dot(tile, head_ref[...]).astype(bf16)
+        shown_ref[:, k * cells : (k + 1) * cells, :] = shown.reshape(rows, cells, shown.shape[1])
+    lat_t_ref[...] = old.T
     xhat_b = xhat.astype(bf16)
     xhat_ref[...] = xhat_b
     act_t_ref[...] = act_b.T
     xhat_t_ref[...] = xhat_b.T
 
 
-def forward(latent, left, right, gain, w_in, w_out):
+def forward(latent, left, right, gain, w_in, w_out, head):
     rows, cells, ch = latent.shape
     hid = w_in.shape[1]
+    nv = head.shape[1]
     n = rows * cells
     step = ROWS_STEP * cells
     return pl.pallas_call(
         forward_kernel,
         grid=(rows // ROWS_STEP,),
         out_shape=(
-            pltpu.HBM((rows, 2 * cells, ch), bf16),
+            pltpu.HBM((rows, 2 * cells, nv), bf16),
+            pltpu.HBM((ch, n), bf16),
             pltpu.HBM((n, hid), bf16),
             pltpu.HBM((hid, n), bf16),
             pltpu.HBM((ch, n), bf16),
@@ -172,9 +178,11 @@
             pl.BlockSpec((1, ch), lambda i: (0, 0)),
             pl.BlockSpec((ch, hid), lambda i: (0, 0)),
             pl.BlockSpec((hid, ch), lambda i: (0, 0)),
+            pl.BlockSpec((ch, nv), lambda i: (0, 0)),
         ],
         out_specs=(
-            pl.BlockSpec((ROWS_STEP, 2 * cells, ch), lambda i: (i, 0, 0)),
+            pl.BlockSpec((ROWS_STEP, 2 * cells, nv), lambda i: (i, 0, 0)),
+            pl.BlockSpec((ch, step), lambda i: (0, i)),
             pl.BlockSpec((step, hid), lambda i: (i, 0)),
             pl.BlockSpec((hid, step), lambda i: (0, i)),
             pl.BlockSpec((ch, step), lambda i: (0, i)),
@@ -185,21 +193,21 @@
         compiler_params=params(),
         cost_estimate=cost(4 * n * ch * hid, 16 * 2**20, 2 * n * hid),
         name="forward",
-    )(latent, left, right, gain, w_in, w_out)
+    )(latent, left, right, gain, w_in, w_out, head)
 
 
 def decode_kernel(
-    core_ref, rows_ref, got_hbm, stk_hbm, head_ref, head_t_ref, w_out_t_ref, w_in_t_ref, gain_ref, ends_ref,
-    slope_hbm, act_t_hbm, xhat_t_hbm,
-    adv_hbm, both_hbm, keep_ref, send_ref, outer_ref,
-    got, stk, slope, act_t, xhat_t, adv_all, both_all, ends, acc_both, acc_new, acc_head, acc_in, acc_out,
-    got_sems, stk_sems, in_sems, out_sems,
+    core_ref, rows_ref, got_hbm, shown_hbm, head_t_ref, joint_ref, w_out_t_ref, w_in_t_ref, gain_ref, ends_ref,
+    slope_hbm, act_t_hbm, xhat_t_hbm, lat_t_hbm,
+    q_hbm, keep_ref, send_ref, outer_ref,
+    got, shown, slope, act_t, xhat_t, lat_t, q_all, ends, acc_q, acc_head, acc_in, acc_act,
+    got_sems, shown_sems, in_sems, q_sems,
 ):
     nb, nr = BLOCKS_STEP, PULL_ROWS
     blocks = got.shape[0]
-    ch, nv = head_ref.shape
+    nv, ch = head_t_ref.shape
     obs = (got.shape[1] - META) // 2
-    rows, cells, _ = acc_both.shape
+    rows, cells, _ = acc_q.shape
     scale = 1.0 / math.sqrt(obs)
     step = nr * cells
 
@@ -207,90 +215,86 @@
         here = pl.ds(i * nb, nb)
         return pltpu.make_async_copy(got_hbm.at[here], got.at[here], got_sems.at[i])
 
-    def stk_copy(b):
-        return pltpu.make_async_copy(stk_hbm.at[rows_ref[0, 0, b]], stk.at[b], stk_sems.at[b])
-
-    def adv_copy(k):
+    def shown_copy(b):
+        return pltpu.make_async_copy(shown_hbm.at[rows_ref[0, 0, b]], shown.at[b], shown_sems.at[b])
+
+    def q_copy(k):
         flat = pl.ds(pl.multiple_of(k * step, step), step)
-        return pltpu.make_async_copy(adv_all.at[flat], adv_hbm.at[flat], out_sems.at[k])
-
-    later = [
-        pltpu.make_async_copy(src, dst, in_sems.at[i])
-        for i, (src, dst) in enumerate(((slope_hbm, slope), (xhat_t_hbm, xhat_t), (act_t_hbm, act_t)))
-    ]
+        return pltpu.make_async_copy(q_all.at[flat], q_hbm.at[flat], q_sems.at[k])
+
+    def chunk_copies(k):
+        flat = pl.ds(pl.multiple_of(k * step, step), step)
+        turned = ((lat_t_hbm, lat_t), (xhat_t_hbm, xhat_t), (act_t_hbm, act_t))
+        return [pltpu.make_async_copy(slope_hbm.at[flat], slope.at[flat], in_sems.at[0, k])] + [
+            pltpu.make_async_copy(src.at[:, flat], dst.at[:, flat], in_sems.at[1 + i, k]) for i, (src, dst) in enumerate(turned)
+        ]
+
     def start(i):
         got_copy(i).start()
         for j in range(nb):
-            stk_copy(i * nb + j).start()
+            shown_copy(i * nb + j).start()
 
     for i in range(AHEAD):
         start(i)
-    for acc in (acc_both, acc_new, acc_head, acc_in, acc_out):
+    for acc in (acc_q, acc_head, acc_in, acc_act):
         acc[...] = jnp.zeros_like(acc)
 
     def observe(i, carry):
         first = i * nb
         got_copy(i).wait()
         for j in range(nb):
-            stk_copy(first + j).wait()
+            shown_copy(first + j).wait()
 
         @pl.when(i + AHEAD < blocks // nb)
         def _():
             start(i + AHEAD)
 
-        @pl.when(i == blocks // nb - 1 - AHEAD)
+        @pl.when(i == LATER_AT)
         def _():
-            for c in later:
-                c.start()
+            for k in range(rows // nr):
+                for c in chunk_copies(k):
+                    c.start()
 
         places = [rows_ref[0, 0, first + j] for j in range(nb)]
         meta = jnp.concatenate([got[first + j, 2 * obs : 2 * obs + META, :].astype(f32) for j in range(nb)], axis=0).T
-        latents, coefs, lives = [], [], []
+        preds = []
+        for j in range(nb):
+            t = meta[:, META * j : META * j + 1]
+            w = got[first + j, 0:obs, :]
+            w_new = w * jnp.broadcast_to(t, w.shape).astype(bf16)
+            preds.append(dot(jnp.concatenate([w - w_new, w_new], axis=1), shown[first + j]))
+        grads = []
         for j in range(nb):
             t, live = meta[:, META * j : META * j + 1], meta[:, META * j + 1 : META * j + 2]
-            w = got[first + j, 0:obs, :]
-            w_new = w * jnp.broadcast_to(t, w.shape).astype(bf16)
-            latents.append(dot(jnp.concatenate([w - w_new, w_new], axis=1), stk[first + j]).astype(bf16))
-            coefs.append(t)
-            lives.append(live)
-        obs_latent = jnp.concatenate(latents, axis=0)
-        pred = dot(obs_latent, head_ref[...])
-        goals = jnp.concatenate([got[first + j, obs : 2 * obs, :] for j in range(nb)], axis=0)
-        live = jnp.concatenate(lives, axis=0)
-        residual = jnp.where(live > 0.5, pred - goals.astype(f32), 0.0)
-        pred_grad = (residual * scale).astype(bf16)
-        acc_head[...] += dot_t(pred_grad, obs_latent)
-        grad = dot(pred_grad, head_t_ref[...])
+            residual = jnp.where(live > 0.5, preds[j] - got[first + j, obs : 2 * obs, :].astype(f32), 0.0) * scale
+            grads.append(jnp.concatenate([residual.astype(bf16), (residual * t).astype(bf16)], axis=1))
+        pulled = [dot_t(got[first + j, 0:obs, :], grads[j]) for j in range(nb)]
         for j in range(nb):
-            g = grad[j * obs : (j + 1) * obs, :]
-            w = got[first + j, 0:obs, :]
-            pulled = dot_t(w, jnp.concatenate([g.astype(bf16), (g * coefs[j]).astype(bf16)], axis=1))
-            acc_both[places[j]] += pulled[:, :ch]
-            acc_new[places[j]] += pulled[:, ch:]
+            acc_q[places[j]] += pulled[j]
         return carry
 
     lax.fori_loop(0, blocks // nb, observe, 0)
-    both_all[...] = acc_both[...].astype(bf16)
-    both_copy = pltpu.make_async_copy(both_all, both_hbm, out_sems.at[rows // nr])
-    both_copy.start()
-    for c in later:
-        c.wait()
-
     def pull(k, carry):
         flat = pl.ds(pl.multiple_of(k * step, step), step)
-        adv = acc_new[pl.ds(k * nr, nr)].reshape(step, ch).astype(bf16)
-        adv_all[flat, :] = adv
-        adv_copy(k).start()
-        pre_grad = (dot(adv, w_out_t_ref[...]) * slope[flat, :].astype(f32)).astype(bf16)
+        for c in chunk_copies(k):
+            c.wait()
+        q = acc_q[pl.ds(k * nr, nr)].reshape(step, 2 * nv).astype(bf16)
+        q_all[flat, :] = q
+        q_copy(k).start()
+        pre_grad = (dot(q[:, nv:], joint_ref[...]) * slope[flat, :].astype(f32)).astype(bf16)
+        acc_act[...] += dot(act_t[:, flat], q[:, nv:])
+        acc_head[...] += dot(lat_t[:, flat], q[:, :nv])
         here = pl.ds(pl.multiple_of(k * nr, nr), nr)
         by_row = pre_grad.reshape(nr, cells, pre_grad.shape[1])
         ends[0, here, :] = by_row[:, 0, :].astype(f32)
         ends[1, here, :] = by_row[:, cells - 1, :].astype(f32)
         acc_in[...] += dot(xhat_t[:, flat], pre_grad)
-        acc_out[...] += dot(act_t[:, flat], adv)
         return carry
 
     lax.fori_loop(0, rows // nr, pull, 0)
+    by_hidden = acc_act[...].astype(bf16)
+    out_sum = dot(by_hidden, head_t_ref[...])
+    head_sum = (acc_head[...] + dot(w_out_t_ref[...], by_hidden)).T
     edges = []
     for k in range(2):
         gained = dot(ends[k].astype(bf16), w_in_t_ref[...]) * gain_ref[...]
@@ -300,14 +304,13 @@
 
         @pl.when(core_ref[0] == core)
         def _(core=core):
-            put_chunks(keep_ref, core, acc_in, acc_out, acc_head)
-            put_chunks(send_ref, 1 - core, acc_in, acc_out, acc_head)
+            put_chunks(keep_ref, core, acc_in, out_sum, head_sum)
+            put_chunks(send_ref, 1 - core, acc_in, out_sum, head_sum)
             outer_ref[...] = edges[core].astype(bf16)
             put_edge(send_ref, edges[1 - core])
 
-    both_copy.wait()
     for k in range(rows // nr):
-        adv_copy(k).wait()
+        q_copy(k).wait()
 
 
 def put_chunks(ref, half, *accs):
@@ -346,10 +349,10 @@
     )
 
 
-def decode(core, rows, got, stk, head, head_t, w_out_t, w_in_t, gain, ends, slope, act_t, xhat_t, chunks):
-    nrow, two_cells, ch = stk.shape
+def decode(core, rows, got, shown, head_t, joint, w_out_t, w_in_t, gain, ends, slope, act_t, xhat_t, lat_t, chunks):
+    nrow, two_cells, nv = shown.shape
     cells = two_cells // 2
-    nv = head.shape[1]
+    ch = head_t.shape[1]
     hid = w_out_t.shape[1]
     n = nrow * cells
     blocks = got.shape[0]
@@ -358,50 +361,50 @@
     return pl.pallas_call(
         decode_kernel,
         out_shape=(
-            pltpu.HBM((n, ch), bf16),
-            pltpu.HBM((nrow, cells, ch), bf16),
+            pltpu.HBM((n, 2 * nv), bf16),
             jax.ShapeDtypeStruct((chunks, 24, 128), f32),
             jax.ShapeDtypeStruct((chunks, 24, 128), bf16),
             jax.ShapeDtypeStruct((nrow, ch), bf16),
         ),
-        in_specs=[scalars] * 2 + [OUTSIDE] * 2 + [INSIDE] * 6 + [OUTSIDE] * 3,
-        out_specs=(OUTSIDE, OUTSIDE) + (INSIDE,) * 3,
-        scratch_shapes=[pltpu.VMEM(x.shape, bf16) for x in (got, stk, slope, act_t, xhat_t)]
+        in_specs=[scalars] * 2 + [OUTSIDE] * 2 + [INSIDE] * 6 + [OUTSIDE] * 4,
+        out_specs=(OUTSIDE,) + (INSIDE,) * 3,
+        scratch_shapes=[pltpu.VMEM(x.shape, bf16) for x in (got, shown, slope, act_t, xhat_t, lat_t)]
         + [
-            pltpu.VMEM((n, ch), bf16),
-            pltpu.VMEM((nrow, cells, ch), bf16),
+            pltpu.VMEM((n, 2 * nv), bf16),
             pltpu.VMEM((2, nrow, hid), f32),
-            pltpu.VMEM((nrow, cells, ch), f32),
-            pltpu.VMEM((nrow, cells, ch), f32),
-            pltpu.VMEM((nv, ch), f32),
+            pltpu.VMEM((nrow, cells, 2 * nv), f32),
+            pltpu.VMEM((ch, nv), f32),
             pltpu.VMEM((ch, hid), f32),
-            pltpu.VMEM((hid, ch), f32),
+            pltpu.VMEM((hid, nv), f32),
             dma((blocks // BLOCKS_STEP,)),
             dma((blocks,)),
-            dma((3,)),
-            dma((nrow // PULL_ROWS + 1,)),
+            dma((4, nrow // PULL_ROWS)),
+            dma((nrow // PULL_ROWS,)),
         ],
         compiler_params=params(),
         cost_estimate=cost(10 * n * ch * hid, 24 * 2**20),
         name="decode",
-    )(core, rows, *in_hbm(got, stk), head, head_t, w_out_t, w_in_t, gain, ends, *in_hbm(slope, act_t, xhat_t))
+    )(core, rows, *in_hbm(got, shown), head_t, joint, w_out_t, w_in_t, gain, ends, *in_hbm(slope, act_t, xhat_t, lat_t))
 
 
 def backward_kernel(
-    left_ref, right_ref, gain_ref, w_in_t_ref, w_out_t_ref, adv_ref, slope_ref, xhat_ref, both_ref, *rest
+    left_ref, right_ref, gain_ref, w_in_t_ref, joint_ref, head_t_ref, q_ref, slope_ref, xhat_ref, *rest
 ):
     out_ref = rest[-1]
     rows, cells, ch = out_ref.shape
-    pre_grad = (dot(adv_ref[...], w_out_t_ref[...]) * slope_ref[...].astype(f32)).astype(bf16)
+    nv = head_t_ref.shape[0]
+    pre_grad = (dot(q_ref[:, nv:], joint_ref[...]) * slope_ref[...].astype(f32)).astype(bf16)
+    both = dot(q_ref[:, :nv], head_t_ref[...]).reshape(rows, cells, ch)
     gained = dot(pre_grad, w_in_t_ref[...]) * gain_ref[...]
     xhat = xhat_ref[...].astype(f32)
     summed_grad = gained - xhat * jnp.mean(gained * xhat, axis=-1, keepdims=True)
-    out_ref[...] = both_ref[...].astype(f32) + mixed(summed_grad.reshape(rows, cells, ch), left_ref[...], right_ref[...])
-
-
-def backward(left, right, gain, w_in_t, w_out_t, adv, inv_slope, xhat, both, begin, end, *before):
-    rows, cells, ch = both.shape
-    hid = w_in_t.shape[0]
+    out_ref[...] = both + mixed(summed_grad.reshape(rows, cells, ch), left_ref[...], right_ref[...])
+
+
+def backward(left, right, gain, w_in_t, joint, head_t, q, inv_slope, xhat, begin, end, *before):
+    rows, ch = left.shape[0], left.shape[2]
+    cells = xhat.shape[0] // rows
+    nv, hid = joint.shape
     nr = BACK_ROWS
     step = nr * cells
     base = begin // nr
@@ -417,11 +420,11 @@
             edge,
             pl.BlockSpec((1, ch), lambda i: (0, 0)),
             pl.BlockSpec((hid, ch), lambda i: (0, 0)),
-            pl.BlockSpec((ch, hid), lambda i: (0, 0)),
-            pl.BlockSpec((step, ch), lambda i: (i + base, 0)),
+            pl.BlockSpec((nv, hid), lambda i: (0, 0)),
+            pl.BlockSpec((nv, ch), lambda i: (0, 0)),
+            pl.BlockSpec((step, 2 * nv), lambda i: (i + base, 0)),
             pl.BlockSpec((step, hid), lambda i: (i + base, 0)),
             pl.BlockSpec((step, ch), lambda i: (i + base, 0)),
-            whole,
         ]
         + [OUTSIDE] * len(before),
         out_specs=whole,
@@ -429,7 +432,7 @@
         compiler_params=params(),
         cost_estimate=cost(4 * share * ch * hid, 3584 * share),
         name="backward",
-    )(left, right, gain, w_in_t, w_out_t, *in_hbm(adv, inv_slope, xhat, both, *before))
+    )(left, right, gain, w_in_t, joint, head_t, *in_hbm(q, inv_slope, xhat, *before))
 
 
 def edge_kernel(core_ref, outer_ref, grad_ref, out_ref):
@@ -546,9 +549,13 @@
     gain_row = gain.reshape(1, -1)
     w_out_t = w_out.T
     w_in_t = w_in.T
-    stk, slope, act_t, xhat_t, xhat, inv_slope, ends = forward(latent, left, right, gain_row, w_in, w_out)
-    adv, both, keep, send, outer = decode(
-        core, row_index, got, stk, head, head.T, w_out_t, w_in_t, gain_row, ends, slope, act_t, xhat_t, groups
+    shown, lat_t, slope, act_t, xhat_t, xhat, inv_slope, ends = forward(
+        latent, left, right, gain_row, w_in, w_out, head
+    )
+    head_t = head.T
+    joint = dot(head_t, w_out_t).astype(bf16)
+    q, keep, send, outer = decode(
+        core, row_index, got, shown, head_t, joint, w_out_t, w_in_t, gain_row, ends, slope, act_t, xhat_t, lat_t, groups
     )
     lons = 2 * lax.axis_size("chip")
     outer = lax.ppermute(outer, LON, [(i, (i + (1 if i % 2 else -1)) % lons) for i in range(lons)])
@@ -556,7 +563,7 @@
     parts = lax.all_to_all(summed, chips, 0, 0, tiled=True)
     grad_left = jnp.where(core == 1, inner, 0.0)[:, None, :]
     grad_right = jnp.where(core == 0, inner, 0.0)[:, None, :]
-    rest = (grad_left, grad_right, gain_row, w_in_t, w_out_t, adv, inv_slope, xhat, both)
+    rest = (grad_left, grad_right, gain_row, w_in_t, joint, head_t, q, inv_slope, xhat)
     rows = latent.shape[0]
     grad = backward(*rest, 0, rows // 2)
     parts, grad, outer = lax.optimization_barrier((parts, grad, outer))

time: 103 us -> 101 us (0.981)
  Pallas kernels: 39.7 us -> 37.4 us
  waiting for transfers between devices: 30.6 us -> 28.9 us
  local copies, waits for them, and re-layouts: 1.65 us -> 3.21 us
    pallas_call x1, Pallas kernels: 13.2 us -> 10.4 us  [decode(): pl.pallas_call(decode_kernel, out_shape=(pltpu.HBM((n, 2 * nv), bf16), ja...]
    all_to_all x1, waiting for transfers between devices: 19 us -> 17.3 us  [body(): got = lax.all_to_all(packed, LON, 0, 0, tiled=True)]
    unnamed x15 -> x19, local copies, waits for them, and re-layouts: 0.42 us -> 1.97 us
  transfers between devices with their start and end apart: 8 -> 8, of which waited for: 6 -> 6; matrix products, arithmetic and copies ran while one was open for 1% -> 1% of each run, Pallas kernels for 23% -> 24%
where the time goes in v8:
time: 101 us; the launch traced here: 100 us
  Pallas kernels  37.4 us (37%)
  starting transfers between devices  29.7 us (29%)
  waiting for transfers between devices  28.9 us (29%)
  local copies, waits for them, and re-layouts  3.21 us (3%)
    all_to_all x1, waiting for transfers between devices, body(): got = lax.all_to_all(packed, LON, 0, 0, tiled=True)  17.3 us
    pallas_call x1, Pallas kernels, decode(): pl.pallas_call(decode_kernel, out_shape=(pltpu.HBM((n, 2 * nv), bf16), ja...  10.4 us
    all_to_all x1, starting transfers between devices, body(): parts = lax.all_to_all(summed, chips, 0, 0, tiled=True)  10.3 us
    pallas_call x2, Pallas kernels, backward(): pl.pallas_call(backward_kernel, grid=((end - begin) // nr,), out_shape=pl...  9.87 us
    pallas_call x1, Pallas kernels, forward(): pl.pallas_call(forward_kernel, grid=(rows // ROWS_STEP,), out_shape=(pltp...  9.74 us
    all_to_all x1, starting transfers between devices, body(): got = lax.all_to_all(packed, LON, 0, 0, tiled=True)  6.32 us
    all_to_all x1, starting transfers between devices, body(): mine = lax.all_to_all(total(parts), chips, 0, 0, tiled=True)  5.56 us
    all_to_all x1, waiting for transfers between devices, body(): parts = lax.all_to_all(summed, chips, 0, 0, tiled=True)  4.17 us
  transfers between devices with their start and end apart: 8, of which 6 were waited for; matrix products, arithmetic and copies ran while one was open for 1% of the time, Pallas kernels for 24%

profile of v8, /device:TPU:1, one launch (start us, length us, event | category | flops | bytes accessed | tf_op | source)
XLA Modules:
  0.0 100.4 jit_solution(7192300739785799607)
XLA Ops:
  0.6 1.0 %fusion = (bf16[32,1,256]{2,1,0:T(2,128)(2,1)S(1)}, bf16[32,1,256]{2,1,0:T(2,128)(2,1)S(1)}) fusion(bf16[32,128,256]{2,1,0:T(8,128)(2,1)} %lat_ref.1), kind=kLoop, calls=%fused_computation.3 | loop fusion | bytes 65536 | tf_op jit(solution)/shard_map/slice | solution.py:545
  1.7 2.7 %collective-permute-start = (bf16[32,1,256]{2,1,0:T(2,128)(2,1)S(1)}, bf16[32,1,256]{2,1,0:T(2,128)(2,1)S(1)}, u32[]{:S(2)}, u32[]{:S(2)}) collective-permute-start(bf16[32,1,256]{2,1,0:T(2,128)(2,1)S(1)} %get-tuple-element.58), channel_id=1, source_target_pairs={{0,1},{1,2},{2,3},{3,4},{4,5},{5,6},{6,7},{7,8},{8,9},{9,10},{10,1... | collective-permute-start | bytes 49160 | tf_op jit(solution)/shard_map/ppermute | solution.py:533
  4.3 0.0 collective-permute-start.1
  4.3 2.7 %pack.1 = bf16[32,264,128]{2,1,0:T(8,128)(2,1)} custom-call(bf16[32,128,128]{2,1,0:T(8,128)(2,1)} %w_hbm.1, bf16[32,128,128]{2,1,0:T(8,128)(2,1)} %t_hbm.1, s32[32,128]{1,0:T(8,128)} %slot_hbm.1, s32[32]{0:T(128)} %count_hbm.1), custom_call_target="tpu_custom_call" | custom-call | flops 1 | bytes 4194304 | tf_op jit(solution)/shard_map/pack/pallas_call | solution.py:91
  7.1 0.0 copy-start.1
  7.1 0.0 copy-start.2
  7.1 0.0 copy-start
  7.1 0.0 copy-start.3
  7.1 0.0 copy-start.4
  7.1 0.0 collective-permute-done
  7.1 0.8 collective-permute-done.1
  8.0 6.3 %all-to-all-start = ((bf16[32,264,128]{2,1,0:T(8,128)(2,1)}), bf16[32,264,128]{2,1,0:T(8,128)(2,1)}, u32[]{:S(2)}, u32[]{:S(2)}) async-start(bf16[32,264,128]{2,1,0:T(8,128)(2,1)} %pack.1), calls=%async_computation | async-start | bytes 4325376 | tf_op jit(solution)/shard_map/all_to_all | solution.py:547
  14.3 0.0 copy-done.1
  14.3 0.1 copy.24
  14.4 0.0 copy-done.2
  14.4 0.1 copy.22
  14.6 0.0 copy-done
  14.6 0.1 copy.23
  14.7 0.2 convolution_convert_fusion.joint_ref
  15.0 0.0 copy-done.3
  15.0 0.0 copy-done.4
  15.0 0.0 copy-start.5
  15.1 9.7 %forward.1 = (bf16[32,256,128]{2,1,0:T(8,128)(2,1)}, bf16[256,4096]{1,0:T(8,128)(2,1)}, bf16[4096,512]{1,0:T(8,128)(2,1)}, bf16[512,4096]{1,0:T(8,128)(2,1)}, bf...) custom-call(bf16[32,128,256]{2,1,0:T(8,128)(2,1)S(1)} %copy-done.4, ...), custom_call_target="tpu_custom_call" | custom-call | flops 2147483648 | bytes 16777216 | tf_op jit(solution)/shard_map/forward/pallas_call | solution.py:161
  24.8 0.0 copy-start.6
  24.8 0.6 copy-done.6
  25.5 17.3 %all-to-all-done.got_hbm = bf16[32,264,128]{2,1,0:T(8,128)(2,1)} async-done(((bf16[32,264,128]{2,1,0:T(8,128)(2,1)}), bf16[32,264,128]{2,1,0:T(8,128)(2,1)}, u32[]{:S(2)}, u32[]{:S(2)}) %all-to-all-start) | async-done | bytes 2162720 | tf_op jit(solution)/shard_map/all_to_all | solution.py:547
  42.8 0.0 copy-done.5
  42.8 0.0 copy-start.7
  42.8 0.9 copy-done.7
  43.7 10.4 %decode.1 = (bf16[4096,256]{1,0:T(8,128)(2,1)}, f32[64,24,128]{2,1,0:T(8,128)S(1)}, bf16[64,24,128]{2,1,0:T(8,128)(2,1)S(1)}, bf16[32,256]{1,0:T(8,128)(2,1)S(1)}) custom-call(s32[1]{0:T(128)} %bitcast.core_ref, s32[1,1,32]{2,1,0:T(1,128)S(1)} %copy-done.5, bf16[32,264,128]{2,1,0:T(8,128)(2,1)} %all-to-all-done.got_hbm, ...), custom_call_target="tpu_custom_call" | custom-call | flops 5368709120 | bytes 25165824 | tf_op jit(solution)/shard_map/decode/pallas_call | solution.py:361
  54.1 0.7 collective-permute-start.2
  54.8 1.3 %collective-permute-done.2.came_ref = bf16[64,24,128]{2,1,0:T(8,128)(2,1)S(1)} collective-permute-done((bf16[64,24,128]{2,1,0:T(8,128)(2,1)S(1)}, bf16[64,24,128]{2,1,0:T(8,128)(2,1)S(1)}, u32[]{:S(2)}, u32[]{:S(2)}) %collective-permute-start.2) | collective-permute-done | bytes 393248 | tf_op jit(solution)/shard_map/ppermute | solution.py:562
  56.1 0.8 pair.1
  57.0 10.3 %all-to-all-start.1 = ((bf16[64,24,128]{2,1,0:T(8,128)(2,1)}), bf16[64,24,128]{2,1,0:T(8,128)(2,1)S(1)}, u32[]{:S(2)}, u32[]{:S(2)}) async-start(bf16[64,24,128]{2,1,0:T(8,128)(2,1)} %get-tuple-element.42), calls=%async_computation.1 | async-start | bytes 786432 | tf_op jit(solution)/shard_map/all_to_all | solution.py:563
  67.3 1.9 %collective-permute-start.3 = (bf16[32,256]{1,0:T(8,128)(2,1)S(1)}, bf16[32,256]{1,0:T(8,128)(2,1)S(1)}, u32[]{:S(2)}, u32[]{:S(2)}) collective-permute-start(bf16[32,256]{1,0:T(8,128)(2,1)S(1)} %get-tuple-element.47), channel_id=1, source_target_pairs={{0,15},{1,2},{2,1},{3,4},{4,3},{5,6},{6,5},{7,8},{8,7},{9,10},{10,... | collective-permute-start | bytes 49160 | tf_op jit(solution)/shard_map/ppermute | solution.py:561
  69.3 4.9 %backward.2.rest_0_ = f32[32,128,256]{2,1,0:T(8,128)} custom-call(f32[32,1,256]{2,1,0:T(1,128)S(1)} %copy.25.left_ref, f32[32,1,256]{2,1,0:T(1,128)S(1)} %broadcast_in_dim.33.right_ref, f32[1,256]{1,0:T(1,128)S(1)} %bitcast.22, bf16[512,256]{1,0:T(8,128)(2,1)S(1)} %bitcast.14, bf16[128,512]{1,0:T(8,128)(2,1)S(1)} %convolution_convert_fusion.joint_ref, ...), custom_call_target="tpu_custom_call" | custom-call | flops 1073741824 | bytes 7340032 | tf_op jit(solution)/shard_map/backward/pallas_call | solution.py:414
  74.2 0.0 collective-permute-done.3
  74.2 4.2 %all-to-all-done.1.got_ref = bf16[64,24,128]{2,1,0:T(8,128)(2,1)S(1)} async-done(((bf16[64,24,128]{2,1,0:T(8,128)(2,1)}), bf16[64,24,128]{2,1,0:T(8,128)(2,1)S(1)}, u32[]{:S(2)}, u32[]{:S(2)}) %all-to-all-start.1) | async-done | bytes 393248 | tf_op jit(solution)/shard_map/all_to_all | solution.py:563
  78.4 0.8 total.1
  79.2 5.6 %all-to-all-start.2 = ((bf16[64,24,128]{2,1,0:T(8,128)(2,1)}), bf16[64,24,128]{2,1,0:T(8,128)(2,1)S(1)}, u32[]{:S(2)}, u32[]{:S(2)}) async-start(bf16[64,24,128]{2,1,0:T(8,128)(2,1)} %total.1), calls=%async_computation.2 | async-start | bytes 786432 | tf_op jit(solution)/shard_map/all_to_all | solution.py:571
  84.8 4.9 %backward.3.grad_ref = f32[32,128,256]{2,1,0:T(8,128)} custom-call(f32[32,1,256]{2,1,0:T(1,128)S(1)} %copy.25.left_ref, f32[32,1,256]{2,1,0:T(1,128)S(1)} %broadcast_in_dim.33.right_ref, f32[1,256]{1,0:T(1,128)S(1)} %bitcast.23, bf16[512,256]{1,0:T(8,128)(2,1)S(1)} %bitcast.15, ...), custom_call_target="tpu_custom_call", output_to_operand_aliasing={{}: (9, {})} | custom-call | flops 1073741824 | bytes 7340032 | tf_op jit(solution)/shard_map/backward/pallas_call | solution.py:414
  89.8 1.7 %edge.1 = f32[32,128,256]{2,1,0:T(8,128)} custom-call(s32[1]{0:T(128)} %bitcast.core_ref, f32[32,1,256]{2,1,0:T(1,128)S(1)} %reshape.28.outer_ref, f32[32,128,256]{2,1,0:T(8,128)} %backward.3.grad_ref), custom_call_target="tpu_custom_call", output_to_operand_aliasing={{}: (2, {})} | custom-call | flops 65536 | bytes 524288 | tf_op jit(solution)/shard_map/edge/pallas_call | solution.py:447
  91.5 4.0 %all-to-all-done.2.mine_ref = bf16[64,24,128]{2,1,0:T(8,128)(2,1)S(1)} async-done(((bf16[64,24,128]{2,1,0:T(8,128)(2,1)}), bf16[64,24,128]{2,1,0:T(8,128)(2,1)S(1)}, u32[]{:S(2)}, u32[]{:S(2)}) %all-to-all-start.2) | async-done | bytes 393248 | tf_op jit(solution)/shard_map/all_to_all | solution.py:571
  95.5 2.2 %collective-permute-start.4 = (bf16[64,24,128]{2,1,0:T(8,128)(2,1)S(1)}, bf16[64,24,128]{2,1,0:T(8,128)(2,1)S(1)}, u32[]{:S(2)}, u32[]{:S(2)}) collective-permute-start(bf16[64,24,128]{2,1,0:T(8,128)(2,1)S(1)} %all-to-all-done.2.mine_ref), channel_id=1, source_target_pairs={{0,1},{1,0},{2,3},{3,2},{4,5},{5,4},{6,7},{7,6},{8,9},{9,8},{10,11... | collective-permute-start | bytes 1179656 | tf_op jit(solution)/shard_map/ppermute | solution.py:574
  97.7 0.1 copy.27.gain_ref
  97.9 1.2 %collective-permute-done.4.other_ref = bf16[64,24,128]{2,1,0:T(8,128)(2,1)S(1)} collective-permute-done((bf16[64,24,128]{2,1,0:T(8,128)(2,1)S(1)}, bf16[64,24,128]{2,1,0:T(8,128)(2,1)S(1)}, u32[]{:S(2)}, u32[]{:S(2)}) %collective-permute-start.4) | collective-permute-done | bytes 393248 | tf_op jit(solution)/shard_map/ppermute | solution.py:574
  99.1 1.3 %finish.1 = (f32[256,512]{1,0:T(8,128)}, f32[512,256]{1,0:T(8,128)}, f32[1,256]{1,0:T(1,128)}, f32[256,128]{1,0:T(8,128)}) custom-call(s32[1]{0:T(128)} %bitcast.core_ref, bf16[64,24,128]{2,1,0:T(8,128)(2,1)S(1)} %all-to-all-done.2.mine_ref, bf16[64,24,128]{2,1,0:T(8,128)(2,1)S(1)} %collective-permute-done.4.other_ref, f32[256,1]{1,0:T(8,128)S(1)} %copy.27.gain_ref, ...), custom_call_target="tpu_custom_call" | custom-call | flops 524288 | bytes 3145728 | tf_op jit(solution)/shard_map/finish/pallas_call | solution.py:512
  (6 shorter events, 0.2 us)
Async XLA Ops:
  1.7 5.5 %collective-permute-start = (bf16[32,1,256]{2,1,0:T(2,128)(2,1)S(1)}, bf16[32,1,256]{2,1,0:T(2,128)(2,1)S(1)}, u32[]{:S(2)}, u32[]{:S(2)}) collective-permute-start(bf16[32,1,256]{2,1,0:T(2,128)(2,1)S(1)} %get-tuple-element.58), channel_id=1, source_target_pairs={{0,1},{1,2},{2,3},{3,4},{4,5},{5,6},{6,7},{7,8},{8,9},{9,10},{10,1... | collective-permute-start | bytes 49160 | tf_op jit(solution)/shard_map/ppermute | solution.py:533
  4.3 3.6 %collective-permute-start.1 = (bf16[32,1,256]{2,1,0:T(2,128)(2,1)S(1)}, bf16[32,1,256]{2,1,0:T(2,128)(2,1)S(1)}, u32[]{:S(2)}, u32[]{:S(2)}) collective-permute-start(bf16[32,1,256]{2,1,0:T(2,128)(2,1)S(1)} %get-tuple-element.57), channel_id=1, source_target_pairs={{1,0},{2,1},{3,2},{4,3},{5,4},{6,5},{7,6},{8,7},{9,8},{10,9},{11,1... | collective-permute-start | bytes 49160 | tf_op jit(solution)/shard_map/ppermute | solution.py:534
  7.1 7.2 %copy-start.1 = (bf16[256,512]{1,0:T(8,128)(2,1)S(1)}, bf16[256,512]{1,0:T(8,128)(2,1)}, u32[]{:S(2)}) copy-start(bf16[256,512]{1,0:T(8,128)(2,1)} %w_in_ref.3) | copy-start | bytes 786436
  7.1 7.3 %copy-start.2 = (bf16[256,128]{1,0:T(8,128)(2,1)S(1)}, bf16[256,128]{1,0:T(8,128)(2,1)}, u32[]{:S(2)}) copy-start(bf16[256,128]{1,0:T(8,128)(2,1)} %head_ref.1) | copy-start | bytes 196612
  7.1 7.5 %copy-start = (bf16[512,256]{1,0:T(8,128)(2,1)S(1)}, bf16[512,256]{1,0:T(8,128)(2,1)}, u32[]{:S(2)}) copy-start(bf16[512,256]{1,0:T(8,128)(2,1)} %w_out_ref.1) | copy-start | bytes 786436
  7.1 7.9 %copy-start.3 = (f32[256]{0:T(256)S(1)}, f32[256]{0:T(256)}, u32[]{:S(2)}) copy-start(f32[256]{0:T(256)} %param.16) | copy-start | bytes 3076
  7.1 7.9 %copy-start.4 = (bf16[32,128,256]{2,1,0:T(8,128)(2,1)S(1)}, bf16[32,128,256]{2,1,0:T(8,128)(2,1)}, u32[]{:S(2)}) copy-start(bf16[32,128,256]{2,1,0:T(8,128)(2,1)} %lat_ref.1) | copy-start | bytes 6291460
  8.0 34.8 %all-to-all-start = ((bf16[32,264,128]{2,1,0:T(8,128)(2,1)}), bf16[32,264,128]{2,1,0:T(8,128)(2,1)}, u32[]{:S(2)}, u32[]{:S(2)}) async-start(bf16[32,264,128]{2,1,0:T(8,128)(2,1)} %pack.1), calls=%async_computation | async-start | bytes 4325376 | tf_op jit(solution)/shard_map/all_to_all | solution.py:547
  15.0 27.8 %copy-start.5 = (s32[1,1,32]{2,1,0:T(1,128)S(1)}, s32[1,1,32]{2,1,0:T(1,128)}, u32[]{:S(2)}) copy-start(s32[1,1,32]{2,1,0:T(1,128)} %rows_ref.1) | copy-start | bytes 388
  24.8 0.7 copy-start.6
  42.8 0.9 copy-start.7
  54.1 2.0 %collective-permute-start.2 = (bf16[64,24,128]{2,1,0:T(8,128)(2,1)S(1)}, bf16[64,24,128]{2,1,0:T(8,128)(2,1)S(1)}, u32[]{:S(2)}, u32[]{:S(2)}) collective-permute-start(bf16[64,24,128]{2,1,0:T(8,128)(2,1)S(1)} %get-tuple-element.41), channel_id=1, source_target_pairs={{0,1},{1,0},{2,3},{3,2},{4,5},{5,4},{6,7},{7,6},{8,9},{9,8},{10,11... | collective-permute-start | bytes 1179656 | tf_op jit(solution)/shard_map/ppermute | solution.py:562
  57.0 21.4 %all-to-all-start.1 = ((bf16[64,24,128]{2,1,0:T(8,128)(2,1)}), bf16[64,24,128]{2,1,0:T(8,128)(2,1)S(1)}, u32[]{:S(2)}, u32[]{:S(2)}) async-start(bf16[64,24,128]{2,1,0:T(8,128)(2,1)} %get-tuple-element.42), calls=%async_computation.1 | async-start | bytes 786432 | tf_op jit(solution)/shard_map/all_to_all | solution.py:563
  67.3 6.9 %collective-permute-start.3 = (bf16[32,256]{1,0:T(8,128)(2,1)S(1)}, bf16[32,256]{1,0:T(8,128)(2,1)S(1)}, u32[]{:S(2)}, u32[]{:S(2)}) collective-permute-start(bf16[32,256]{1,0:T(8,128)(2,1)S(1)} %get-tuple-element.47), channel_id=1, source_target_pairs={{0,15},{1,2},{2,1},{3,4},{4,3},{5,6},{6,5},{7,8},{8,7},{9,10},{10,... | collective-permute-start | bytes 49160 | tf_op jit(solution)/shard_map/ppermute | solution.py:561
  79.2 16.3 %all-to-all-start.2 = ((bf16[64,24,128]{2,1,0:T(8,128)(2,1)}), bf16[64,24,128]{2,1,0:T(8,128)(2,1)S(1)}, u32[]{:S(2)}, u32[]{:S(2)}) async-start(bf16[64,24,128]{2,1,0:T(8,128)(2,1)} %total.1), calls=%async_computation.2 | async-start | bytes 786432 | tf_op jit(solution)/shard_map/all_to_all | solution.py:571
  95.5 3.6 %collective-permute-start.4 = (bf16[64,24,128]{2,1,0:T(8,128)(2,1)S(1)}, bf16[64,24,128]{2,1,0:T(8,128)(2,1)S(1)}, u32[]{:S(2)}, u32[]{:S(2)}) collective-permute-start(bf16[64,24,128]{2,1,0:T(8,128)(2,1)S(1)} %all-to-all-done.2.mine_ref), channel_id=1, source_target_pairs={{0,1},{1,0},{2,3},{3,2},{4,5},{5,4},{6,7},{7,6},{8,9},{9,8},{10,11... | collective-permute-start | bytes 1179656 | tf_op jit(solution)/shard_map/ppermute | solution.py:574

commit v9 on v8

--- a/solution.py
+++ b/solution.py
@@ -169,7 +169,7 @@
             pltpu.HBM((ch, n), bf16),
             pltpu.HBM((n, ch), bf16),
             pltpu.HBM((n, hid), bf16),
-            jax.ShapeDtypeStruct((4, rows, ch), f32),
+            pltpu.HBM((4, rows, ch), f32),
         ),
         in_specs=[
             pl.BlockSpec((ROWS_STEP, cells, ch), lambda i: (i, 0, 0)),
@@ -197,11 +197,11 @@
 
 
 def decode_kernel(
-    core_ref, rows_ref, got_hbm, shown_hbm, head_t_ref, joint_ref, w_out_t_ref, w_in_t_ref, gain_ref, ends_ref,
-    slope_hbm, act_t_hbm, xhat_t_hbm, lat_t_hbm,
+    core_ref, rows_ref, got_hbm, shown_hbm, head_t_ref, joint_ref, w_out_t_ref, w_in_t_ref, gain_ref,
+    ends_hbm, slope_hbm, act_t_hbm, xhat_t_hbm, lat_t_hbm,
     q_hbm, keep_ref, send_ref, outer_ref,
-    got, shown, slope, act_t, xhat_t, lat_t, q_all, ends, acc_q, acc_head, acc_in, acc_act,
-    got_sems, shown_sems, in_sems, q_sems,
+    got, shown, slope, act_t, xhat_t, lat_t, q_all, ends_ref, ends, acc_q, acc_head, acc_in, acc_act,
+    got_sems, shown_sems, in_sems, q_sems, ends_sem,
 ):
     nb, nr = BLOCKS_STEP, PULL_ROWS
     blocks = got.shape[0]
@@ -236,6 +236,8 @@
 
     for i in range(AHEAD):
         start(i)
+    ends_copy = pltpu.make_async_copy(ends_hbm, ends_ref, ends_sem.at[0])
+    ends_copy.start()
     for acc in (acc_q, acc_head, acc_in, acc_act):
         acc[...] = jnp.zeros_like(acc)
 
@@ -292,6 +294,7 @@
         return carry
 
     lax.fori_loop(0, rows // nr, pull, 0)
+    ends_copy.wait()
     by_hidden = acc_act[...].astype(bf16)
     out_sum = dot(by_hidden, head_t_ref[...])
     head_sum = (acc_head[...] + dot(w_out_t_ref[...], by_hidden)).T
@@ -366,11 +369,12 @@
             jax.ShapeDtypeStruct((chunks, 24, 128), bf16),
             jax.ShapeDtypeStruct((nrow, ch), bf16),
         ),
-        in_specs=[scalars] * 2 + [OUTSIDE] * 2 + [INSIDE] * 6 + [OUTSIDE] * 4,
+        in_specs=[scalars] * 2 + [OUTSIDE] * 2 + [INSIDE] * 5 + [OUTSIDE] * 5,
         out_specs=(OUTSIDE,) + (INSIDE,) * 3,
         scratch_shapes=[pltpu.VMEM(x.shape, bf16) for x in (got, shown, slope, act_t, xhat_t, lat_t)]
         + [
             pltpu.VMEM((n, 2 * nv), bf16),
+            pltpu.VMEM(ends.shape, f32),
             pltpu.VMEM((2, nrow, hid), f32),
             pltpu.VMEM((nrow, cells, 2 * nv), f32),
             pltpu.VMEM((ch, nv), f32),
@@ -380,11 +384,12 @@
             dma((blocks,)),
             dma((4, nrow // PULL_ROWS)),
             dma((nrow // PULL_ROWS,)),
+            dma((1,)),
         ],
         compiler_params=params(),
         cost_estimate=cost(10 * n * ch * hid, 24 * 2**20),
         name="decode",
-    )(core, rows, *in_hbm(got, shown), head_t, joint, w_out_t, w_in_t, gain, ends, *in_hbm(slope, act_t, xhat_t, lat_t))
+    )(core, rows, *in_hbm(got, shown), head_t, joint, w_out_t, w_in_t, gain, *in_hbm(ends, slope, act_t, xhat_t, lat_t))
 
 
 def backward_kernel(

time: 101 us -> 99.9 us (0.989)
  local copies, waits for them, and re-layouts: 3.21 us -> 1.65 us
    unnamed x19 -> x15, local copies, waits for them, and re-layouts: 1.97 us -> 0.42 us
where the time goes in v9:
time: 99.9 us; the launch traced here: 99.5 us
  Pallas kernels  37.4 us (37%)
  starting transfers between devices  29.7 us (30%)
  waiting for transfers between devices  29.6 us (30%)
  local copies, waits for them, and re-layouts  1.65 us (2%)
    all_to_all x1, waiting for transfers between devices, body(): got = lax.all_to_all(packed, LON, 0, 0, tiled=True)  18 us
    pallas_call x1, Pallas kernels, decode(): pl.pallas_call(decode_kernel, out_shape=(pltpu.HBM((n, 2 * nv), bf16), ja...  10.4 us
    all_to_all x1, starting transfers between devices, body(): parts = lax.all_to_all(summed, chips, 0, 0, tiled=True)  10.3 us
    pallas_call x2, Pallas kernels, backward(): pl.pallas_call(backward_kernel, grid=((end - begin) // nr,), out_shape=pl...  9.88 us
    pallas_call x1, Pallas kernels, forward(): pl.pallas_call(forward_kernel, grid=(rows // ROWS_STEP,), out_shape=(pltp...  9.75 us
    all_to_all x1, starting transfers between devices, body(): got = lax.all_to_all(packed, LON, 0, 0, tiled=True)  6.32 us
    all_to_all x1, starting transfers between devices, body(): mine = lax.all_to_all(total(parts), chips, 0, 0, tiled=True)  5.57 us
    all_to_all x1, waiting for transfers between devices, body(): parts = lax.all_to_all(summed, chips, 0, 0, tiled=True)  4.16 us
  transfers between devices with their start and end apart: 8, of which 6 were waited for; matrix products, arithmetic and copies ran while one was open for 1% of the time, Pallas kernels for 24%

profile of v9, /device:TPU:1, one launch (start us, length us, event | category | flops | bytes accessed | tf_op | source)
XLA Modules:
  0.0 99.5 jit_solution(430490067752665805)
XLA Ops:
  0.6 1.0 %fusion = (bf16[32,1,256]{2,1,0:T(2,128)(2,1)S(1)}, bf16[32,1,256]{2,1,0:T(2,128)(2,1)S(1)}) fusion(bf16[32,128,256]{2,1,0:T(8,128)(2,1)} %lat_ref.1), kind=kLoop, calls=%fused_computation.3 | loop fusion | bytes 65536 | tf_op jit(solution)/shard_map/slice | solution.py:550
  1.7 2.7 %collective-permute-start = (bf16[32,1,256]{2,1,0:T(2,128)(2,1)S(1)}, bf16[32,1,256]{2,1,0:T(2,128)(2,1)S(1)}, u32[]{:S(2)}, u32[]{:S(2)}) collective-permute-start(bf16[32,1,256]{2,1,0:T(2,128)(2,1)S(1)} %get-tuple-element.58), channel_id=1, source_target_pairs={{0,1},{1,2},{2,3},{3,4},{4,5},{5,6},{6,7},{7,8},{8,9},{9,10},{10,1... | collective-permute-start | bytes 49160 | tf_op jit(solution)/shard_map/ppermute | solution.py:538
  4.3 0.0 collective-permute-start.1
  4.3 2.7 %pack.1 = bf16[32,264,128]{2,1,0:T(8,128)(2,1)} custom-call(bf16[32,128,128]{2,1,0:T(8,128)(2,1)} %w_hbm.1, bf16[32,128,128]{2,1,0:T(8,128)(2,1)} %t_hbm.1, s32[32,128]{1,0:T(8,128)} %slot_hbm.1, s32[32]{0:T(128)} %count_hbm.1), custom_call_target="tpu_custom_call" | custom-call | flops 1 | bytes 4194304 | tf_op jit(solution)/shard_map/pack/pallas_call | solution.py:91
  7.1 0.0 copy-start.1
  7.1 0.0 copy-start.2
  7.1 0.0 copy-start
  7.1 0.0 copy-start.3
  7.1 0.0 copy-start.4
  7.1 0.0 collective-permute-done
  7.1 0.8 collective-permute-done.1
  8.0 6.3 %all-to-all-start = ((bf16[32,264,128]{2,1,0:T(8,128)(2,1)}), bf16[32,264,128]{2,1,0:T(8,128)(2,1)}, u32[]{:S(2)}, u32[]{:S(2)}) async-start(bf16[32,264,128]{2,1,0:T(8,128)(2,1)} %pack.1), calls=%async_computation | async-start | bytes 4325376 | tf_op jit(solution)/shard_map/all_to_all | solution.py:552
  14.3 0.0 copy-done.1
  14.3 0.1 copy.24
  14.4 0.0 copy-done.2
  14.4 0.1 copy.22
  14.6 0.0 copy-done
  14.6 0.1 copy.23
  14.7 0.2 convolution_convert_fusion.joint_ref
  15.0 0.0 copy-done.3
  15.0 0.0 copy-done.4
  15.0 0.0 copy-start.5
  15.1 9.8 %forward.1 = (bf16[32,256,128]{2,1,0:T(8,128)(2,1)}, bf16[256,4096]{1,0:T(8,128)(2,1)}, bf16[4096,512]{1,0:T(8,128)(2,1)}, bf16[512,4096]{1,0:T(8,128)(2,1)}, bf...) custom-call(bf16[32,128,256]{2,1,0:T(8,128)(2,1)S(1)} %copy-done.4, ...), custom_call_target="tpu_custom_call" | custom-call | flops 2147483648 | bytes 16777216 | tf_op jit(solution)/shard_map/forward/pallas_call | solution.py:161
  24.8 18.0 %all-to-all-done.got_hbm = bf16[32,264,128]{2,1,0:T(8,128)(2,1)} async-done(((bf16[32,264,128]{2,1,0:T(8,128)(2,1)}), bf16[32,264,128]{2,1,0:T(8,128)(2,1)}, u32[]{:S(2)}, u32[]{:S(2)}) %all-to-all-start) | async-done | bytes 2162720 | tf_op jit(solution)/shard_map/all_to_all | solution.py:552
  42.8 0.0 copy-done.5
  42.8 10.4 %decode.1 = (bf16[4096,256]{1,0:T(8,128)(2,1)}, f32[64,24,128]{2,1,0:T(8,128)S(1)}, bf16[64,24,128]{2,1,0:T(8,128)(2,1)S(1)}, bf16[32,256]{1,0:T(8,128)(2,1)S(1)}) custom-call(s32[1]{0:T(128)} %bitcast.core_ref, s32[1,1,32]{2,1,0:T(1,128)S(1)} %copy-done.5, bf16[32,264,128]{2,1,0:T(8,128)(2,1)} %all-to-all-done.got_hbm, ...), custom_call_target="tpu_custom_call" | custom-call | flops 5368709120 | bytes 25165824 | tf_op jit(solution)/shard_map/decode/pallas_call | solution.py:364
  53.2 0.7 collective-permute-start.2
  53.9 1.3 %collective-permute-done.2.came_ref = bf16[64,24,128]{2,1,0:T(8,128)(2,1)S(1)} collective-permute-done((bf16[64,24,128]{2,1,0:T(8,128)(2,1)S(1)}, bf16[64,24,128]{2,1,0:T(8,128)(2,1)S(1)}, u32[]{:S(2)}, u32[]{:S(2)}) %collective-permute-start.2) | collective-permute-done | bytes 393248 | tf_op jit(solution)/shard_map/ppermute | solution.py:567
  55.2 0.8 pair.1
  56.1 10.3 %all-to-all-start.1 = ((bf16[64,24,128]{2,1,0:T(8,128)(2,1)}), bf16[64,24,128]{2,1,0:T(8,128)(2,1)S(1)}, u32[]{:S(2)}, u32[]{:S(2)}) async-start(bf16[64,24,128]{2,1,0:T(8,128)(2,1)} %get-tuple-element.42), calls=%async_computation.1 | async-start | bytes 786432 | tf_op jit(solution)/shard_map/all_to_all | solution.py:568
  66.4 1.9 %collective-permute-start.3 = (bf16[32,256]{1,0:T(8,128)(2,1)S(1)}, bf16[32,256]{1,0:T(8,128)(2,1)S(1)}, u32[]{:S(2)}, u32[]{:S(2)}) collective-permute-start(bf16[32,256]{1,0:T(8,128)(2,1)S(1)} %get-tuple-element.47), channel_id=1, source_target_pairs={{0,15},{1,2},{2,1},{3,4},{4,3},{5,6},{6,5},{7,8},{8,7},{9,10},{10,... | collective-permute-start | bytes 49160 | tf_op jit(solution)/shard_map/ppermute | solution.py:566
  68.4 4.9 %backward.2.rest_0_ = f32[32,128,256]{2,1,0:T(8,128)} custom-call(f32[32,1,256]{2,1,0:T(1,128)S(1)} %copy.25.left_ref, f32[32,1,256]{2,1,0:T(1,128)S(1)} %broadcast_in_dim.33.right_ref, f32[1,256]{1,0:T(1,128)S(1)} %bitcast.22, bf16[512,256]{1,0:T(8,128)(2,1)S(1)} %bitcast.14, bf16[128,512]{1,0:T(8,128)(2,1)S(1)} %convolution_convert_fusion.joint_ref, ...), custom_call_target="tpu_custom_call" | custom-call | flops 1073741824 | bytes 7340032 | tf_op jit(solution)/shard_map/backward/pallas_call | solution.py:419
  73.3 0.0 collective-permute-done.3
  73.3 4.2 %all-to-all-done.1.got_ref = bf16[64,24,128]{2,1,0:T(8,128)(2,1)S(1)} async-done(((bf16[64,24,128]{2,1,0:T(8,128)(2,1)}), bf16[64,24,128]{2,1,0:T(8,128)(2,1)S(1)}, u32[]{:S(2)}, u32[]{:S(2)}) %all-to-all-start.1) | async-done | bytes 393248 | tf_op jit(solution)/shard_map/all_to_all | solution.py:568
  77.5 0.8 total.1
  78.3 5.6 %all-to-all-start.2 = ((bf16[64,24,128]{2,1,0:T(8,128)(2,1)}), bf16[64,24,128]{2,1,0:T(8,128)(2,1)S(1)}, u32[]{:S(2)}, u32[]{:S(2)}) async-start(bf16[64,24,128]{2,1,0:T(8,128)(2,1)} %total.1), calls=%async_computation.2 | async-start | bytes 786432 | tf_op jit(solution)/shard_map/all_to_all | solution.py:576
  83.9 4.9 %backward.3.grad_ref = f32[32,128,256]{2,1,0:T(8,128)} custom-call(f32[32,1,256]{2,1,0:T(1,128)S(1)} %copy.25.left_ref, f32[32,1,256]{2,1,0:T(1,128)S(1)} %broadcast_in_dim.33.right_ref, f32[1,256]{1,0:T(1,128)S(1)} %bitcast.23, bf16[512,256]{1,0:T(8,128)(2,1)S(1)} %bitcast.15, ...), custom_call_target="tpu_custom_call", output_to_operand_aliasing={{}: (9, {})} | custom-call | flops 1073741824 | bytes 7340032 | tf_op jit(solution)/shard_map/backward/pallas_call | solution.py:419
  88.9 1.7 %edge.1 = f32[32,128,256]{2,1,0:T(8,128)} custom-call(s32[1]{0:T(128)} %bitcast.core_ref, f32[32,1,256]{2,1,0:T(1,128)S(1)} %reshape.28.outer_ref, f32[32,128,256]{2,1,0:T(8,128)} %backward.3.grad_ref), custom_call_target="tpu_custom_call", output_to_operand_aliasing={{}: (2, {})} | custom-call | flops 65536 | bytes 524288 | tf_op jit(solution)/shard_map/edge/pallas_call | solution.py:452
  90.6 4.1 %all-to-all-done.2.mine_ref = bf16[64,24,128]{2,1,0:T(8,128)(2,1)S(1)} async-done(((bf16[64,24,128]{2,1,0:T(8,128)(2,1)}), bf16[64,24,128]{2,1,0:T(8,128)(2,1)S(1)}, u32[]{:S(2)}, u32[]{:S(2)}) %all-to-all-start.2) | async-done | bytes 393248 | tf_op jit(solution)/shard_map/all_to_all | solution.py:576
  94.6 2.2 %collective-permute-start.4 = (bf16[64,24,128]{2,1,0:T(8,128)(2,1)S(1)}, bf16[64,24,128]{2,1,0:T(8,128)(2,1)S(1)}, u32[]{:S(2)}, u32[]{:S(2)}) collective-permute-start(bf16[64,24,128]{2,1,0:T(8,128)(2,1)S(1)} %all-to-all-done.2.mine_ref), channel_id=1, source_target_pairs={{0,1},{1,0},{2,3},{3,2},{4,5},{5,4},{6,7},{7,6},{8,9},{9,8},{10,11... | collective-permute-start | bytes 1179656 | tf_op jit(solution)/shard_map/ppermute | solution.py:579
  96.8 0.1 copy.27.gain_ref
  97.0 1.2 %collective-permute-done.4.other_ref = bf16[64,24,128]{2,1,0:T(8,128)(2,1)S(1)} collective-permute-done((bf16[64,24,128]{2,1,0:T(8,128)(2,1)S(1)}, bf16[64,24,128]{2,1,0:T(8,128)(2,1)S(1)}, u32[]{:S(2)}, u32[]{:S(2)}) %collective-permute-start.4) | collective-permute-done | bytes 393248 | tf_op jit(solution)/shard_map/ppermute | solution.py:579
  98.2 1.3 %finish.1 = (f32[256,512]{1,0:T(8,128)}, f32[512,256]{1,0:T(8,128)}, f32[1,256]{1,0:T(1,128)}, f32[256,128]{1,0:T(8,128)}) custom-call(s32[1]{0:T(128)} %bitcast.core_ref, bf16[64,24,128]{2,1,0:T(8,128)(2,1)S(1)} %all-to-all-done.2.mine_ref, bf16[64,24,128]{2,1,0:T(8,128)(2,1)S(1)} %collective-permute-done.4.other_ref, f32[256,1]{1,0:T(8,128)S(1)} %copy.27.gain_ref, ...), custom_call_target="tpu_custom_call" | custom-call | flops 524288 | bytes 3145728 | tf_op jit(solution)/shard_map/finish/pallas_call | solution.py:517
  (6 shorter events, 0.2 us)
Async XLA Ops:
  1.7 5.5 %collective-permute-start = (bf16[32,1,256]{2,1,0:T(2,128)(2,1)S(1)}, bf16[32,1,256]{2,1,0:T(2,128)(2,1)S(1)}, u32[]{:S(2)}, u32[]{:S(2)}) collective-permute-start(bf16[32,1,256]{2,1,0:T(2,128)(2,1)S(1)} %get-tuple-element.58), channel_id=1, source_target_pairs={{0,1},{1,2},{2,3},{3,4},{4,5},{5,6},{6,7},{7,8},{8,9},{9,10},{10,1... | collective-permute-start | bytes 49160 | tf_op jit(solution)/shard_map/ppermute | solution.py:538
  4.3 3.6 %collective-permute-start.1 = (bf16[32,1,256]{2,1,0:T(2,128)(2,1)S(1)}, bf16[32,1,256]{2,1,0:T(2,128)(2,1)S(1)}, u32[]{:S(2)}, u32[]{:S(2)}) collective-permute-start(bf16[32,1,256]{2,1,0:T(2,128)(2,1)S(1)} %get-tuple-element.57), channel_id=1, source_target_pairs={{1,0},{2,1},{3,2},{4,3},{5,4},{6,5},{7,6},{8,7},{9,8},{10,9},{11,1... | collective-permute-start | bytes 49160 | tf_op jit(solution)/shard_map/ppermute | solution.py:539
  7.1 7.2 %copy-start.1 = (bf16[256,512]{1,0:T(8,128)(2,1)S(1)}, bf16[256,512]{1,0:T(8,128)(2,1)}, u32[]{:S(2)}) copy-start(bf16[256,512]{1,0:T(8,128)(2,1)} %w_in_ref.3) | copy-start | bytes 786436
  7.1 7.3 %copy-start.2 = (bf16[256,128]{1,0:T(8,128)(2,1)S(1)}, bf16[256,128]{1,0:T(8,128)(2,1)}, u32[]{:S(2)}) copy-start(bf16[256,128]{1,0:T(8,128)(2,1)} %head_ref.1) | copy-start | bytes 196612
  7.1 7.5 %copy-start = (bf16[512,256]{1,0:T(8,128)(2,1)S(1)}, bf16[512,256]{1,0:T(8,128)(2,1)}, u32[]{:S(2)}) copy-start(bf16[512,256]{1,0:T(8,128)(2,1)} %w_out_ref.1) | copy-start | bytes 786436
  7.1 7.9 %copy-start.3 = (f32[256]{0:T(256)S(1)}, f32[256]{0:T(256)}, u32[]{:S(2)}) copy-start(f32[256]{0:T(256)} %param.16) | copy-start | bytes 3076
  7.1 7.9 %copy-start.4 = (bf16[32,128,256]{2,1,0:T(8,128)(2,1)S(1)}, bf16[32,128,256]{2,1,0:T(8,128)(2,1)}, u32[]{:S(2)}) copy-start(bf16[32,128,256]{2,1,0:T(8,128)(2,1)} %lat_ref.1) | copy-start | bytes 6291460
  8.0 34.8 %all-to-all-start = ((bf16[32,264,128]{2,1,0:T(8,128)(2,1)}), bf16[32,264,128]{2,1,0:T(8,128)(2,1)}, u32[]{:S(2)}, u32[]{:S(2)}) async-start(bf16[32,264,128]{2,1,0:T(8,128)(2,1)} %pack.1), calls=%async_computation | async-start | bytes 4325376 | tf_op jit(solution)/shard_map/all_to_all | solution.py:552
  15.0 27.8 %copy-start.5 = (s32[1,1,32]{2,1,0:T(1,128)S(1)}, s32[1,1,32]{2,1,0:T(1,128)}, u32[]{:S(2)}) copy-start(s32[1,1,32]{2,1,0:T(1,128)} %rows_ref.1) | copy-start | bytes 388
  53.2 2.0 %collective-permute-start.2 = (bf16[64,24,128]{2,1,0:T(8,128)(2,1)S(1)}, bf16[64,24,128]{2,1,0:T(8,128)(2,1)S(1)}, u32[]{:S(2)}, u32[]{:S(2)}) collective-permute-start(bf16[64,24,128]{2,1,0:T(8,128)(2,1)S(1)} %get-tuple-element.41), channel_id=1, source_target_pairs={{0,1},{1,0},{2,3},{3,2},{4,5},{5,4},{6,7},{7,6},{8,9},{9,8},{10,11... | collective-permute-start | bytes 1179656 | tf_op jit(solution)/shard_map/ppermute | solution.py:567
  56.1 21.4 %all-to-all-start.1 = ((bf16[64,24,128]{2,1,0:T(8,128)(2,1)}), bf16[64,24,128]{2,1,0:T(8,128)(2,1)S(1)}, u32[]{:S(2)}, u32[]{:S(2)}) async-start(bf16[64,24,128]{2,1,0:T(8,128)(2,1)} %get-tuple-element.42), calls=%async_computation.1 | async-start | bytes 786432 | tf_op jit(solution)/shard_map/all_to_all | solution.py:568
  66.4 6.9 %collective-permute-start.3 = (bf16[32,256]{1,0:T(8,128)(2,1)S(1)}, bf16[32,256]{1,0:T(8,128)(2,1)S(1)}, u32[]{:S(2)}, u32[]{:S(2)}) collective-permute-start(bf16[32,256]{1,0:T(8,128)(2,1)S(1)} %get-tuple-element.47), channel_id=1, source_target_pairs={{0,15},{1,2},{2,1},{3,4},{4,3},{5,6},{6,5},{7,8},{8,7},{9,10},{10,... | collective-permute-start | bytes 49160 | tf_op jit(solution)/shard_map/ppermute | solution.py:566
  78.3 16.3 %all-to-all-start.2 = ((bf16[64,24,128]{2,1,0:T(8,128)(2,1)}), bf16[64,24,128]{2,1,0:T(8,128)(2,1)S(1)}, u32[]{:S(2)}, u32[]{:S(2)}) async-start(bf16[64,24,128]{2,1,0:T(8,128)(2,1)} %total.1), calls=%async_computation.2 | async-start | bytes 786432 | tf_op jit(solution)/shard_map/all_to_all | solution.py:576
  94.6 3.6 %collective-permute-start.4 = (bf16[64,24,128]{2,1,0:T(8,128)(2,1)S(1)}, bf16[64,24,128]{2,1,0:T(8,128)(2,1)S(1)}, u32[]{:S(2)}, u32[]{:S(2)}) collective-permute-start(bf16[64,24,128]{2,1,0:T(8,128)(2,1)S(1)} %all-to-all-done.2.mine_ref), channel_id=1, source_target_pairs={{0,1},{1,0},{2,3},{3,2},{4,5},{5,4},{6,7},{7,6},{8,9},{9,8},{10,11... | collective-permute-start | bytes 1179656 | tf_op jit(solution)/shard_map/ppermute | solution.py:579

commit v10 on v9

--- a/solution.py
+++ b/solution.py
@@ -45,13 +45,18 @@
     return pl.CostEstimate(flops=flops, bytes_accessed=nbytes, transcendentals=trans)
 
 
-def pack_kernel(w_hbm, t_hbm, slot_hbm, count_hbm, out_hbm, buf, slots, counts, small_sems, in_sems, out_sems):
+def pack_kernel(
+    w_hbm, t_hbm, slot_hbm, count_hbm, lat_hbm, out_hbm, first_ref, last_ref,
+    buf, slots, counts, ends, small_sems, in_sems, out_sems,
+):
     blocks, obs = slots.shape
     nv = t_hbm.shape[1]
     n = blocks // PACK_CHUNKS
     small = [
         pltpu.make_async_copy(slot_hbm, slots, small_sems.at[0]),
         pltpu.make_async_copy(count_hbm, counts, small_sems.at[1]),
+        pltpu.make_async_copy(lat_hbm.at[:, pl.ds(0, 8), :], ends.at[0], small_sems.at[2]),
+        pltpu.make_async_copy(lat_hbm.at[:, pl.ds(lat_hbm.shape[1] - 8, 8), :], ends.at[1], small_sems.at[3]),
     ]
     arrive, leave = [], []
     for c in range(PACK_CHUNKS):
@@ -76,6 +81,8 @@
     for b in range(blocks):
         live = jnp.where(lane < counts[b], 1.0, 0.0)
         buf[b, obs + nv : obs + nv + META, :] = jnp.where(row == 0, coef[b : b + 1, :], live).astype(bf16)
+    first_ref[...] = ends[0].astype(f32)[:, 0, :].astype(bf16)
+    last_ref[...] = ends[1].astype(f32)[:, 7, :].astype(bf16)
     for pair, out in zip(arrive, leave):
         for c in pair:
             c.wait()
@@ -84,27 +91,30 @@
         c.wait()
 
 
-def pack(weights, targets, slots, counts):
+def pack(weights, targets, slots, counts, latent):
     blocks, obs, cells = weights.shape
     shape = (blocks, 2 * obs + META, cells)
+    rows, _, ch = latent.shape
+    edge = jax.ShapeDtypeStruct((rows, ch), bf16)
     dma = pltpu.SemaphoreType.DMA
     return pl.pallas_call(
         pack_kernel,
-        out_shape=pltpu.HBM(shape, bf16),
-        in_specs=[OUTSIDE] * 4,
-        out_specs=OUTSIDE,
+        out_shape=(pltpu.HBM(shape, bf16), edge, edge),
+        in_specs=[OUTSIDE] * 5,
+        out_specs=(OUTSIDE, INSIDE, INSIDE),
         scratch_shapes=[
             pltpu.VMEM(shape, bf16),
             pltpu.VMEM(slots.shape, jnp.int32),
             pltpu.SMEM(counts.shape, jnp.int32),
-            dma((2,)),
+            pltpu.VMEM((2, rows, 8, ch), bf16),
+            dma((4,)),
             dma((2 * PACK_CHUNKS,)),
             dma((PACK_CHUNKS,)),
         ],
         compiler_params=params(),
         cost_estimate=cost(1, 4 * 2**20),
         name="pack",
-    )(*in_hbm(weights, targets, slots, counts))
+    )(*in_hbm(weights, targets, slots, counts, latent))
 
 
 def mixed(x, left, right):
@@ -545,12 +555,11 @@
     swap = [(0, 1), (1, 0)]
     groups = lax.axis_size("band") * lax.axis_size("chip")
     core = lax.axis_index("core").astype(jnp.int32).reshape(1)
-    cells = latent.shape[1]
-    packed = pack(weights, targets, slots, counts)
-    left, right = from_sides(latent[:, 0:1, :], latent[:, cells - 1 : cells, :])
+    packed, first, last = pack(weights, targets, slots, counts, latent)
+    left, right = from_sides(first, last)
     packed, left, right = lax.optimization_barrier((packed, left, right))
     got = lax.all_to_all(packed, LON, 0, 0, tiled=True)
-    left, right = left.astype(f32), right.astype(f32)
+    left, right = left.astype(f32)[:, None, :], right.astype(f32)[:, None, :]
     gain_row = gain.reshape(1, -1)
     w_out_t = w_out.T
     w_in_t = w_in.T

time: 99.9 us -> 102 us (1.021)
  waiting for transfers between devices: 29.6 us -> 32.3 us
    ppermute x1, waiting for transfers between devices: 0.83 us -> 2.59 us  [from_sides(): lax.ppermute(first, LON, [((i + 1) % count, i) for i in range(count)])]
    slice x1 -> x0, local copies, waits for them, and re-layouts: 1.03 us -> none  [body(): left, right = from_sides(latent[:, 0:1, :], latent[:, cells - 1:cells, :])]
  transfers between devices with their start and end apart: 8 -> 8, of which waited for: 6 -> 7; matrix products, arithmetic and copies ran while one was open for 1% -> 1% of each run, Pallas kernels for 24% -> 21%
where the time goes in v10:
time: 102 us
  Pallas kernels  37.8 us (37%)
  waiting for transfers between devices  32.3 us (32%)
  starting transfers between devices  29.8 us (29%)
    all_to_all x1, waiting for transfers between devices, body(): got = lax.all_to_all(packed, LON, 0, 0, tiled=True)  18 us
    pallas_call x1, Pallas kernels, decode(): pl.pallas_call(decode_kernel, out_shape=(pltpu.HBM((n, 2 * nv), bf16), ja...  10.4 us
    all_to_all x1, starting transfers between devices, body(): parts = lax.all_to_all(summed, chips, 0, 0, tiled=True)  10.1 us
    pallas_call x2, Pallas kernels, backward(): pl.pallas_call(backward_kernel, grid=((end - begin) // nr,), out_shape=pl...  9.88 us
    pallas_call x1, Pallas kernels, forward(): pl.pallas_call(forward_kernel, grid=(rows // ROWS_STEP,), out_shape=(pltp...  9.75 us
    all_to_all x1, starting transfers between devices, body(): got = lax.all_to_all(packed, LON, 0, 0, tiled=True)  6.59 us
    all_to_all x1, starting transfers between devices, body(): mine = lax.all_to_all(total(parts), chips, 0, 0, tiled=True)  5.56 us
    all_to_all x1, waiting for transfers between devices, body(): parts = lax.all_to_all(summed, chips, 0, 0, tiled=True)  4.16 us
  transfers between devices with their start and end apart: 8, of which 7 were waited for; matrix products, arithmetic and copies ran while one was open for 1% of the time, Pallas kernels for 21%

profile of v10, /device:TPU:1, one launch (start us, length us, event | category | flops | bytes accessed | tf_op | source)
XLA Modules:
  0.0 101.5 jit_solution(8864217182995450218)
XLA Ops:
  0.6 3.1 %pack.1 = (bf16[32,264,128]{2,1,0:T(8,128)(2,1)}, bf16[32,256]{1,0:T(8,128)(2,1)S(1)}, bf16[32,256]{1,0:T(8,128)(2,1)S(1)}) custom-call(bf16[32,128,128]{2,1,0:T(8,128)(2,1)} %w_hbm.1, bf16[32,128,128]{2,1,0:T(8,128)(2,1)} %t_hbm.1, s32[32,128]{1,0:T(8,128)} %slot_hbm.1, s32[32]{0:T(128)} %count_hbm.1, bf16[32,128,256]{2,1,0:T(8,128)(2,1)} %lat_ref.1), custom_call_target="tpu_custom_call" | custom-call | flops 1 | bytes 4194304 | tf_op jit(solution)/shard_map/pack/pallas_call | solution.py:100
  3.8 2.7 %collective-permute-start = (bf16[32,256]{1,0:T(8,128)(2,1)S(1)}, bf16[32,256]{1,0:T(8,128)(2,1)S(1)}, u32[]{:S(2)}, u32[]{:S(2)}) collective-permute-start(bf16[32,256]{1,0:T(8,128)(2,1)S(1)} %get-tuple-element.35), channel_id=1, source_target_pairs={{0,1},{1,2},{2,3},{3,4},{4,5},{5,6},{6,7},{7,8},{8,9},{9,10},{10,1... | collective-permute-start | bytes 49160 | tf_op jit(solution)/shard_map/ppermute | solution.py:548
  6.4 0.0 collective-permute-start.1
  6.4 0.9 collective-permute-done
  7.3 2.6 %collective-permute-done.1 = bf16[32,256]{1,0:T(8,128)(2,1)S(1)} collective-permute-done((bf16[32,256]{1,0:T(8,128)(2,1)S(1)}, bf16[32,256]{1,0:T(8,128)(2,1)S(1)}, u32[]{:S(2)}, u32[]{:S(2)}) %collective-permute-start.1) | collective-permute-done | bytes 16416 | tf_op jit(solution)/shard_map/ppermute | solution.py:549
  9.9 0.0 copy-start.2
  9.9 0.0 copy-start.3
  9.9 0.0 copy-start.1
  9.9 0.0 copy-start
  9.9 0.0 copy-start.4
  9.9 6.6 %all-to-all-start = ((bf16[32,264,128]{2,1,0:T(8,128)(2,1)}), bf16[32,264,128]{2,1,0:T(8,128)(2,1)}, u32[]{:S(2)}, u32[]{:S(2)}) async-start(bf16[32,264,128]{2,1,0:T(8,128)(2,1)} %get-tuple-element.37), calls=%async_computation | async-start | bytes 4325376 | tf_op jit(solution)/shard_map/all_to_all | solution.py:561
  16.5 0.0 copy-done.2
  16.5 0.1 copy.24
  16.7 0.0 copy-done.3
  16.7 0.1 copy.22
  16.8 0.0 copy-done.1
  16.8 0.1 copy.23
  16.9 0.2 convolution_convert_fusion.joint_ref
  17.2 0.0 copy-done
  17.2 0.0 copy-done.4
  17.2 0.0 copy-start.5
  17.3 9.8 %forward.1 = (bf16[32,256,128]{2,1,0:T(8,128)(2,1)}, bf16[256,4096]{1,0:T(8,128)(2,1)}, bf16[4096,512]{1,0:T(8,128)(2,1)}, bf16[512,4096]{1,0:T(8,128)(2,1)}, bf...) custom-call(bf16[32,128,256]{2,1,0:T(8,128)(2,1)S(1)} %copy-done, ...), custom_call_target="tpu_custom_call" | custom-call | flops 2147483648 | bytes 16777216 | tf_op jit(solution)/shard_map/forward/pallas_call | solution.py:171
  27.0 18.0 %all-to-all-done.got_hbm = bf16[32,264,128]{2,1,0:T(8,128)(2,1)} async-done(((bf16[32,264,128]{2,1,0:T(8,128)(2,1)}), bf16[32,264,128]{2,1,0:T(8,128)(2,1)}, u32[]{:S(2)}, u32[]{:S(2)}) %all-to-all-start) | async-done | bytes 2162720 | tf_op jit(solution)/shard_map/all_to_all | solution.py:561
  45.0 0.0 copy-done.5
  45.0 10.4 %decode.1 = (bf16[4096,256]{1,0:T(8,128)(2,1)}, f32[64,24,128]{2,1,0:T(8,128)S(1)}, bf16[64,24,128]{2,1,0:T(8,128)(2,1)S(1)}, bf16[32,256]{1,0:T(8,128)(2,1)S(1)}) custom-call(s32[1]{0:T(128)} %bitcast.core_ref, s32[1,1,32]{2,1,0:T(1,128)S(1)} %copy-done.5, bf16[32,264,128]{2,1,0:T(8,128)(2,1)} %all-to-all-done.got_hbm, ...), custom_call_target="tpu_custom_call" | custom-call | flops 5368709120 | bytes 25165824 | tf_op jit(solution)/shard_map/decode/pallas_call | solution.py:374
  55.5 0.7 collective-permute-start.2
  56.1 1.3 %collective-permute-done.2.came_ref = bf16[64,24,128]{2,1,0:T(8,128)(2,1)S(1)} collective-permute-done((bf16[64,24,128]{2,1,0:T(8,128)(2,1)S(1)}, bf16[64,24,128]{2,1,0:T(8,128)(2,1)S(1)}, u32[]{:S(2)}, u32[]{:S(2)}) %collective-permute-start.2) | collective-permute-done | bytes 393248 | tf_op jit(solution)/shard_map/ppermute | solution.py:576
  57.5 0.8 pair.1
  58.3 10.1 %all-to-all-start.1 = ((bf16[64,24,128]{2,1,0:T(8,128)(2,1)}), bf16[64,24,128]{2,1,0:T(8,128)(2,1)S(1)}, u32[]{:S(2)}, u32[]{:S(2)}) async-start(bf16[64,24,128]{2,1,0:T(8,128)(2,1)} %get-tuple-element.48), calls=%async_computation.1 | async-start | bytes 786432 | tf_op jit(solution)/shard_map/all_to_all | solution.py:577
  68.4 1.9 %collective-permute-start.3 = (bf16[32,256]{1,0:T(8,128)(2,1)S(1)}, bf16[32,256]{1,0:T(8,128)(2,1)S(1)}, u32[]{:S(2)}, u32[]{:S(2)}) collective-permute-start(bf16[32,256]{1,0:T(8,128)(2,1)S(1)} %get-tuple-element.53), channel_id=1, source_target_pairs={{0,15},{1,2},{2,1},{3,4},{4,3},{5,6},{6,5},{7,8},{8,7},{9,10},{10,... | collective-permute-start | bytes 49160 | tf_op jit(solution)/shard_map/ppermute | solution.py:575
  70.4 4.9 %backward.2.rest_0_ = f32[32,128,256]{2,1,0:T(8,128)} custom-call(f32[32,1,256]{2,1,0:T(1,128)S(1)} %copy.25.left_ref, f32[32,1,256]{2,1,0:T(1,128)S(1)} %broadcast_in_dim.47.right_ref, f32[1,256]{1,0:T(1,128)S(1)} %bitcast.22, bf16[512,256]{1,0:T(8,128)(2,1)S(1)} %bitcast.14, bf16[128,512]{1,0:T(8,128)(2,1)S(1)} %convolution_convert_fusion.joint_ref, ...), custom_call_target="tpu_custom_call" | custom-call | flops 1073741824 | bytes 7340032 | tf_op jit(solution)/shard_map/backward/pallas_call | solution.py:429
  75.4 0.0 collective-permute-done.3
  75.4 4.2 %all-to-all-done.1.got_ref = bf16[64,24,128]{2,1,0:T(8,128)(2,1)S(1)} async-done(((bf16[64,24,128]{2,1,0:T(8,128)(2,1)}), bf16[64,24,128]{2,1,0:T(8,128)(2,1)S(1)}, u32[]{:S(2)}, u32[]{:S(2)}) %all-to-all-start.1) | async-done | bytes 393248 | tf_op jit(solution)/shard_map/all_to_all | solution.py:577
  79.5 0.8 total.1
  80.4 5.6 %all-to-all-start.2 = ((bf16[64,24,128]{2,1,0:T(8,128)(2,1)}), bf16[64,24,128]{2,1,0:T(8,128)(2,1)S(1)}, u32[]{:S(2)}, u32[]{:S(2)}) async-start(bf16[64,24,128]{2,1,0:T(8,128)(2,1)} %total.1), calls=%async_computation.2 | async-start | bytes 786432 | tf_op jit(solution)/shard_map/all_to_all | solution.py:585
  85.9 4.9 %backward.3.grad_ref = f32[32,128,256]{2,1,0:T(8,128)} custom-call(f32[32,1,256]{2,1,0:T(1,128)S(1)} %copy.25.left_ref, f32[32,1,256]{2,1,0:T(1,128)S(1)} %broadcast_in_dim.47.right_ref, f32[1,256]{1,0:T(1,128)S(1)} %bitcast.23, bf16[512,256]{1,0:T(8,128)(2,1)S(1)} %bitcast.15, ...), custom_call_target="tpu_custom_call", output_to_operand_aliasing={{}: (9, {})} | custom-call | flops 1073741824 | bytes 7340032 | tf_op jit(solution)/shard_map/backward/pallas_call | solution.py:429
  90.9 1.7 %edge.1 = f32[32,128,256]{2,1,0:T(8,128)} custom-call(s32[1]{0:T(128)} %bitcast.core_ref, f32[32,1,256]{2,1,0:T(1,128)S(1)} %reshape.30.outer_ref, f32[32,128,256]{2,1,0:T(8,128)} %backward.3.grad_ref), custom_call_target="tpu_custom_call", output_to_operand_aliasing={{}: (2, {})} | custom-call | flops 65536 | bytes 524288 | tf_op jit(solution)/shard_map/edge/pallas_call | solution.py:462
  92.6 4.1 %all-to-all-done.2.mine_ref = bf16[64,24,128]{2,1,0:T(8,128)(2,1)S(1)} async-done(((bf16[64,24,128]{2,1,0:T(8,128)(2,1)}), bf16[64,24,128]{2,1,0:T(8,128)(2,1)S(1)}, u32[]{:S(2)}, u32[]{:S(2)}) %all-to-all-start.2) | async-done | bytes 393248 | tf_op jit(solution)/shard_map/all_to_all | solution.py:585
  96.6 2.2 %collective-permute-start.4 = (bf16[64,24,128]{2,1,0:T(8,128)(2,1)S(1)}, bf16[64,24,128]{2,1,0:T(8,128)(2,1)S(1)}, u32[]{:S(2)}, u32[]{:S(2)}) collective-permute-start(bf16[64,24,128]{2,1,0:T(8,128)(2,1)S(1)} %all-to-all-done.2.mine_ref), channel_id=1, source_target_pairs={{0,1},{1,0},{2,3},{3,2},{4,5},{5,4},{6,7},{7,6},{8,9},{9,8},{10,11... | collective-permute-start | bytes 1179656 | tf_op jit(solution)/shard_map/ppermute | solution.py:588
  98.9 0.1 copy.27.gain_ref
  99.0 1.2 %collective-permute-done.4.other_ref = bf16[64,24,128]{2,1,0:T(8,128)(2,1)S(1)} collective-permute-done((bf16[64,24,128]{2,1,0:T(8,128)(2,1)S(1)}, bf16[64,24,128]{2,1,0:T(8,128)(2,1)S(1)}, u32[]{:S(2)}, u32[]{:S(2)}) %collective-permute-start.4) | collective-permute-done | bytes 393248 | tf_op jit(solution)/shard_map/ppermute | solution.py:588
  100.2 1.3 %finish.1 = (f32[256,512]{1,0:T(8,128)}, f32[512,256]{1,0:T(8,128)}, f32[1,256]{1,0:T(1,128)}, f32[256,128]{1,0:T(8,128)}) custom-call(s32[1]{0:T(128)} %bitcast.core_ref, bf16[64,24,128]{2,1,0:T(8,128)(2,1)S(1)} %all-to-all-done.2.mine_ref, bf16[64,24,128]{2,1,0:T(8,128)(2,1)S(1)} %collective-permute-done.4.other_ref, f32[256,1]{1,0:T(8,128)S(1)} %copy.27.gain_ref, ...), custom_call_target="tpu_custom_call" | custom-call | flops 524288 | bytes 3145728 | tf_op jit(solution)/shard_map/finish/pallas_call | solution.py:527
  (6 shorter events, 0.1 us)
Async XLA Ops:
  3.8 3.5 %collective-permute-start = (bf16[32,256]{1,0:T(8,128)(2,1)S(1)}, bf16[32,256]{1,0:T(8,128)(2,1)S(1)}, u32[]{:S(2)}, u32[]{:S(2)}) collective-permute-start(bf16[32,256]{1,0:T(8,128)(2,1)S(1)} %get-tuple-element.35), channel_id=1, source_target_pairs={{0,1},{1,2},{2,3},{3,4},{4,5},{5,6},{6,7},{7,8},{8,9},{9,10},{10,1... | collective-permute-start | bytes 49160 | tf_op jit(solution)/shard_map/ppermute | solution.py:548
  6.4 3.5 %collective-permute-start.1 = (bf16[32,256]{1,0:T(8,128)(2,1)S(1)}, bf16[32,256]{1,0:T(8,128)(2,1)S(1)}, u32[]{:S(2)}, u32[]{:S(2)}) collective-permute-start(bf16[32,256]{1,0:T(8,128)(2,1)S(1)} %get-tuple-element.36), channel_id=1, source_target_pairs={{1,0},{2,1},{3,2},{4,3},{5,4},{6,5},{7,6},{8,7},{9,8},{10,9},{11,1... | collective-permute-start | bytes 49160 | tf_op jit(solution)/shard_map/ppermute | solution.py:549
  9.9 6.6 %copy-start.2 = (bf16[256,512]{1,0:T(8,128)(2,1)S(1)}, bf16[256,512]{1,0:T(8,128)(2,1)}, u32[]{:S(2)}) copy-start(bf16[256,512]{1,0:T(8,128)(2,1)} %w_in_ref.3) | copy-start | bytes 786436
  9.9 6.8 %copy-start.3 = (bf16[256,128]{1,0:T(8,128)(2,1)S(1)}, bf16[256,128]{1,0:T(8,128)(2,1)}, u32[]{:S(2)}) copy-start(bf16[256,128]{1,0:T(8,128)(2,1)} %head_ref.1) | copy-start | bytes 196612
  9.9 6.9 %copy-start.1 = (bf16[512,256]{1,0:T(8,128)(2,1)S(1)}, bf16[512,256]{1,0:T(8,128)(2,1)}, u32[]{:S(2)}) copy-start(bf16[512,256]{1,0:T(8,128)(2,1)} %w_out_ref.1) | copy-start | bytes 786436
  9.9 7.3 %copy-start = (bf16[32,128,256]{2,1,0:T(8,128)(2,1)S(1)}, bf16[32,128,256]{2,1,0:T(8,128)(2,1)}, u32[]{:S(2)}) copy-start(bf16[32,128,256]{2,1,0:T(8,128)(2,1)} %lat_ref.1) | copy-start | bytes 6291460
  9.9 7.3 %copy-start.4 = (f32[256]{0:T(256)S(1)}, f32[256]{0:T(256)}, u32[]{:S(2)}) copy-start(f32[256]{0:T(256)} %param.16) | copy-start | bytes 3076
  9.9 35.1 %all-to-all-start = ((bf16[32,264,128]{2,1,0:T(8,128)(2,1)}), bf16[32,264,128]{2,1,0:T(8,128)(2,1)}, u32[]{:S(2)}, u32[]{:S(2)}) async-start(bf16[32,264,128]{2,1,0:T(8,128)(2,1)} %get-tuple-element.37), calls=%async_computation | async-start | bytes 4325376 | tf_op jit(solution)/shard_map/all_to_all | solution.py:561
  17.2 27.8 %copy-start.5 = (s32[1,1,32]{2,1,0:T(1,128)S(1)}, s32[1,1,32]{2,1,0:T(1,128)}, u32[]{:S(2)}) copy-start(s32[1,1,32]{2,1,0:T(1,128)} %rows_ref.1) | copy-start | bytes 388
  55.5 2.0 %collective-permute-start.2 = (bf16[64,24,128]{2,1,0:T(8,128)(2,1)S(1)}, bf16[64,24,128]{2,1,0:T(8,128)(2,1)S(1)}, u32[]{:S(2)}, u32[]{:S(2)}) collective-permute-start(bf16[64,24,128]{2,1,0:T(8,128)(2,1)S(1)} %get-tuple-element.47), channel_id=1, source_target_pairs={{0,1},{1,0},{2,3},{3,2},{4,5},{5,4},{6,7},{7,6},{8,9},{9,8},{10,11... | collective-permute-start | bytes 1179656 | tf_op jit(solution)/shard_map/ppermute | solution.py:576
  58.3 21.2 %all-to-all-start.1 = ((bf16[64,24,128]{2,1,0:T(8,128)(2,1)}), bf16[64,24,128]{2,1,0:T(8,128)(2,1)S(1)}, u32[]{:S(2)}, u32[]{:S(2)}) async-start(bf16[64,24,128]{2,1,0:T(8,128)(2,1)} %get-tuple-element.48), calls=%async_computation.1 | async-start | bytes 786432 | tf_op jit(solution)/shard_map/all_to_all | solution.py:577
  68.4 6.9 %collective-permute-start.3 = (bf16[32,256]{1,0:T(8,128)(2,1)S(1)}, bf16[32,256]{1,0:T(8,128)(2,1)S(1)}, u32[]{:S(2)}, u32[]{:S(2)}) collective-permute-start(bf16[32,256]{1,0:T(8,128)(2,1)S(1)} %get-tuple-element.53), channel_id=1, source_target_pairs={{0,15},{1,2},{2,1},{3,4},{4,3},{5,6},{6,5},{7,8},{8,7},{9,10},{10,... | collective-permute-start | bytes 49160 | tf_op jit(solution)/shard_map/ppermute | solution.py:575
  80.4 16.3 %all-to-all-start.2 = ((bf16[64,24,128]{2,1,0:T(8,128)(2,1)}), bf16[64,24,128]{2,1,0:T(8,128)(2,1)S(1)}, u32[]{:S(2)}, u32[]{:S(2)}) async-start(bf16[64,24,128]{2,1,0:T(8,128)(2,1)} %total.1), calls=%async_computation.2 | async-start | bytes 786432 | tf_op jit(solution)/shard_map/all_to_all | solution.py:585
  96.6 3.6 %collective-permute-start.4 = (bf16[64,24,128]{2,1,0:T(8,128)(2,1)S(1)}, bf16[64,24,128]{2,1,0:T(8,128)(2,1)S(1)}, u32[]{:S(2)}, u32[]{:S(2)}) collective-permute-start(bf16[64,24,128]{2,1,0:T(8,128)(2,1)S(1)} %all-to-all-done.2.mine_ref), channel_id=1, source_target_pairs={{0,1},{1,0},{2,3},{3,2},{4,5},{5,4},{6,7},{7,6},{8,9},{9,8},{10,11... | collective-permute-start | bytes 1179656 | tf_op jit(solution)/shard_map/ppermute | solution.py:588
